TPU v7x, 32 devices: a whole 2x2x4 slice. The times are simulated.
32 devices in a mesh: loop: 16 (over z, y, x), rep: 2 (over core).
Axes of the slice: x: 2, y: 2, z: 4, core: 2. Of those that a mesh axis runs over, the one named last changes fastest.
Arguments:
- node_features: bfloat16 [4096, 256], P(('loop', 'rep')), may hold values from -6 to 6
- weight: bfloat16 [256, 256], replicated, may hold values from -0.375 to 0.375
- bias_vector: float32 [256], replicated, may hold values from -3 to 3
- tile_values: bfloat16 [16, 2, 16, 2, 128, 128], P('loop', 'rep'), may hold values from 0 to 0.029907227
- tile_place: int32 [16, 2, 16, 2], P('loop', 'rep'), may hold values from 0 to 1
- tile_count: int32 [16, 2, 16], P('loop', 'rep'), may hold values from 0 to 2, as said below
- cotangent: bfloat16 [4096, 256], P(('loop', 'rep')), may hold values from -6 to 6
Outputs:
- output: bfloat16 [4096, 256], P(('loop', 'rep'))
- grad_features: bfloat16 [4096, 256], P(('loop', 'rep'))
- grad_weight: float32 [256, 256], replicated
- grad_bias: float32 [256], replicated
Inputs may be any that keep to these rules, and one draw needn't show every extreme that they name: Slot s of list [i, r, p] is live exactly when s < tile_count[i, r, p]; lists of some devices are far fuller than those of others.
All inputs are finite; a program needn't handle non-finite values.
Results may differ from a plain program's by a relative error of at most 0.0053.
Values may be sent and summed in bfloat16 or wider, within the bound.
No kernel may reach another device: no remote copies, remote signals or barrier semaphores. Data moves between devices by JAX's collectives and lax.ppermute only.
A program may use at most 64 MiB of HBM per device.

v0:
```python
from functools import partial

import jax
import jax.numpy as jnp
from jax import lax
from jax.sharding import PartitionSpec as P


def from_behind(value, axis, steps):
    count = lax.axis_size(axis)
    pairs = [(source, (source + steps) % count) for source in range(count)]
    return lax.ppermute(value, axis, pairs)


def slot_lists(tile_values, tile_place, tile_count, partner):
    tiles = lax.dynamic_index_in_dim(tile_values[0, 0], partner, 0, keepdims=False)
    places = lax.dynamic_index_in_dim(tile_place[0, 0], partner, 0, keepdims=False)
    counted = lax.dynamic_index_in_dim(tile_count[0, 0], partner, 0, keepdims=False)
    return (tiles, places, counted)


def tile_times(one_tile, rows_all, offset, tile_width):
    return jnp.dot(one_tile, rows_all, preferred_element_type=jnp.float32)


def tile_adjoint(one_tile, rows_all, offset, tile_width):
    left_rows = lax.dynamic_slice_in_dim(rows_all, offset, tile_width, 0)
    return lax.dot_general(
        one_tile, left_rows, (((0,), (0,)), ((), ())), preferred_element_type=jnp.float32
    )


def add_tile(totals, offset, producer, is_live):
    live_factor = is_live.astype(jnp.float32)
    product = producer() * live_factor
    earlier = lax.dynamic_slice_in_dim(totals, offset, product.shape[0], 0)
    return lax.dynamic_update_slice_in_dim(totals, earlier + product, offset, 0)


def forward_partner(totals, partner_rows, slots):
    tiles, places, counted = slots
    tile_width = tiles.shape[-1]
    per_side = partner_rows.shape[0] // tile_width
    for number in range(tiles.shape[0]):
        target = places[number] // per_side
        source = places[number] % per_side
        is_live = jnp.logical_and(number < counted, True)
        producer = partial(tile_times, tiles[number], partner_rows, source * tile_width, tile_width)
        totals = add_tile(totals, target * tile_width, producer, is_live)
    return totals


def backward_partner(buffer, grad_panel, slots):
    tiles, places, counted = slots
    tile_width = tiles.shape[-1]
    per_side = buffer.shape[0] // tile_width
    for number in range(tiles.shape[0]):
        target = places[number] // per_side
        source = places[number] % per_side
        is_live = jnp.logical_and(number < counted, True)
        producer = partial(tile_adjoint, tiles[number], grad_panel, target * tile_width, tile_width)
        buffer = add_tile(buffer, source * tile_width, producer, is_live)
    return buffer


def body(node_features, weight, bias_vector, tile_values, tile_place, tile_count, cotangent):
    loop_size = lax.axis_size("loop")
    rep_size = lax.axis_size("rep")
    position = lax.axis_index("loop")
    rows_own = node_features.shape[0]
    width_out = weight.shape[1]

    def slots_for(partner):
        return slot_lists(tile_values, tile_place, tile_count, jnp.mod(partner, loop_size))

    projected = jnp.dot(node_features, weight, preferred_element_type=jnp.float32).astype(
        jnp.bfloat16
    )
    totals = jnp.zeros((rows_own * rep_size, width_out), jnp.float32)
    totals = forward_partner(totals, projected, slots_for(position))

    def forward_once(rotation, carried):
        sums_now, moving = carried
        moving = from_behind(moving, "loop", 1)
        sums_now = forward_partner(sums_now, moving, slots_for(position - rotation))
        return (sums_now, moving)

    totals, moving = lax.fori_loop(1, loop_size, forward_once, (totals, projected))
    row_sums = lax.psum_scatter(totals, "rep", scatter_dimension=0, tiled=True)
    preact = row_sums + bias_vector[None, :]
    negative = jnp.minimum(preact, 0.0)
    output = jnp.where(preact > 0, preact, jnp.expm1(negative)).astype(jnp.bfloat16)
    slope = jnp.where(preact > 0, 1.0, jnp.exp(negative))
    grad_pre = (cotangent.astype(jnp.float32) * slope).astype(jnp.bfloat16)
    grad_panel = lax.all_gather(grad_pre, "rep", axis=0, tiled=True)
    empty = jnp.zeros((rows_own, width_out), jnp.float32)
    adjoint = backward_partner(empty, grad_panel, slots_for(position - 1))

    def backward_once(rotation, buffer):
        buffer = from_behind(buffer, "loop", 1)
        return backward_partner(buffer, grad_panel, slots_for(position - 1 - rotation))

    adjoint = lax.fori_loop(1, loop_size, backward_once, adjoint)
    adjoint_low = adjoint.astype(jnp.bfloat16)
    grad_features = lax.dot_general(
        adjoint_low, weight, (((1,), (1,)), ((), ())), preferred_element_type=jnp.float32
    ).astype(jnp.bfloat16)
    local_weight = lax.dot_general(
        node_features, adjoint_low, (((0,), (0,)), ((), ())), preferred_element_type=jnp.float32
    )
    local_bias = jnp.sum(grad_pre.astype(jnp.float32), axis=0)
    summed_weight, summed_bias = lax.psum((local_weight, local_bias), ("loop", "rep"))
    scale_factor = float(rows_own * loop_size * rep_size) ** (-0.5)
    return (output, grad_features, summed_weight * scale_factor, summed_bias * scale_factor)


def solution(mesh):
    return jax.shard_map(
        body,
        mesh=mesh,
        in_specs=(
            P(("loop", "rep"), None),
            P(),
            P(),
            P("loop", "rep", None, None, None, None),
            P("loop", "rep", None, None),
            P("loop", "rep", None),
            P(("loop", "rep"), None),
        ),
        out_specs=(P(("loop", "rep"), None), P(("loop", "rep"), None), P(), P()),
        check_vma=False,
    )
```

profile of v0, /device:TPU:0, one launch (start us, length us, event | category | flops | bytes accessed | tf_op | source)
XLA Modules:
  0.0 453.7 jit_solution(11314749896915600387)
XLA Ops:
  14.5 148.2 %while.34 = (s32[]{:T(128)}, f32[256,256]{1,0:T(8,128)S(1)}, bf16[128,256]{1,0:T(8,128)(2,1)S(1)}, s32[]{:T(128)}, s32[1,1,16,2]{2,3,1,0:T(2,128)S(1)}, /*index=...) while((s32[]{:T(128)}, f32[256,256]{1,0:T(8,128)S(1)}, ...), condition=%wide.region_1.2_spmd, body=%wide.region_0.1_spmd.sunk | while | flops 16908316 | bytes 1115664 | solution.py:88
  29.5 4.0 collective-permute-done
  39.3 4.0 collective-permute-done
  49.0 4.0 collective-permute-done
  58.8 4.0 collective-permute-done
  68.5 4.0 collective-permute-done
  78.3 4.0 collective-permute-done
  88.1 4.4 collective-permute-done
  98.2 4.0 collective-permute-done
  108.0 4.0 collective-permute-done
  117.8 4.0 collective-permute-done
  127.5 4.0 collective-permute-done
  137.3 4.0 collective-permute-done
  147.1 4.0 collective-permute-done
  156.8 4.0 collective-permute-done
  174.0 146.5 %while.35 = (s32[]{:T(128)}, f32[128,256]{1,0:T(8,128)S(1)}, s32[]{:T(128)}, bf16[1,1,16,2,128,128]{5,4,3,2,1,0:T(8,128)(2,1)}, s32[1,1,16,2]{2,3,1,0:T(2,128)S(...) while((s32[]{:T(128)}, f32[128,256]{1,0:T(8,128)S(1)}, ...), condition=%wide.region_4.5_spmd, body=%wide.region_3.4_spmd.sunk | while | flops 16908316 | bytes 1246736 | solution.py:103
  189.3 3.8 collective-permute-done.1
  237.2 3.9 collective-permute-done.1
  246.9 5.0 %collective-permute-done.1 = f32[128,256]{1,0:T(8,128)S(1)} collective-permute-done((f32[128,256]{1,0:T(8,128)S(1)}, f32[128,256]{1,0:T(8,128)S(1)}, u32[]{:S(2)}, u32[]{:S(2)}) %collective-permute-start.1) | collective-permute-done | bytes 131104 | tf_op jit(solution)/shard_map/while/body/eval_jaxpr/ppermute | solution.py:12
  257.7 4.3 collective-permute-done.1
  267.9 3.8 collective-permute-done.1
  287.0 3.8 collective-permute-done.1
  322.3 36.9 %psum.15 = f32[256]{0:T(256)S(1)} all-reduce(f32[256]{0:T(256)S(1)} %get-tuple-element.465), channel_id=1, replica_groups=mesh['loop'=16,'rep'=2] {'loop','rep'}, use_global_device_ids=true, to_apply=%region_7.8 | all-reduce | flops 256 | bytes 2048 | tf_op jit(solution)/shard_map/psum | solution.py:112
  359.8 85.3 %all-reduce.2.cloned.1.call-done = f32[256,256]{0,1:T(8,128)} async-done(((f32[256,256]{0,1:T(8,128)}), f32[256,256]{0,1:T(8,128)}) %all-reduce.2.cloned.1.call-update) | async-done | bytes 262160 | tf_op jit(solution)/shard_map/psum | solution.py:112
  (240 shorter events, 151.8 us)
Async XLA Ops:
  7.2 161.4 %reduce-scatter.2.cloned.1.call-start = ((), (), s32[]{:S(2)}) async-start(), calls=%async_computation.1 | async-start | bytes 393216 | tf_op jit(solution)/shard_map/reduce_scatter | solution.py:89
  14.5 9.2 %collective-permute-start = (bf16[128,256]{1,0:T(8,128)(2,1)S(1)}, bf16[128,256]{1,0:T(8,128)(2,1)S(1)}, u32[]{:S(2)}, u32[]{:S(2)}) collective-permute-start(bf16[128,256]{1,0:T(8,128)(2,1)S(1)} %get-tuple-element.605), channel_id=1, source_target_pairs={{0,2},{2,4},{4,6},{6,8},{8,10},{10,12},{12,14},{14,16},{16,18},{18... | collective-permute-start | bytes 196616 | tf_op jit(solution)/shard_map/while/body/eval_jaxpr/ppermute | solution.py:12
  35.3 7.9 %collective-permute-start = (bf16[128,256]{1,0:T(8,128)(2,1)S(1)}, bf16[128,256]{1,0:T(8,128)(2,1)S(1)}, u32[]{:S(2)}, u32[]{:S(2)}) collective-permute-start(bf16[128,256]{1,0:T(8,128)(2,1)S(1)} %get-tuple-element.605), channel_id=1, source_target_pairs={{0,2},{2,4},{4,6},{6,8},{8,10},{10,12},{12,14},{14,16},{16,18},{18... | collective-permute-start | bytes 196616 | tf_op jit(solution)/shard_map/while/body/eval_jaxpr/ppermute | solution.py:12
  45.1 7.9 %collective-permute-start = (bf16[128,256]{1,0:T(8,128)(2,1)S(1)}, bf16[128,256]{1,0:T(8,128)(2,1)S(1)}, u32[]{:S(2)}, u32[]{:S(2)}) collective-permute-start(bf16[128,256]{1,0:T(8,128)(2,1)S(1)} %get-tuple-element.605), channel_id=1, source_target_pairs={{0,2},{2,4},{4,6},{6,8},{8,10},{10,12},{12,14},{14,16},{16,18},{18... | collective-permute-start | bytes 196616 | tf_op jit(solution)/shard_map/while/body/eval_jaxpr/ppermute | solution.py:12
  74.4 7.9 %collective-permute-start = (bf16[128,256]{1,0:T(8,128)(2,1)S(1)}, bf16[128,256]{1,0:T(8,128)(2,1)S(1)}, u32[]{:S(2)}, u32[]{:S(2)}) collective-permute-start(bf16[128,256]{1,0:T(8,128)(2,1)S(1)} %get-tuple-element.605), channel_id=1, source_target_pairs={{0,2},{2,4},{4,6},{6,8},{8,10},{10,12},{12,14},{14,16},{16,18},{18... | collective-permute-start | bytes 196616 | tf_op jit(solution)/shard_map/while/body/eval_jaxpr/ppermute | solution.py:12
  84.2 8.3 %collective-permute-start = (bf16[128,256]{1,0:T(8,128)(2,1)S(1)}, bf16[128,256]{1,0:T(8,128)(2,1)S(1)}, u32[]{:S(2)}, u32[]{:S(2)}) collective-permute-start(bf16[128,256]{1,0:T(8,128)(2,1)S(1)} %get-tuple-element.605), channel_id=1, source_target_pairs={{0,2},{2,4},{4,6},{6,8},{8,10},{10,12},{12,14},{14,16},{16,18},{18... | collective-permute-start | bytes 196616 | tf_op jit(solution)/shard_map/while/body/eval_jaxpr/ppermute | solution.py:12
  113.9 7.9 %collective-permute-start = (bf16[128,256]{1,0:T(8,128)(2,1)S(1)}, bf16[128,256]{1,0:T(8,128)(2,1)S(1)}, u32[]{:S(2)}, u32[]{:S(2)}) collective-permute-start(bf16[128,256]{1,0:T(8,128)(2,1)S(1)} %get-tuple-element.605), channel_id=1, source_target_pairs={{0,2},{2,4},{4,6},{6,8},{8,10},{10,12},{12,14},{14,16},{16,18},{18... | collective-permute-start | bytes 196616 | tf_op jit(solution)/shard_map/while/body/eval_jaxpr/ppermute | solution.py:12
  123.6 7.9 %collective-permute-start = (bf16[128,256]{1,0:T(8,128)(2,1)S(1)}, bf16[128,256]{1,0:T(8,128)(2,1)S(1)}, u32[]{:S(2)}, u32[]{:S(2)}) collective-permute-start(bf16[128,256]{1,0:T(8,128)(2,1)S(1)} %get-tuple-element.605), channel_id=1, source_target_pairs={{0,2},{2,4},{4,6},{6,8},{8,10},{10,12},{12,14},{14,16},{16,18},{18... | collective-permute-start | bytes 196616 | tf_op jit(solution)/shard_map/while/body/eval_jaxpr/ppermute | solution.py:12
  163.4 281.7 %all-reduce.2.cloned.1.call-start = ((), (), s32[]{:S(2)}) async-start(), calls=%async_computation.2 | async-start | bytes 524288 | tf_op jit(solution)/shard_map/psum | solution.py:112
  174.0 9.4 %collective-permute-start.1 = (f32[128,256]{1,0:T(8,128)S(1)}, f32[128,256]{1,0:T(8,128)S(1)}, u32[]{:S(2)}, u32[]{:S(2)}) collective-permute-start(f32[128,256]{1,0:T(8,128)S(1)} %get-tuple-element.649), channel_id=1, source_target_pairs={{0,2},{2,4},{4,6},{6,8},{8,10},{10,12},{12,14},{14,16},{16,18},{18... | collective-permute-start | bytes 393224 | tf_op jit(solution)/shard_map/while/body/eval_jaxpr/ppermute | solution.py:12
  184.4 8.6 %collective-permute-start.1 = (f32[128,256]{1,0:T(8,128)S(1)}, f32[128,256]{1,0:T(8,128)S(1)}, u32[]{:S(2)}, u32[]{:S(2)}) collective-permute-start(f32[128,256]{1,0:T(8,128)S(1)} %get-tuple-element.649), channel_id=1, source_target_pairs={{0,2},{2,4},{4,6},{6,8},{8,10},{10,12},{12,14},{14,16},{16,18},{18... | collective-permute-start | bytes 393224 | tf_op jit(solution)/shard_map/while/body/eval_jaxpr/ppermute | solution.py:12
  194.0 8.6 %collective-permute-start.1 = (f32[128,256]{1,0:T(8,128)S(1)}, f32[128,256]{1,0:T(8,128)S(1)}, u32[]{:S(2)}, u32[]{:S(2)}) collective-permute-start(f32[128,256]{1,0:T(8,128)S(1)} %get-tuple-element.649), channel_id=1, source_target_pairs={{0,2},{2,4},{4,6},{6,8},{8,10},{10,12},{12,14},{14,16},{16,18},{18... | collective-permute-start | bytes 393224 | tf_op jit(solution)/shard_map/while/body/eval_jaxpr/ppermute | solution.py:12
  203.6 8.6 %collective-permute-start.1 = (f32[128,256]{1,0:T(8,128)S(1)}, f32[128,256]{1,0:T(8,128)S(1)}, u32[]{:S(2)}, u32[]{:S(2)}) collective-permute-start(f32[128,256]{1,0:T(8,128)S(1)} %get-tuple-element.649), channel_id=1, source_target_pairs={{0,2},{2,4},{4,6},{6,8},{8,10},{10,12},{12,14},{14,16},{16,18},{18... | collective-permute-start | bytes 393224 | tf_op jit(solution)/shard_map/while/body/eval_jaxpr/ppermute | solution.py:12
  213.2 8.6 %collective-permute-start.1 = (f32[128,256]{1,0:T(8,128)S(1)}, f32[128,256]{1,0:T(8,128)S(1)}, u32[]{:S(2)}, u32[]{:S(2)}) collective-permute-start(f32[128,256]{1,0:T(8,128)S(1)} %get-tuple-element.649), channel_id=1, source_target_pairs={{0,2},{2,4},{4,6},{6,8},{8,10},{10,12},{12,14},{14,16},{16,18},{18... | collective-permute-start | bytes 393224 | tf_op jit(solution)/shard_map/while/body/eval_jaxpr/ppermute | solution.py:12
  222.8 8.6 %collective-permute-start.1 = (f32[128,256]{1,0:T(8,128)S(1)}, f32[128,256]{1,0:T(8,128)S(1)}, u32[]{:S(2)}, u32[]{:S(2)}) collective-permute-start(f32[128,256]{1,0:T(8,128)S(1)} %get-tuple-element.649), channel_id=1, source_target_pairs={{0,2},{2,4},{4,6},{6,8},{8,10},{10,12},{12,14},{14,16},{16,18},{18... | collective-permute-start | bytes 393224 | tf_op jit(solution)/shard_map/while/body/eval_jaxpr/ppermute | solution.py:12
  232.3 8.7 %collective-permute-start.1 = (f32[128,256]{1,0:T(8,128)S(1)}, f32[128,256]{1,0:T(8,128)S(1)}, u32[]{:S(2)}, u32[]{:S(2)}) collective-permute-start(f32[128,256]{1,0:T(8,128)S(1)} %get-tuple-element.649), channel_id=1, source_target_pairs={{0,2},{2,4},{4,6},{6,8},{8,10},{10,12},{12,14},{14,16},{16,18},{18... | collective-permute-start | bytes 393224 | tf_op jit(solution)/shard_map/while/body/eval_jaxpr/ppermute | solution.py:12
  242.0 9.9 %collective-permute-start.1 = (f32[128,256]{1,0:T(8,128)S(1)}, f32[128,256]{1,0:T(8,128)S(1)}, u32[]{:S(2)}, u32[]{:S(2)}) collective-permute-start(f32[128,256]{1,0:T(8,128)S(1)} %get-tuple-element.649), channel_id=1, source_target_pairs={{0,2},{2,4},{4,6},{6,8},{8,10},{10,12},{12,14},{14,16},{16,18},{18... | collective-permute-start | bytes 393224 | tf_op jit(solution)/shard_map/while/body/eval_jaxpr/ppermute | solution.py:12
  252.9 9.2 %collective-permute-start.1 = (f32[128,256]{1,0:T(8,128)S(1)}, f32[128,256]{1,0:T(8,128)S(1)}, u32[]{:S(2)}, u32[]{:S(2)}) collective-permute-start(f32[128,256]{1,0:T(8,128)S(1)} %get-tuple-element.649), channel_id=1, source_target_pairs={{0,2},{2,4},{4,6},{6,8},{8,10},{10,12},{12,14},{14,16},{16,18},{18... | collective-permute-start | bytes 393224 | tf_op jit(solution)/shard_map/while/body/eval_jaxpr/ppermute | solution.py:12
  263.0 8.6 %collective-permute-start.1 = (f32[128,256]{1,0:T(8,128)S(1)}, f32[128,256]{1,0:T(8,128)S(1)}, u32[]{:S(2)}, u32[]{:S(2)}) collective-permute-start(f32[128,256]{1,0:T(8,128)S(1)} %get-tuple-element.649), channel_id=1, source_target_pairs={{0,2},{2,4},{4,6},{6,8},{8,10},{10,12},{12,14},{14,16},{16,18},{18... | collective-permute-start | bytes 393224 | tf_op jit(solution)/shard_map/while/body/eval_jaxpr/ppermute | solution.py:12
  272.6 8.6 %collective-permute-start.1 = (f32[128,256]{1,0:T(8,128)S(1)}, f32[128,256]{1,0:T(8,128)S(1)}, u32[]{:S(2)}, u32[]{:S(2)}) collective-permute-start(f32[128,256]{1,0:T(8,128)S(1)} %get-tuple-element.649), channel_id=1, source_target_pairs={{0,2},{2,4},{4,6},{6,8},{8,10},{10,12},{12,14},{14,16},{16,18},{18... | collective-permute-start | bytes 393224 | tf_op jit(solution)/shard_map/while/body/eval_jaxpr/ppermute | solution.py:12
  282.2 8.6 %collective-permute-start.1 = (f32[128,256]{1,0:T(8,128)S(1)}, f32[128,256]{1,0:T(8,128)S(1)}, u32[]{:S(2)}, u32[]{:S(2)}) collective-permute-start(f32[128,256]{1,0:T(8,128)S(1)} %get-tuple-element.649), channel_id=1, source_target_pairs={{0,2},{2,4},{4,6},{6,8},{8,10},{10,12},{12,14},{14,16},{16,18},{18... | collective-permute-start | bytes 393224 | tf_op jit(solution)/shard_map/while/body/eval_jaxpr/ppermute | solution.py:12
  291.8 8.6 %collective-permute-start.1 = (f32[128,256]{1,0:T(8,128)S(1)}, f32[128,256]{1,0:T(8,128)S(1)}, u32[]{:S(2)}, u32[]{:S(2)}) collective-permute-start(f32[128,256]{1,0:T(8,128)S(1)} %get-tuple-element.649), channel_id=1, source_target_pairs={{0,2},{2,4},{4,6},{6,8},{8,10},{10,12},{12,14},{14,16},{16,18},{18... | collective-permute-start | bytes 393224 | tf_op jit(solution)/shard_map/while/body/eval_jaxpr/ppermute | solution.py:12
  301.3 8.6 %collective-permute-start.1 = (f32[128,256]{1,0:T(8,128)S(1)}, f32[128,256]{1,0:T(8,128)S(1)}, u32[]{:S(2)}, u32[]{:S(2)}) collective-permute-start(f32[128,256]{1,0:T(8,128)S(1)} %get-tuple-element.649), channel_id=1, source_target_pairs={{0,2},{2,4},{4,6},{6,8},{8,10},{10,12},{12,14},{14,16},{16,18},{18... | collective-permute-start | bytes 393224 | tf_op jit(solution)/shard_map/while/body/eval_jaxpr/ppermute | solution.py:12
  310.9 8.6 %collective-permute-start.1 = (f32[128,256]{1,0:T(8,128)S(1)}, f32[128,256]{1,0:T(8,128)S(1)}, u32[]{:S(2)}, u32[]{:S(2)}) collective-permute-start(f32[128,256]{1,0:T(8,128)S(1)} %get-tuple-element.649), channel_id=1, source_target_pairs={{0,2},{2,4},{4,6},{6,8},{8,10},{10,12},{12,14},{14,16},{16,18},{18... | collective-permute-start | bytes 393224 | tf_op jit(solution)/shard_map/while/body/eval_jaxpr/ppermute | solution.py:12
  (15 other events, 84.5 us)
Sparse Core Ops, SparseCore 0:
  163.5 5.0 reduce-scatter.1
  322.4 122.6 all-reduce.1
where the time goes:
time: 459 us; the launch traced here: 454 us
  waiting for transfers between devices  204 us (44%)
  loops' own time  79.7 us (17%)
  matrix products  61.7 us (13%)
  blocking collectives  38.8 us (8%)
  local copies, waits for them, and re-layouts  22.5 us (5%)
  other arithmetic  21.2 us (5%)
  between operations  19.3 us (4%)
  starting transfers between devices  6.46 us (1%)
    ppermute x30, waiting for transfers between devices, from_behind(): return lax.ppermute(value, axis, pairs)  116 us
    psum x1, waiting for transfers between devices, body(): lax.psum((local_weight, local_bias), ('loop', 'rep'))  85.3 us
    another operation x1, loops' own time, body(): adjoint = lax.fori_loop(1, loop_size, backward_once, adjoint)  40 us
    another operation x1, loops' own time, body(): lax.fori_loop(1, loop_size, forward_once, (totals, projected))  39.7 us
    psum x1, blocking collectives, body(): lax.psum((local_weight, local_bias), ('loop', 'rep'))  36.9 us
    dot_general x32, matrix products, tile_adjoint(): lax.dot_general(one_tile, left_rows, (((0,), (0,)), ((), ())), preferred_...  30.7 us
    dot_general x32, matrix products, tile_times(): return jnp.dot(one_tile, rows_all, preferred_element_type=jnp.float32)  29.2 us
  transfers between devices with their start and end apart: 32, of which 32 were waited for; matrix products, arithmetic and copies ran while one was open for 11% of the time, Pallas kernels for 0%

commit v1 on v0

v1 whole, which is shorter than its diff:
```python
import jax
import jax.numpy as jnp
from jax import lax
from jax.experimental import pallas as pl
from jax.experimental.pallas import tpu as pltpu
from jax.sharding import PartitionSpec as P

BF16 = jnp.bfloat16
F32 = jnp.float32
DENSE_BYTES = 4 << 20


def dot(left, right, contract=((1,), (0,))):
    return lax.dot_general(left, right, (contract, ((), ())), preferred_element_type=F32)


def rounded(value):
    return lax.reduce_precision(value, 8, 7)


def axis_orders(loop_size):
    bits = [1 << b for b in range(loop_size.bit_length() - 1)]
    low, high = bits[: len(bits) // 2], bits[len(bits) // 2 :]
    return (high + low, high[::-1] + low[::-1])


def exchange(value, step, orders, loop_size, rep_size):
    pairs = []
    for place in range(loop_size):
        for rep in range(rep_size):
            partner = place ^ orders[rep % 2][step]
            pairs.append((place * rep_size + rep, partner * rep_size + rep))
    return lax.ppermute(value, ("loop", "rep"), pairs)


def swap_rep(value, mask, rep_size):
    return lax.ppermute(value, "rep", [(r, r ^ mask) for r in range(rep_size)])


def partner_masks(order):
    masks = [0]
    for bit in order:
        masks = masks + [m ^ bit for m in masks]
    return masks


def lay_out_kernel(row_ref, tiles_ref, near_ref, far_ref, near_t_ref, far_t_ref):
    partners, slots, tile = tiles_ref.shape[0], tiles_ref.shape[1], tiles_ref.shape[2]
    panel = near_ref.shape[0] // (slots * tile)
    half = partners // 2
    for k in range(partners):
        source = row_ref[k, slots]
        out, out_t = (near_ref, near_t_ref) if k < half else (far_ref, far_t_ref)
        cols = pl.ds((k % half) * tile, tile)
        for s in range(slots):
            one = tiles_ref[source, s]
            one_t = one.T
            for t in range(panel):
                keep = (row_ref[k, s] == t).astype(BF16)
                rows = pl.ds((s * panel + t) * tile, tile)
                out[rows, cols] = one * keep
                out_t[cols, rows] = one_t * keep


def lay_out(row_table, tiles, panel):
    partners, slots, tile, _ = tiles.shape
    wide, deep = partners // 2 * tile, slots * panel * tile
    near = jax.ShapeDtypeStruct((deep, wide), BF16)
    near_t = jax.ShapeDtypeStruct((wide, deep), BF16)
    vmem = pl.BlockSpec(memory_space=pltpu.VMEM)
    return pl.pallas_call(
        lay_out_kernel,
        out_shape=(near, near, near_t, near_t),
        in_specs=[pl.BlockSpec(memory_space=pltpu.SMEM), vmem],
        out_specs=(vmem,) * 4,
        compiler_params=pltpu.CompilerParams(vmem_limit_bytes=32 << 20),
        name="lay_out",
    )(row_table, tiles)


def body(node_features, weight, bias_vector, tile_values, tile_place, tile_count, cotangent):
    loop_size = lax.axis_size("loop")
    rep_size = lax.axis_size("rep")
    position = lax.axis_index("loop")
    rep = lax.axis_index("rep")
    rows_own, width_in = node_features.shape
    width_out = weight.shape[1]
    _, _, partners, slots, tile, _ = tile_values.shape
    per_side = rows_own // tile
    panel = rep_size * per_side
    orders = axis_orders(loop_size)
    steps = len(orders[0])
    half = partners // 2
    tiles = tile_values[0, 0]

    masks = jnp.where(
        rep % 2 == 0,
        jnp.array(partner_masks(orders[0]), jnp.int32),
        jnp.array(partner_masks(orders[1]), jnp.int32),
    )
    partner = jnp.bitwise_xor(position.astype(jnp.int32), masks)
    places = tile_place[0, 0][partner]
    target = places // per_side
    target = jnp.bitwise_xor(target // per_side, rep.astype(jnp.int32)) * per_side + target % per_side
    live = jnp.arange(slots, dtype=jnp.int32)[None, :] < tile_count[0, 0][partner][:, None]
    target = jnp.where(live, target, -1)
    dense = per_side == 1 and 2 * slots * panel * tile * partners * tile <= DENSE_BYTES

    cotangent_rows = cotangent
    for bit in range(rep_size.bit_length() - 1):
        cotangent_rows = jnp.concatenate(
            [cotangent_rows, swap_rep(cotangent_rows, 1 << bit, rep_size)], axis=0
        )

    gathered = node_features
    for step in range(steps - 1):
        gathered = jnp.concatenate(
            [gathered, exchange(gathered, step, orders, loop_size, rep_size)], axis=0
        )
    arriving = exchange(gathered, steps - 1, orders, loop_size, rep_size)

    if dense:
        table = jnp.concatenate([target, partner[:, None]], axis=1)
        near, far, near_t, far_t = lay_out(table, tiles, panel)
        both = dot(near, gathered) + dot(far, arriving)
        sums = jnp.sum(both.reshape(slots, panel * tile, width_in), axis=0)
    else:
        source = places % per_side
        everything = jnp.concatenate([gathered, arriving], axis=0)

        def forward_tile(number, totals):
            k, s = number // slots, number % slots
            right = lax.dynamic_slice_in_dim(
                everything, k * rows_own + source[k, s] * tile, tile, 0
            )
            product = dot(tiles[partner[k], s], right)
            product = product * (target[k, s] >= 0).astype(F32)
            start = jnp.maximum(target[k, s], 0) * tile
            earlier = lax.dynamic_slice_in_dim(totals, start, tile, 0)
            return lax.dynamic_update_slice_in_dim(totals, earlier + product, start, 0)

        sums = lax.fori_loop(
            0, partners * slots, forward_tile, jnp.zeros((panel * tile, width_in), F32)
        )

    for bit in range(rep_size.bit_length() - 1):
        other = swap_rep(sums, 1 << bit, rep_size)
        blocks = other.reshape(rep_size, rows_own, width_in)
        blocks = jnp.stack([blocks[t ^ (1 << bit)] for t in range(rep_size)])
        sums = sums + blocks.reshape(sums.shape)

    sums_high = rounded(sums)
    sums_low = (sums - sums_high).astype(BF16)
    sums_high = sums_high.astype(BF16)
    preact = dot(sums_high, weight) + dot(sums_low, weight) + bias_vector[None, :]
    negative = jnp.minimum(preact, 0.0)
    own = preact[:rows_own]
    output = jnp.where(own > 0, own, jnp.expm1(negative[:rows_own])).astype(BF16)
    slope = jnp.where(preact > 0, 1.0, jnp.exp(negative))
    grad_pre = (cotangent_rows.astype(F32) * slope).astype(BF16)
    grad_back = dot(grad_pre, weight, ((1,), (1,))).astype(BF16)

    share = width_in // rep_size
    own_columns = lax.dynamic_slice_in_dim(sums_high, rep * share, share, 1)
    weight_term = dot(own_columns, grad_pre, ((0,), (0,)))
    bias_term = jnp.sum(grad_pre[:rows_own].astype(F32), axis=0, keepdims=True)

    if dense:
        doubled = jnp.concatenate([grad_back] * slots, axis=0)
        sending = dot(far_t, doubled)
        keeping = dot(near_t, doubled)
    else:

        def backward_tile(number, totals):
            k, s = number // slots, number % slots
            start = jnp.maximum(target[k, s], 0) * tile
            left = lax.dynamic_slice_in_dim(grad_back, start, tile, 0)
            product = dot(tiles[partner[k], s], left, ((0,), (0,)))
            product = product * (target[k, s] >= 0).astype(F32)
            place = k * rows_own + source[k, s] * tile
            earlier = lax.dynamic_slice_in_dim(totals, place, tile, 0)
            return lax.dynamic_update_slice_in_dim(totals, earlier + product, place, 0)

        partial = lax.fori_loop(
            0, partners * slots, backward_tile, jnp.zeros((partners * rows_own, width_in), F32)
        )
        keeping, sending = partial[: half * rows_own], partial[half * rows_own :]

    for step in range(steps - 1, -1, -1):
        weight_term = rounded(weight_term)
        bias_high = rounded(bias_term)
        bias_low = rounded(bias_term - bias_high)
        blank = jnp.zeros((14, width_out), BF16)
        message = jnp.concatenate(
            [sending.astype(BF16), weight_term.astype(BF16), bias_high.astype(BF16), bias_low.astype(BF16), blank],
            axis=0,
        )
        received = exchange(message, step, orders, loop_size, rep_size).astype(F32)
        size = sending.shape[0]
        keeping = keeping + received[:size]
        weight_term = weight_term + received[size : size + share]
        tail = received[size + share :]
        bias_term = (bias_high + bias_low) + (tail[0:1] + tail[1:2])
        if step:
            keeping, sending = keeping[: size // 2], keeping[size // 2 :]
    grad_features = keeping.astype(BF16)

    scale_factor = float(rows_own * loop_size * rep_size) ** (-0.5)
    shares = jnp.concatenate(
        [weight_term, bias_term, jnp.zeros((7, width_out), F32)], axis=0
    )[None] * scale_factor
    for bit in range(rep_size.bit_length() - 1):
        shares = jnp.concatenate([shares, swap_rep(shares, 1 << bit, rep_size)], axis=0)
    by_rep = jnp.bitwise_xor(jnp.arange(rep_size, dtype=jnp.int32), rep.astype(jnp.int32))
    shares = shares[by_rep]
    grad_weight = shares[:, :share].reshape(width_in, width_out)
    grad_bias = jnp.sum(shares[:, share], axis=0)
    return (output, grad_features, grad_weight, grad_bias)


def solution(mesh):
    return jax.shard_map(
        body,
        mesh=mesh,
        in_specs=(
            P(("loop", "rep"), None),
            P(),
            P(),
            P("loop", "rep", None, None, None, None),
            P("loop", "rep", None, None),
            P("loop", "rep", None),
            P(("loop", "rep"), None),
        ),
        out_specs=(P(("loop", "rep"), None), P(("loop", "rep"), None), P(), P()),
        check_vma=False,
    )
```

time: 459 us -> 89.2 us (0.19); the launches traced: 454 us -> 88.7 us
  waiting for transfers between devices: 204 us -> 44.6 us
  loops' own time: 79.7 us -> 0 us
  matrix products: 61.7 us -> 6.27 us
  blocking collectives: 38.8 us -> 0 us
  between operations: 19.3 us -> 1.16 us
  other arithmetic: 21.2 us -> 7.43 us
  local copies, waits for them, and re-layouts: 22.5 us -> 11.7 us
  starting transfers between devices: 6.46 us -> 16.1 us
    psum x1 -> x0, waiting for transfers between devices: 85.3 us -> none  [body(): lax.psum((local_weight, local_bias), ('loop', 'rep'))]
    another operation x2 -> x0, loops' own time: 79.7 us -> none  [the longest x1 40 us: body(): adjoint = lax.fori_loop(1, loop_size, backward_once, adjoint)]
    ppermute x30 -> x11, waiting for transfers between devices: 116 us -> 44.6 us  [the longest x8 43 us: exchange(): return lax.ppermute(value, ('loop', 'rep'), pairs)]
    dot_general x67 -> x8, matrix products: 61.7 us -> 6.27 us  [dot(): lax.dot_general(left, right, (contract, ((), ())), preferred_element_type...]
    psum x1 -> x0, blocking collectives: 36.9 us -> none  [body(): lax.psum((local_weight, local_bias), ('loop', 'rep'))]
    gt x30 -> x0, other arithmetic: 18 us -> none  [the longest x15 9.17 us: forward_partner(): is_live = jnp.logical_and(number < counted, True)]
    slice x31 -> x5, local copies, waits for them, and re-layouts: 16.6 us -> 0.79 us  [the longest x1 0.72 us: body(): grad_weight = shares[:, :share].reshape(width_in, width_out)]
    ppermute x30 -> x11, starting transfers between devices: 6.38 us -> 16.1 us  [the longest x8 15.4 us: exchange(): return lax.ppermute(value, ('loop', 'rep'), pairs)]
  transfers between devices with their start and end apart: 32 -> 11, of which waited for: 32 -> 10; matrix products, arithmetic and copies ran while one was open for 11% -> 6% of each run, Pallas kernels for 0% -> 2%
where the time goes in v1:
time: 89.2 us; the launch traced here: 88.7 us
  waiting for transfers between devices  44.6 us (50%)
  starting transfers between devices  16.1 us (18%)
  local copies, waits for them, and re-layouts  11.7 us (13%)
  other arithmetic  7.43 us (8%)
  matrix products  6.27 us (7%)
  Pallas kernels  1.45 us (2%)
  between operations  1.16 us (1%)
    ppermute x8, waiting for transfers between devices, exchange(): return lax.ppermute(value, ('loop', 'rep'), pairs)  43 us
    ppermute x8, starting transfers between devices, exchange(): return lax.ppermute(value, ('loop', 'rep'), pairs)  15.4 us
    dot_general x8, matrix products, dot(): lax.dot_general(left, right, (contract, ((), ())), preferred_element_type...  6.27 us
    concatenate x4, local copies, waits for them, and re-layouts, body(): jnp.concatenate([sending.astype(BF16), weight_term.astype(BF16), bias_hig...  4.82 us
    unnamed x45, local copies, waits for them, and re-layouts  3.36 us
  transfers between devices with their start and end apart: 11, of which 10 were waited for; matrix products, arithmetic and copies ran while one was open for 6% of the time, Pallas kernels for 2%

profile of v1, /device:TPU:0, one launch (start us, length us, event | category | flops | bytes accessed | tf_op | source)
XLA Modules:
  0.0 88.7 jit_solution(17415700668421759110)
XLA Ops:
  0.7 3.1 %collective-permute-start = (bf16[128,256]{1,0:T(8,128)(2,1)}, bf16[128,256]{1,0:T(8,128)(2,1)S(1)}, u32[]{:S(2)}, u32[]{:S(2)}) collective-permute-start(bf16[128,256]{1,0:T(8,128)(2,1)} %param.9), channel_id=1, source_target_pairs={{0,8},{1,17},{2,10},{3,19},{4,12},{5,21},{6,14},{7,23},{8,0},{9,25... | collective-permute-start | bytes 196616 | tf_op jit(solution)/shard_map/ppermute | solution.py:33
  3.8 3.2 %collective-permute-done = bf16[128,256]{1,0:T(8,128)(2,1)S(1)} collective-permute-done((bf16[128,256]{1,0:T(8,128)(2,1)}, bf16[128,256]{1,0:T(8,128)(2,1)S(1)}, u32[]{:S(2)}, u32[]{:S(2)}) %collective-permute-start) | collective-permute-done | bytes 65568 | tf_op jit(solution)/shard_map/ppermute | solution.py:33
  7.8 2.4 %collective-permute-start.1 = (bf16[256,256]{1,0:T(8,128)(2,1)S(1)}, bf16[256,256]{1,0:T(8,128)(2,1)S(1)}, u32[]{:S(2)}, u32[]{:S(2)}) collective-permute-start(bf16[256,256]{1,0:T(8,128)(2,1)S(1)} %pad_maximum_fusion.8), channel_id=1, source_target_pairs={{0,16},{1,9},{2,18},{3,11},{4,20},{5,13},{6,22},{7,15},{8,24},{9,1... | collective-permute-start | bytes 393224 | tf_op jit(solution)/shard_map/ppermute | solution.py:33
  10.2 3.6 %collective-permute-done.1 = bf16[256,256]{1,0:T(8,128)(2,1)S(1)} collective-permute-done((bf16[256,256]{1,0:T(8,128)(2,1)S(1)}, bf16[256,256]{1,0:T(8,128)(2,1)S(1)}, u32[]{:S(2)}, u32[]{:S(2)}) %collective-permute-start.1) | collective-permute-done | bytes 131104 | tf_op jit(solution)/shard_map/ppermute | solution.py:33
  13.8 0.9 pad_maximum_fusion.1
  14.6 3.1 %collective-permute-start.2 = (bf16[512,256]{1,0:T(8,128)(2,1)S(1)}, bf16[512,256]{1,0:T(8,128)(2,1)S(1)}, u32[]{:S(2)}, u32[]{:S(2)}) collective-permute-start(bf16[512,256]{1,0:T(8,128)(2,1)S(1)} %pad_maximum_fusion.1), channel_id=1, source_target_pairs={{0,2},{1,5},{2,0},{3,7},{4,6},{5,1},{6,4},{7,3},{8,10},{9,13},{10,... | collective-permute-start | bytes 786440 | tf_op jit(solution)/shard_map/ppermute | solution.py:33
  17.8 1.5 %constant_dynamic-update-slice_fusion.3 = bf16[1024,256]{1,0:T(8,128)(2,1)} fusion(bf16[128,256]{1,0:T(8,128)(2,1)} %param.9), kind=kLoop, calls=%fused_computation.51 | loop fusion | bytes 131072
  20.5 2.9 %collective-permute-done.2 = bf16[512,256]{1,0:T(8,128)(2,1)S(1)} collective-permute-done((bf16[512,256]{1,0:T(8,128)(2,1)S(1)}, bf16[512,256]{1,0:T(8,128)(2,1)S(1)}, u32[]{:S(2)}, u32[]{:S(2)}) %collective-permute-start.2) | collective-permute-done | bytes 262176 | tf_op jit(solution)/shard_map/ppermute | solution.py:33
  24.1 2.5 %collective-permute-start.3 = (bf16[1024,256]{1,0:T(8,128)(2,1)}, bf16[1024,256]{1,0:T(8,128)(2,1)}, u32[]{:S(2)}, u32[]{:S(2)}) collective-permute-start(bf16[1024,256]{1,0:T(8,128)(2,1)} %constant_dynamic-update-slice_fusion), channel_id=1, source_target_pairs={{0,4},{1,3},{2,6},{3,1},{4,0},{5,7},{6,2},{7,5},{8,12},{9,11},{10,... | collective-permute-start | bytes 1572872 | tf_op jit(solution)/shard_map/ppermute | solution.py:33
  28.2 1.5 %lay_out.1 = (bf16[512,1024]{1,0:T(8,128)(2,1)S(1)}, bf16[512,1024]{1,0:T(8,128)(2,1)S(1)}, bf16[1024,512]{1,0:T(8,128)(2,1)S(1)}, bf16[1024,512]{1,0:T(8,128)(2,1)S(1)}) custom-call(s32[16,3]{1,0:T(8,128)S(1)} %pad_add_fusion.row_ref, bf16[16,2,128,128]{3,2,1,0:T(8,128)(2,1)S(1)} %bitcast.34), custom_call_target="tpu_custom_call" | custom-call | tf_op jit(solution)/shard_map/lay_out/pallas_call | solution.py:71
  29.7 4.4 %collective-permute-done.3 = bf16[1024,256]{1,0:T(8,128)(2,1)} collective-permute-done((bf16[1024,256]{1,0:T(8,128)(2,1)}, bf16[1024,256]{1,0:T(8,128)(2,1)}, u32[]{:S(2)}, u32[]{:S(2)}) %collective-permute-start.3) | collective-permute-done | bytes 524320 | tf_op jit(solution)/shard_map/ppermute | solution.py:33
  34.1 1.5 %fusion.34 = f32[512,256]{1,0:T(8,128)S(1)} fusion(bf16[512,1024]{1,0:T(8,128)(2,1)S(1)} %get-tuple-element.9, bf16[1024,256]{1,0:T(8,128)(2,1)} %collective-permute-done.3), kind=kOutput, calls=%fused_computation.89 | convolution fusion | flops 268435456 | bytes 2097152 | tf_op jit(solution)/shard_map/dot_general | solution.py:14
  35.6 1.5 %convolution_add_fusion = f32[512,256]{1,0:T(8,128)S(1)} fusion(f32[512,256]{1,0:T(8,128)S(1)} %fusion.34, bf16[512,1024]{1,0:T(8,128)(2,1)S(1)} %get-tuple-element.8, bf16[1024,256]{1,0:T(8,128)(2,1)} %constant_dynamic-update-slice_fusion), kind=kOutput, calls=%fused_computation.4 | convolution fusion | flops 268566528 | bytes 2621440 | tf_op jit(solution)/shard_map/dot_general | solution.py:14
  37.8 1.0 %collective-permute-done.4 = f32[256,256]{1,0:T(8,128)S(1)} collective-permute-done((f32[256,256]{1,0:T(8,128)S(1)}, f32[256,256]{1,0:T(8,128)S(1)}, u32[]{:S(2)}, u32[]{:S(2)}) %collective-permute-start.4) | collective-permute-done | bytes 262176 | tf_op jit(solution)/shard_map/ppermute | solution.py:37
  39.1 1.0 %multiply_convert_fusion = (bf16[256,256]{1,0:T(8,128)(2,1)S(1)}, f32[256,256]{1,0:T(8,128)}, f32[256,256]{1,0:T(8,128)}) fusion(bf16[128,256]{1,0:T(8,128)(2,1)S(1)} %collective-permute-done.5, bf16[128,256]{1,0:T(8,128)(2,1)S(1)} %copy-done.11, f32[256]{0:T(256)S(1)} %copy-done.17, f32[256,256]{1,0:T(8,128)S(1)} %fusion.35, ...), kind=kOutput, calls=%fused_computation.23 | convolution fusion | flops 34471936 | bytes 1442816 | tf_op jit(solution)/shard_map/dot_general | solution.py:14
  40.6 1.2 %convolution_convert_fusion = bf16[1024,256]{1,0:T(8,128)(2,1)} fusion(bf16[1024,512]{1,0:T(8,128)(2,1)S(1)} %get-tuple-element.11, bf16[256,256]{1,0:T(8,128)(2,1)S(1)} %convolution_convert_fusion.1), kind=kOutput, calls=%fused_computation.3 | convolution fusion | flops 269221888 | bytes 1703936 | tf_op jit(solution)/shard_map/dot_general | solution.py:14
  41.9 2.1 %concatenate.55 = bf16[1168,256]{1,0:T(8,128)(2,1)S(1)} concatenate(bf16[1024,256]{1,0:T(8,128)(2,1)} %convolution_convert_fusion, bf16[128,256]{1,0:T(8,128)(2,1)S(1)} %get-tuple-element.33, bf16[1,256]{1,0:T(2,128)(2,1)S(1)} %get-tuple-element.29, bf16[1,256]{1,0:T(2,128)(2,1)S(1)} %get-tuple-element.28, bf16[14,256]{1,0:T(8,128)(2,1)S(1)} %broadcast.89), dimensions={0} | concatenate | bytes 1196032 | tf_op jit(solution)/shard_map/concatenate | solution.py:194
  43.9 2.1 %collective-permute-start.6 = (bf16[1168,256]{1,0:T(8,128)(2,1)S(1)}, bf16[1168,256]{1,0:T(8,128)(2,1)S(1)}, u32[]{:S(2)}, u32[]{:S(2)}) collective-permute-start(bf16[1168,256]{1,0:T(8,128)(2,1)S(1)} %concatenate.55), channel_id=1, source_target_pairs={{0,4},{1,3},{2,6},{3,1},{4,0},{5,7},{6,2},{7,5},{8,12},{9,11},{10,... | collective-permute-start | bytes 1794056 | tf_op jit(solution)/shard_map/ppermute | solution.py:33
  46.0 7.9 %collective-permute-done.6 = bf16[1168,256]{1,0:T(8,128)(2,1)S(1)} collective-permute-done((bf16[1168,256]{1,0:T(8,128)(2,1)S(1)}, bf16[1168,256]{1,0:T(8,128)(2,1)S(1)}, u32[]{:S(2)}, u32[]{:S(2)}) %collective-permute-start.6) | collective-permute-done | bytes 598048 | tf_op jit(solution)/shard_map/ppermute | solution.py:33
  56.4 2.4 %concatenate.56 = bf16[656,256]{1,0:T(8,128)(2,1)S(1)} concatenate(bf16[512,256]{1,0:T(8,128)(2,1)S(1)} %slice.234, bf16[128,256]{1,0:T(8,128)(2,1)} %fusion.11, bf16[1,256]{1,0:T(2,128)(2,1)} %reduce-precision_convert_fusion.3, bf16[1,256]{1,0:T(2,128)(2,1)} %get-tuple-element.18, bf16[14,256]{1,0:T(8,128)(2,1)} %copy-done.8), dimensions={0} | concatenate | bytes 671744 | tf_op jit(solution)/shard_map/concatenate | solution.py:194
  58.8 2.1 %collective-permute-start.7 = (bf16[656,256]{1,0:T(8,128)(2,1)S(1)}, bf16[656,256]{1,0:T(8,128)(2,1)S(1)}, u32[]{:S(2)}, u32[]{:S(2)}) collective-permute-start(bf16[656,256]{1,0:T(8,128)(2,1)S(1)} %concatenate.56), channel_id=1, source_target_pairs={{0,2},{1,5},{2,0},{3,7},{4,6},{5,1},{6,4},{7,3},{8,10},{9,13},{10,... | collective-permute-start | bytes 1007624 | tf_op jit(solution)/shard_map/ppermute | solution.py:33
  60.9 5.2 %collective-permute-done.7 = bf16[656,256]{1,0:T(8,128)(2,1)S(1)} collective-permute-done((bf16[656,256]{1,0:T(8,128)(2,1)S(1)}, bf16[656,256]{1,0:T(8,128)(2,1)S(1)}, u32[]{:S(2)}, u32[]{:S(2)}) %collective-permute-start.7) | collective-permute-done | bytes 335904 | tf_op jit(solution)/shard_map/ppermute | solution.py:33
  68.3 10.8 %collective-permute-done.8 = bf16[400,256]{1,0:T(8,128)(2,1)S(1)} collective-permute-done((bf16[400,256]{1,0:T(8,128)(2,1)S(1)}, bf16[400,256]{1,0:T(8,128)(2,1)S(1)}, u32[]{:S(2)}, u32[]{:S(2)}) %collective-permute-start.8) | collective-permute-done | bytes 204832 | tf_op jit(solution)/shard_map/ppermute | solution.py:33
  79.6 4.9 %collective-permute-done.9 = bf16[272,256]{1,0:T(8,128)(2,1)S(1)} collective-permute-done((bf16[272,256]{1,0:T(8,128)(2,1)S(1)}, bf16[272,256]{1,0:T(8,128)(2,1)S(1)}, u32[]{:S(2)}, u32[]{:S(2)}) %collective-permute-start.9) | collective-permute-done | bytes 139296 | tf_op jit(solution)/shard_map/ppermute | solution.py:33
  (104 shorter events, 14.8 us)
Async XLA Ops:
  0.6 38.3 %copy-start = (bf16[256,256]{1,0:T(8,128)(2,1)S(1)}, bf16[256,256]{1,0:T(8,128)(2,1)}, u32[]{:S(2)}) copy-start(bf16[256,256]{1,0:T(8,128)(2,1)} %param.10) | copy-start | bytes 393220
  0.6 26.0 %copy-start.19 = (s32[16]{0:T(128)S(1)}, s32[16]{0:T(128)}, u32[]{:S(2)}) copy-start(s32[16]{0:T(128)} %constant.77.clone) | copy-start | bytes 196
  0.7 26.0 %copy-start.20 = (s32[16]{0:T(128)S(1)}, s32[16]{0:T(128)}, u32[]{:S(2)}) copy-start(s32[16]{0:T(128)} %constant.78.clone) | copy-start | bytes 196
  0.7 26.0 %copy-start.18 = (s32[1,1,16,2]{2,3,1,0:T(2,128)S(1)}, s32[1,1,16,2]{2,3,1,0:T(2,128)}, u32[]{:S(2)}) copy-start(s32[1,1,16,2]{2,3,1,0:T(2,128)} %param.13) | copy-start | bytes 388
  0.7 26.7 %copy-start.2 = (s32[1,1,16]{2,1,0:T(1,128)S(1)}, s32[1,1,16]{2,1,0:T(1,128)}, u32[]{:S(2)}) copy-start(s32[1,1,16]{2,1,0:T(1,128)} %param.14) | copy-start | bytes 196
  0.7 6.2 %collective-permute-start = (bf16[128,256]{1,0:T(8,128)(2,1)}, bf16[128,256]{1,0:T(8,128)(2,1)S(1)}, u32[]{:S(2)}, u32[]{:S(2)}) collective-permute-start(bf16[128,256]{1,0:T(8,128)(2,1)} %param.9), channel_id=1, source_target_pairs={{0,8},{1,17},{2,10},{3,19},{4,12},{5,21},{6,14},{7,23},{8,0},{9,25... | collective-permute-start | bytes 196616 | tf_op jit(solution)/shard_map/ppermute | solution.py:33
  7.8 20.4 %copy-start.1 = (bf16[1,1,16,2,128,128]{5,4,3,2,1,0:T(8,128)(2,1)S(1)}, bf16[1,1,16,2,128,128]{5,4,3,2,1,0:T(8,128)(2,1)}, u32[]{:S(2)}) copy-start(bf16[1,1,16,2,128,128]{5,4,3,2,1,0:T(8,128)(2,1)} %param.12) | copy-start | bytes 3145732
  7.8 6.0 %collective-permute-start.1 = (bf16[256,256]{1,0:T(8,128)(2,1)S(1)}, bf16[256,256]{1,0:T(8,128)(2,1)S(1)}, u32[]{:S(2)}, u32[]{:S(2)}) collective-permute-start(bf16[256,256]{1,0:T(8,128)(2,1)S(1)} %pad_maximum_fusion.8), channel_id=1, source_target_pairs={{0,16},{1,9},{2,18},{3,11},{4,20},{5,13},{6,22},{7,15},{8,24},{9,1... | collective-permute-start | bytes 393224 | tf_op jit(solution)/shard_map/ppermute | solution.py:33
  14.6 8.8 %collective-permute-start.2 = (bf16[512,256]{1,0:T(8,128)(2,1)S(1)}, bf16[512,256]{1,0:T(8,128)(2,1)S(1)}, u32[]{:S(2)}, u32[]{:S(2)}) collective-permute-start(bf16[512,256]{1,0:T(8,128)(2,1)S(1)} %pad_maximum_fusion.1), channel_id=1, source_target_pairs={{0,2},{1,5},{2,0},{3,7},{4,6},{5,1},{6,4},{7,3},{8,10},{9,13},{10,... | collective-permute-start | bytes 786440 | tf_op jit(solution)/shard_map/ppermute | solution.py:33
  24.1 10.0 %collective-permute-start.3 = (bf16[1024,256]{1,0:T(8,128)(2,1)}, bf16[1024,256]{1,0:T(8,128)(2,1)}, u32[]{:S(2)}, u32[]{:S(2)}) collective-permute-start(bf16[1024,256]{1,0:T(8,128)(2,1)} %constant_dynamic-update-slice_fusion), channel_id=1, source_target_pairs={{0,4},{1,3},{2,6},{3,1},{4,0},{5,7},{6,2},{7,5},{8,12},{9,11},{10,... | collective-permute-start | bytes 1572872 | tf_op jit(solution)/shard_map/ppermute | solution.py:33
  37.2 1.6 %collective-permute-start.4 = (f32[256,256]{1,0:T(8,128)S(1)}, f32[256,256]{1,0:T(8,128)S(1)}, u32[]{:S(2)}, u32[]{:S(2)}) collective-permute-start(f32[256,256]{1,0:T(8,128)S(1)} %reduce_sum.29), channel_id=1, source_target_pairs={{0,1},{1,0},{2,3},{3,2},{4,5},{5,4},{6,7},{7,6},{8,9},{9,8},{10,11... | collective-permute-start | bytes 786440 | tf_op jit(solution)/shard_map/ppermute | solution.py:37
  37.3 1.8 %collective-permute-start.5 = (bf16[128,256]{1,0:T(8,128)(2,1)S(1)}, bf16[128,256]{1,0:T(8,128)(2,1)S(1)}, u32[]{:S(2)}, u32[]{:S(2)}) collective-permute-start(bf16[128,256]{1,0:T(8,128)(2,1)S(1)} %copy-done.11), channel_id=1, source_target_pairs={{0,1},{1,0},{2,3},{3,2},{4,5},{5,4},{6,7},{7,6},{8,9},{9,8},{10,11... | collective-permute-start | bytes 196616 | tf_op jit(solution)/shard_map/ppermute | solution.py:37
  43.9 12.0 %copy-start.7 = (bf16[256,256]{1,0:T(8,128)(2,1)S(1)}, bf16[256,256]{1,0:T(8,128)(2,1)}, u32[]{:S(2)}) copy-start(bf16[256,256]{1,0:T(8,128)(2,1)} %copy-done.6) | copy-start | bytes 393220
  43.9 10.0 %collective-permute-start.6 = (bf16[1168,256]{1,0:T(8,128)(2,1)S(1)}, bf16[1168,256]{1,0:T(8,128)(2,1)S(1)}, u32[]{:S(2)}, u32[]{:S(2)}) collective-permute-start(bf16[1168,256]{1,0:T(8,128)(2,1)S(1)} %concatenate.55), channel_id=1, source_target_pairs={{0,4},{1,3},{2,6},{3,1},{4,0},{5,7},{6,2},{7,5},{8,12},{9,11},{10,... | collective-permute-start | bytes 1794056 | tf_op jit(solution)/shard_map/ppermute | solution.py:33
  56.3 9.8 %copy-start.15 = (f32[1,256]{1,0:T(1,128)S(1)}, f32[1,256]{1,0:T(1,128)}, u32[]{:S(2)}) copy-start(f32[1,256]{1,0:T(1,128)} %copy-done.14) | copy-start | bytes 3076
  58.8 7.2 %collective-permute-start.7 = (bf16[656,256]{1,0:T(8,128)(2,1)S(1)}, bf16[656,256]{1,0:T(8,128)(2,1)S(1)}, u32[]{:S(2)}, u32[]{:S(2)}) collective-permute-start(bf16[656,256]{1,0:T(8,128)(2,1)S(1)} %concatenate.56), channel_id=1, source_target_pairs={{0,2},{1,5},{2,0},{3,7},{4,6},{5,1},{6,4},{7,3},{8,10},{9,13},{10,... | collective-permute-start | bytes 1007624 | tf_op jit(solution)/shard_map/ppermute | solution.py:33
  67.4 11.8 %copy-start.3 = (f32[128,256]{1,0:T(8,128)S(1)}, f32[128,256]{1,0:T(8,128)}, u32[]{:S(2)}) copy-start(f32[128,256]{1,0:T(8,128)} %get-tuple-element.17) | copy-start | bytes 393220
  67.4 11.7 %copy-start.13 = (f32[1,256]{1,0:T(1,128)S(1)}, f32[1,256]{1,0:T(1,128)}, u32[]{:S(2)}) copy-start(f32[1,256]{1,0:T(1,128)} %copy-done.12) | copy-start | bytes 3076
  67.5 11.8 %copy-start.10 = (bf16[14,256]{1,0:T(8,128)(2,1)S(1)}, bf16[14,256]{1,0:T(8,128)(2,1)}, u32[]{:S(2)}) copy-start(bf16[14,256]{1,0:T(8,128)(2,1)} %copy-done.8) | copy-start | bytes 21508
  68.2 10.9 %collective-permute-start.8 = (bf16[400,256]{1,0:T(8,128)(2,1)S(1)}, bf16[400,256]{1,0:T(8,128)(2,1)S(1)}, u32[]{:S(2)}, u32[]{:S(2)}) collective-permute-start(bf16[400,256]{1,0:T(8,128)(2,1)S(1)} %concatenate.57), channel_id=1, source_target_pairs={{0,16},{1,9},{2,18},{3,11},{4,20},{5,13},{6,22},{7,15},{8,24},{9,1... | collective-permute-start | bytes 614408 | tf_op jit(solution)/shard_map/ppermute | solution.py:33
  79.2 6.3 %copy-start.4 = (f32[256,256]{1,0:T(8,128)S(1)}, f32[256,256]{1,0:T(8,128)}, u32[]{:S(2)}) copy-start(f32[256,256]{1,0:T(8,128)} %get-tuple-element.25) | copy-start | bytes 786436
  79.2 6.3 %copy-start.5 = (f32[256,256]{1,0:T(8,128)S(1)}, f32[256,256]{1,0:T(8,128)}, u32[]{:S(2)}) copy-start(f32[256,256]{1,0:T(8,128)} %get-tuple-element.32) | copy-start | bytes 786436
  79.4 5.1 %collective-permute-start.9 = (bf16[272,256]{1,0:T(8,128)(2,1)S(1)}, bf16[272,256]{1,0:T(8,128)(2,1)S(1)}, u32[]{:S(2)}, u32[]{:S(2)}) collective-permute-start(bf16[272,256]{1,0:T(8,128)(2,1)S(1)} %concatenate.58), channel_id=1, source_target_pairs={{0,8},{1,17},{2,10},{3,19},{4,12},{5,21},{6,14},{7,23},{8,0},{9,25... | collective-permute-start | bytes 417800 | tf_op jit(solution)/shard_map/ppermute | solution.py:33
  85.4 1.4 %collective-permute-start.10 = (f32[1,136,256]{2,1,0:T(8,128)S(1)}, f32[1,136,256]{2,1,0:T(8,128)S(1)}, u32[]{:S(2)}, u32[]{:S(2)}) collective-permute-start(f32[1,136,256]{2,1,0:T(8,128)S(1)} %maximum_multiply_fusion), channel_id=1, source_target_pairs={{0,1},{1,0},{2,3},{3,2},{4,5},{5,4},{6,7},{7,6},{8,9},{9,8},{10,11... | collective-permute-start | bytes 417800 | tf_op jit(solution)/shard_map/ppermute | solution.py:37
  (8 other events, 12.2 us)

commit v2 on v1

v2 whole, which is shorter than its diff:
```python
from functools import partial

import jax
import jax.numpy as jnp
from jax import lax
from jax.experimental import pallas as pl
from jax.experimental.pallas import tpu as pltpu
from jax.sharding import PartitionSpec as P

BF16 = jnp.bfloat16
F32 = jnp.float32
DENSE_BYTES = 4 << 20


def dot(left, right, contract=((1,), (0,))):
    return lax.dot_general(left, right, (contract, ((), ())), preferred_element_type=F32)


def axis_orders(loop_size):
    bits = [1 << b for b in range(loop_size.bit_length() - 1)]
    low, high = bits[: len(bits) // 2], bits[len(bits) // 2 :]
    return (high + low, high[::-1] + low[::-1])


def exchange(value, step, orders, loop_size, rep_size):
    pairs = []
    for place in range(loop_size):
        for rep in range(rep_size):
            partner = place ^ orders[rep % 2][step]
            pairs.append((place * rep_size + rep, partner * rep_size + rep))
    return lax.ppermute(value, ("loop", "rep"), pairs)


def swap_rep(value, mask, rep_size):
    return lax.ppermute(value, "rep", [(r, r ^ mask) for r in range(rep_size)])


def partner_masks(order):
    masks = [0]
    for bit in order:
        masks = masks + [m ^ bit for m in masks]
    return masks


def scatter_tiles(row_ref, tiles_ref, k, out, out_t, first):
    slots, tile = tiles_ref.shape[1], tiles_ref.shape[2]
    panel = out_t.shape[1] // (slots * tile)
    source = row_ref[k, slots]
    cols = pl.ds((k - first) * tile, tile)
    for s in range(slots):
        one = tiles_ref[source, s]
        one_t = one.T
        for t in range(panel):
            keep = (row_ref[k, s] == t).astype(BF16)
            rows = pl.ds((s * panel + t) * tile, tile)
            out[rows, cols] = one * keep
            out_t[cols, rows] = one_t * keep


def fold(both):
    half = both.shape[0] // 2
    return both[:half] + both[half:]


def near_kernel(row_ref, tiles_ref, right_ref, sums_ref, far_ref, near_t_ref, far_t_ref, near_ref):
    partners = tiles_ref.shape[0]
    half = partners // 2
    for k in range(half):
        scatter_tiles(row_ref, tiles_ref, k, near_ref, near_t_ref, 0)
    sums_ref[...] = fold(dot(near_ref[...], right_ref[...]))
    for k in range(half, partners):
        scatter_tiles(row_ref, tiles_ref, k, far_ref, far_t_ref, half)


def far_kernel(sums_ref, far_ref, right_ref, out_ref):
    out_ref[...] = sums_ref[...] + fold(dot(far_ref[...], right_ref[...]))


def split(value):
    high = value.astype(BF16)
    return high, (value - high.astype(F32)).astype(BF16)


def exp_less_one(value, grown):
    series = value * (1.0 + value * (1 / 2 + value * (1 / 6 + value * (1 / 24))))
    return jnp.where(value > -0.0625, series, grown - 1.0)


def middle_kernel(
    mine_ref, other_ref, weight_ref, bias_ref, own_ref, pair_ref, far_t_ref,
    message_ref, output_ref, back_ref, grad_ref, sums_ref,
):
    rows = own_ref.shape[0]
    sums_ref[:rows] = mine_ref[:rows] + other_ref[rows:]
    sums_ref[rows:] = mine_ref[rows:] + other_ref[:rows]
    high, low = split(sums_ref[...])
    weight = weight_ref[...]
    preact = dot(high, weight) + dot(low, weight) + bias_ref[...]
    negative = jnp.minimum(preact, 0.0)
    grown = jnp.exp(negative)
    slope = jnp.where(preact > 0, 1.0, grown)
    own = preact[:rows]
    below = exp_less_one(negative[:rows], grown[:rows])
    output_ref[...] = jnp.where(own > 0, own, below).astype(BF16)
    grad_ref[:rows] = (own_ref[...].astype(F32) * slope[:rows]).astype(BF16)
    grad_ref[rows:] = (pair_ref[...].astype(F32) * slope[rows:]).astype(BF16)
    back = dot(grad_ref[...], weight, ((1,), (1,))).astype(BF16)
    back_ref[: 2 * rows] = back
    back_ref[2 * rows :] = back
    message_ref[...] = dot(far_t_ref[...], back_ref[...]).astype(BF16)


def keep_kernel(rep_ref, near_t_ref, back_ref, grad_ref, sums_ref, keep_ref, term_ref):
    share = term_ref.shape[0] - 8
    sums = sums_ref[...]
    mine = jnp.where(rep_ref[0, 0] == 0, sums[:, :share], sums[:, share:])
    high, low = split(mine)
    grad = grad_ref[...]
    rows = ((0,), (0,))
    term_ref[:share] = dot(high, grad, rows) + dot(low, grad, rows)
    own = grad[: grad.shape[0] // 2].astype(F32)
    term_ref[share:] = jnp.broadcast_to(jnp.sum(own, axis=0, keepdims=True), (8, own.shape[1]))
    keep_ref[...] = dot(near_t_ref[...], back_ref[...])


def final_kernel(rep_ref, mine_ref, other_ref, weight_ref, bias_ref, *, scale):
    share = weight_ref.shape[0] // 2
    mine, other = mine_ref[...] * scale, other_ref[...] * scale
    first = rep_ref[0, 0] == 0
    weight_ref[:share] = jnp.where(first, mine[:share], other[:share])
    weight_ref[share:] = jnp.where(first, other[:share], mine[:share])
    bias_ref[...] = mine[share : share + 1] + other[share : share + 1]


def on_chip(kernel, shapes, scratch=(), scalars=0):
    vmem = pl.BlockSpec(memory_space=pltpu.VMEM)
    smem = pl.BlockSpec(memory_space=pltpu.SMEM)

    def call(*operands):
        return pl.pallas_call(
            kernel,
            out_shape=tuple(jax.ShapeDtypeStruct(*shape) for shape in shapes),
            in_specs=[smem] * scalars + [vmem] * (len(operands) - scalars),
            out_specs=(vmem,) * len(shapes),
            scratch_shapes=list(scratch),
            compiler_params=pltpu.CompilerParams(vmem_limit_bytes=40 << 20),
        )(*operands)

    return call


def tile_loop(target, source, partner, tiles, totals, right_of, product_of, place_of):
    slots = tiles.shape[1]

    def one(number, totals):
        k, s = number // slots, number % slots
        product = product_of(tiles[partner[k], s], right_of(k, s))
        product = product * (target[k, s] >= 0).astype(F32)
        start = place_of(k, s)
        earlier = lax.dynamic_slice_in_dim(totals, start, product.shape[0], 0)
        return lax.dynamic_update_slice_in_dim(totals, earlier + product, start, 0)

    return lax.fori_loop(0, target.shape[0] * slots, one, totals)


def body(node_features, weight, bias_vector, tile_values, tile_place, tile_count, cotangent):
    loop_size = lax.axis_size("loop")
    rep_size = lax.axis_size("rep")
    position = lax.axis_index("loop").astype(jnp.int32)
    rep = lax.axis_index("rep").astype(jnp.int32)
    rows_own, width_in = node_features.shape
    width_out = weight.shape[1]
    _, _, partners, slots, tile, _ = tile_values.shape
    per_side = rows_own // tile
    panel = rep_size * per_side
    orders = axis_orders(loop_size)
    steps = len(orders[0])
    half = partners // 2
    share = width_in // rep_size
    scale_factor = float(rows_own * loop_size * rep_size) ** (-0.5)
    tiles = tile_values[0, 0]
    rep_bits = [1 << bit for bit in range(rep_size.bit_length() - 1)]
    dense_bytes = 2 * slots * panel * tile * partners * tile
    dense = per_side == 1 and rep_size == 2 and slots == 2 and dense_bytes <= DENSE_BYTES

    masks = jnp.where(
        rep % 2 == 0,
        jnp.array(partner_masks(orders[0]), jnp.int32),
        jnp.array(partner_masks(orders[1]), jnp.int32),
    )
    partner = jnp.bitwise_xor(position, masks)
    places = tile_place[0, 0][partner]
    target = places // per_side
    target = jnp.bitwise_xor(target // per_side, rep) * per_side + target % per_side
    live = jnp.arange(slots, dtype=jnp.int32)[None, :] < tile_count[0, 0][partner][:, None]
    target = jnp.where(live, target, -1)

    gathered = node_features
    for step in range(steps - 1):
        gathered = jnp.concatenate(
            [gathered, exchange(gathered, step, orders, loop_size, rep_size)], axis=0
        )
    arriving = exchange(gathered, steps - 1, orders, loop_size, rep_size)

    cotangent_rows = [cotangent]
    for bit in rep_bits:
        cotangent_rows += [swap_rep(rows, bit, rep_size) for rows in cotangent_rows]

    if dense:
        table = jnp.concatenate([target, partner[:, None]], axis=1)
        wide, deep, rows = half * tile, slots * panel * tile, panel * tile
        rep_word = rep.reshape(1, 1)
        sums, far, near_t, far_t = on_chip(
            near_kernel,
            [((rows, width_in), F32), ((deep, wide), BF16), ((wide, deep), BF16), ((wide, deep), BF16)],
            [pltpu.VMEM((deep, wide), BF16)],
            1,
        )(table, tiles, gathered)
        (sums,) = on_chip(far_kernel, [((rows, width_in), F32)])(sums, far, arriving)
        other = swap_rep(sums, 1, rep_size)
        sending, output, back, grad_pre, sums = on_chip(
            middle_kernel,
            [
                ((wide, width_in), BF16),
                ((rows_own, width_out), BF16),
                ((slots * rows, width_in), BF16),
                ((rows, width_out), BF16),
                ((rows, width_in), F32),
            ],
        )(sums, other, weight, bias_vector.reshape(1, width_out), *cotangent_rows, far_t)
        keeping, term = on_chip(
            keep_kernel, [((wide, width_in), F32), ((share + 8, width_out), F32)], (), 1
        )(rep_word, near_t, back, grad_pre, sums)
    else:
        source = places % per_side
        everything = jnp.concatenate([gathered, arriving], axis=0)
        sums = tile_loop(
            target, source, partner, tiles, jnp.zeros((panel * tile, width_in), F32),
            lambda k, s: lax.dynamic_slice_in_dim(
                everything, k * rows_own + source[k, s] * tile, tile, 0
            ),
            dot,
            lambda k, s: jnp.maximum(target[k, s], 0) * tile,
        )
        for bit in rep_bits:
            other = swap_rep(sums, bit, rep_size)
            blocks = other.reshape(rep_size, rows_own, width_in)
            blocks = jnp.stack([blocks[t ^ bit] for t in range(rep_size)])
            sums = sums + blocks.reshape(sums.shape)
        high = lax.reduce_precision(sums, 8, 7)
        low = (sums - high).astype(BF16)
        high = high.astype(BF16)
        preact = dot(high, weight) + dot(low, weight) + bias_vector[None, :]
        negative = jnp.minimum(preact, 0.0)
        own = preact[:rows_own]
        output = jnp.where(own > 0, own, jnp.expm1(negative[:rows_own])).astype(BF16)
        slope = jnp.where(preact > 0, 1.0, jnp.exp(negative))
        cotangent_rows = jnp.concatenate(cotangent_rows, axis=0)
        grad_pre = (cotangent_rows.astype(F32) * slope).astype(BF16)
        back = dot(grad_pre, weight, ((1,), (1,))).astype(BF16)
        start = rep * share
        term = dot(lax.dynamic_slice_in_dim(high, start, share, 1), grad_pre, ((0,), (0,)))
        term = term + dot(lax.dynamic_slice_in_dim(low, start, share, 1), grad_pre, ((0,), (0,)))
        bias_term = jnp.sum(grad_pre[:rows_own].astype(F32), axis=0, keepdims=True)
        term = jnp.concatenate([term, jnp.broadcast_to(bias_term, (8, width_out))], axis=0)
        adjoint = tile_loop(
            target, source, partner, tiles, jnp.zeros((partners * rows_own, width_in), F32),
            lambda k, s: lax.dynamic_slice_in_dim(
                back, jnp.maximum(target[k, s], 0) * tile, tile, 0
            ),
            lambda left, right: dot(left, right, ((0,), (0,))),
            lambda k, s: k * rows_own + source[k, s] * tile,
        )
        keeping, sending = adjoint[: half * rows_own], adjoint[half * rows_own :].astype(BF16)

    received = []
    for step in range(steps - 1, -1, -1):
        received.append(exchange(sending, step, orders, loop_size, rep_size))
        term = term + exchange(term, (step + steps // 2) % steps, orders, loop_size, rep_size)
        size = sending.shape[0] // 2 if step else 0
        end = 2 * size if step else rows_own
        total = keeping[size:end]
        for part in received:
            total = total + part[size:end].astype(F32)
        sending = total.astype(BF16)
    grad_features = sending

    if dense:
        grad_weight, grad_bias = on_chip(
            partial(final_kernel, scale=scale_factor),
            [((width_in, width_out), F32), ((1, width_out), F32)],
            (),
            1,
        )(rep_word, term, swap_rep(term, 1, rep_size))
        grad_bias = grad_bias.reshape(width_out)
    else:
        shares = term[None] * scale_factor
        for bit in rep_bits:
            shares = jnp.concatenate([shares, swap_rep(shares, bit, rep_size)], axis=0)
        shares = shares[jnp.bitwise_xor(jnp.arange(rep_size, dtype=jnp.int32), rep)]
        grad_weight = shares[:, :share].reshape(width_in, width_out)
        grad_bias = jnp.sum(shares[:, share], axis=0)
    return (output, grad_features, grad_weight, grad_bias)


def solution(mesh):
    return jax.shard_map(
        body,
        mesh=mesh,
        in_specs=(
            P(("loop", "rep"), None),
            P(),
            P(),
            P("loop", "rep", None, None, None, None),
            P("loop", "rep", None, None),
            P("loop", "rep", None),
            P(("loop", "rep"), None),
        ),
        out_specs=(P(("loop", "rep"), None), P(("loop", "rep"), None), P(), P()),
        check_vma=False,
    )
```

time: 89.2 us -> 72.7 us (0.82)
  local copies, waits for them, and re-layouts: 11.7 us -> 3.13 us
  matrix products: 6.27 us -> 0 us
  other arithmetic: 7.43 us -> 1.92 us
  starting transfers between devices: 16.1 us -> 21.4 us
  waiting for transfers between devices: 44.6 us -> 41.1 us
  Pallas kernels: 1.45 us -> 4.13 us
    dot_general x8 -> x0, matrix products: 6.27 us -> none  [dot(): lax.dot_general(left, right, (contract, ((), ())), preferred_element_type...]
    ppermute x8 -> x12, starting transfers between devices: 15.4 us -> 21.1 us  [exchange(): return lax.ppermute(value, ('loop', 'rep'), pairs)]
    concatenate x5 -> x0, local copies, waits for them, and re-layouts: 4.89 us -> none  [the longest x4 4.82 us: body(): jnp.concatenate([sending.astype(BF16), weight_term.astype(BF16), bias_hig...]
    convert_element_type x15 -> x4, other arithmetic: 3.93 us -> 0.81 us  [body(): sending = total.astype(BF16)]
    ppermute x8 -> x12, waiting for transfers between devices: 43 us -> 40 us  [exchange(): return lax.ppermute(value, ('loop', 'rep'), pairs)]
    pallas_call x1 -> x5, Pallas kernels: 1.45 us -> 4.13 us  [call(): pl.pallas_call(kernel, out_shape=tuple((jax.ShapeDtypeStruct(*shape) for...]
    unnamed x45 -> x21, local copies, waits for them, and re-layouts: 3.36 us -> 1.73 us
  transfers between devices with their start and end apart: 11 -> 15, of which waited for: 10 -> 11; matrix products, arithmetic and copies ran while one was open for 6% -> 2% of each run, Pallas kernels for 2% -> 4%
where the time goes in v2:
time: 72.7 us; the launch traced here: 72.5 us
  waiting for transfers between devices  41.1 us (57%)
  starting transfers between devices  21.4 us (29%)
  Pallas kernels  4.13 us (6%)
  local copies, waits for them, and re-layouts  3.13 us (4%)
  other arithmetic  1.92 us (3%)
  between operations  0.84 us (1%)
    ppermute x12, waiting for transfers between devices, exchange(): return lax.ppermute(value, ('loop', 'rep'), pairs)  40 us
    ppermute x12, starting transfers between devices, exchange(): return lax.ppermute(value, ('loop', 'rep'), pairs)  21.1 us
    pallas_call x5, Pallas kernels, call(): pl.pallas_call(kernel, out_shape=tuple((jax.ShapeDtypeStruct(*shape) for...  4.13 us
    unnamed x21, local copies, waits for them, and re-layouts  1.73 us
  transfers between devices with their start and end apart: 15, of which 11 were waited for; matrix products, arithmetic and copies ran while one was open for 2% of the time, Pallas kernels for 4%

profile of v2, /device:TPU:0, one launch (start us, length us, event | category | flops | bytes accessed | tf_op | source)
XLA Modules:
  0.0 72.5 jit_solution(10002928132989623897)
XLA Ops:
  0.7 3.1 %collective-permute-start = (bf16[128,256]{1,0:T(8,128)(2,1)}, bf16[128,256]{1,0:T(8,128)(2,1)S(1)}, u32[]{:S(2)}, u32[]{:S(2)}) collective-permute-start(bf16[128,256]{1,0:T(8,128)(2,1)} %param.9), channel_id=1, source_target_pairs={{0,8},{1,17},{2,10},{3,19},{4,12},{5,21},{6,14},{7,23},{8,0},{9,25... | collective-permute-start | bytes 196616 | tf_op jit(solution)/shard_map/ppermute | solution.py:31
  3.7 3.2 %collective-permute-done = bf16[128,256]{1,0:T(8,128)(2,1)S(1)} collective-permute-done((bf16[128,256]{1,0:T(8,128)(2,1)}, bf16[128,256]{1,0:T(8,128)(2,1)S(1)}, u32[]{:S(2)}, u32[]{:S(2)}) %collective-permute-start) | collective-permute-done | bytes 65568 | tf_op jit(solution)/shard_map/ppermute | solution.py:31
  6.9 0.8 %pad_maximum_fusion.1 = bf16[256,256]{1,0:T(8,128)(2,1)S(1)} fusion(bf16[128,256]{1,0:T(8,128)(2,1)S(1)} %collective-permute-done, bf16[128,256]{1,0:T(8,128)(2,1)} %param.9), kind=kLoop, calls=%fused_computation.5 | loop fusion | flops 262144 | bytes 262144 | tf_op jit(solution)/shard_map/concatenate | solution.py:200
  7.8 2.4 %collective-permute-start.1 = (bf16[256,256]{1,0:T(8,128)(2,1)S(1)}, bf16[256,256]{1,0:T(8,128)(2,1)S(1)}, u32[]{:S(2)}, u32[]{:S(2)}) collective-permute-start(bf16[256,256]{1,0:T(8,128)(2,1)S(1)} %pad_maximum_fusion.1), channel_id=1, source_target_pairs={{0,16},{1,9},{2,18},{3,11},{4,20},{5,13},{6,22},{7,15},{8,24},{9,1... | collective-permute-start | bytes 393224 | tf_op jit(solution)/shard_map/ppermute | solution.py:31
  10.2 3.6 %collective-permute-done.1 = bf16[256,256]{1,0:T(8,128)(2,1)S(1)} collective-permute-done((bf16[256,256]{1,0:T(8,128)(2,1)S(1)}, bf16[256,256]{1,0:T(8,128)(2,1)S(1)}, u32[]{:S(2)}, u32[]{:S(2)}) %collective-permute-start.1) | collective-permute-done | bytes 131104 | tf_op jit(solution)/shard_map/ppermute | solution.py:31
  13.8 3.1 %collective-permute-start.2 = (bf16[512,256]{1,0:T(8,128)(2,1)S(1)}, bf16[512,256]{1,0:T(8,128)(2,1)S(1)}, u32[]{:S(2)}, u32[]{:S(2)}) collective-permute-start(bf16[512,256]{1,0:T(8,128)(2,1)S(1)} %pad_maximum_fusion), channel_id=1, source_target_pairs={{0,2},{1,5},{2,0},{3,7},{4,6},{5,1},{6,4},{7,3},{8,10},{9,13},{10,... | collective-permute-start | bytes 786440 | tf_op jit(solution)/shard_map/ppermute | solution.py:31
  17.0 6.4 %collective-permute-done.2 = bf16[512,256]{1,0:T(8,128)(2,1)S(1)} collective-permute-done((bf16[512,256]{1,0:T(8,128)(2,1)S(1)}, bf16[512,256]{1,0:T(8,128)(2,1)S(1)}, u32[]{:S(2)}, u32[]{:S(2)}) %collective-permute-start.2) | collective-permute-done | bytes 262176 | tf_op jit(solution)/shard_map/ppermute | solution.py:31
  23.4 2.6 %collective-permute-start.3 = (bf16[1024,256]{1,0:T(8,128)(2,1)S(1)}, bf16[1024,256]{1,0:T(8,128)(2,1)S(1)}, u32[]{:S(2)}, u32[]{:S(2)}) collective-permute-start(bf16[1024,256]{1,0:T(8,128)(2,1)S(1)} %constant_dynamic-update-slice_fusion.right_ref), channel_id=1, source_target_pairs={{0,4},{1,3},{2,6},{3,1},{4,0},{5,7},{6,2},{7,5},{8,12},{9,11},{10,... | collective-permute-start | bytes 1572872 | tf_op jit(solution)/shard_map/ppermute | solution.py:31
  28.3 1.5 %shard_map.120 = (f32[256,256]{1,0:T(8,128)S(1)}, bf16[512,1024]{1,0:T(8,128)(2,1)S(1)}, bf16[1024,512]{1,0:T(8,128)(2,1)S(1)}, bf16[1024,512]{1,0:T(8,128)(2,1)S(1)}) custom-call(s32[16,3]{1,0:T(8,128)S(1)} %pad_add_fusion.row_ref, bf16[16,2,128,128]{3,2,1,0:T(8,128)(2,1)S(1)} %bitcast.9, bf16[1024,256]{1,0:T(8,128)(2,1)S(1)} %constant_dynamic-update-slice_fusion.right_ref), custom_call_target="tpu_custom_call" | custom-call | tf_op jit(solution)/shard_map/pallas_call | solution.py:140
  29.8 3.4 %collective-permute-done.3.right_ref = bf16[1024,256]{1,0:T(8,128)(2,1)S(1)} collective-permute-done((bf16[1024,256]{1,0:T(8,128)(2,1)S(1)}, bf16[1024,256]{1,0:T(8,128)(2,1)S(1)}, u32[]{:S(2)}, u32[]{:S(2)}) %collective-permute-start.3) | collective-permute-done | bytes 524320 | tf_op jit(solution)/shard_map/ppermute | solution.py:31
  34.2 1.1 %collective-permute-done.5.pair_ref = bf16[128,256]{1,0:T(8,128)(2,1)S(1)} collective-permute-done((bf16[128,256]{1,0:T(8,128)(2,1)S(1)}, bf16[128,256]{1,0:T(8,128)(2,1)S(1)}, u32[]{:S(2)}, u32[]{:S(2)}) %collective-permute-start.5) | collective-permute-done | bytes 65568 | tf_op jit(solution)/shard_map/ppermute | solution.py:35
  36.0 0.9 %shard_map.122 = (bf16[1024,256]{1,0:T(8,128)(2,1)S(1)}, bf16[128,256]{1,0:T(8,128)(2,1)}, bf16[512,256]{1,0:T(8,128)(2,1)S(1)}, bf16[256,256]{1,0:T(8,128)(2,1)S(1)}, f32[256,256]{1,0:T(8,128)S(1)}) custom-call(f32[256,256]{1,0:T(8,128)S(1)} %shard_map.121.mine_ref, f32[256,256]{1,0:T(8,128)S(1)} %collective-permute-done.4.other_ref, ...), custom_call_target="tpu_custom_call" | custom-call | tf_op jit(solution)/shard_map/pallas_call | solution.py:140
  36.9 2.0 %collective-permute-start.6 = (bf16[1024,256]{1,0:T(8,128)(2,1)S(1)}, bf16[1024,256]{1,0:T(8,128)(2,1)S(1)}, u32[]{:S(2)}, u32[]{:S(2)}) collective-permute-start(bf16[1024,256]{1,0:T(8,128)(2,1)S(1)} %get-tuple-element.26), channel_id=1, source_target_pairs={{0,4},{1,3},{2,6},{3,1},{4,0},{5,7},{6,2},{7,5},{8,12},{9,11},{10,... | collective-permute-start | bytes 1572872 | tf_op jit(solution)/shard_map/ppermute | solution.py:31
  39.5 6.9 %collective-permute-done.10 = f32[136,256]{1,0:T(8,128)S(1)} collective-permute-done((f32[136,256]{1,0:T(8,128)S(1)}, f32[136,256]{1,0:T(8,128)S(1)}, u32[]{:S(2)}, u32[]{:S(2)}) %collective-permute-start.10) | collective-permute-done | bytes 139296 | tf_op jit(solution)/shard_map/ppermute | solution.py:31
  46.6 2.7 %collective-permute-start.7 = (bf16[512,256]{1,0:T(8,128)(2,1)S(1)}, bf16[512,256]{1,0:T(8,128)(2,1)S(1)}, u32[]{:S(2)}, u32[]{:S(2)}) collective-permute-start(bf16[512,256]{1,0:T(8,128)(2,1)S(1)} %add_convert_fusion), channel_id=1, source_target_pairs={{0,2},{1,5},{2,0},{3,7},{4,6},{5,1},{6,4},{7,3},{8,10},{9,13},{10,... | collective-permute-start | bytes 786440 | tf_op jit(solution)/shard_map/ppermute | solution.py:31
  49.3 2.3 %collective-permute-done.11 = f32[136,256]{1,0:T(8,128)S(1)} collective-permute-done((f32[136,256]{1,0:T(8,128)S(1)}, f32[136,256]{1,0:T(8,128)S(1)}, u32[]{:S(2)}, u32[]{:S(2)}) %collective-permute-start.11) | collective-permute-done | bytes 139296 | tf_op jit(solution)/shard_map/ppermute | solution.py:31
  51.6 1.6 %collective-permute-start.12 = (f32[136,256]{1,0:T(8,128)S(1)}, f32[136,256]{1,0:T(8,128)S(1)}, u32[]{:S(2)}, u32[]{:S(2)}) collective-permute-start(f32[136,256]{1,0:T(8,128)S(1)} %add.70), channel_id=1, source_target_pairs={{0,4},{1,3},{2,6},{3,1},{4,0},{5,7},{6,2},{7,5},{8,12},{9,11},{10,... | collective-permute-start | bytes 417800 | tf_op jit(solution)/shard_map/ppermute | solution.py:31
  53.2 3.6 %collective-permute-done.12 = f32[136,256]{1,0:T(8,128)S(1)} collective-permute-done((f32[136,256]{1,0:T(8,128)S(1)}, f32[136,256]{1,0:T(8,128)S(1)}, u32[]{:S(2)}, u32[]{:S(2)}) %collective-permute-start.12) | collective-permute-done | bytes 139296 | tf_op jit(solution)/shard_map/ppermute | solution.py:31
  56.8 3.3 %collective-permute-start.13 = (f32[136,256]{1,0:T(8,128)S(1)}, f32[136,256]{1,0:T(8,128)S(1)}, u32[]{:S(2)}, u32[]{:S(2)}) collective-permute-start(f32[136,256]{1,0:T(8,128)S(1)} %add.71), channel_id=1, source_target_pairs={{0,2},{1,5},{2,0},{3,7},{4,6},{5,1},{6,4},{7,3},{8,10},{9,13},{10,... | collective-permute-start | bytes 417800 | tf_op jit(solution)/shard_map/ppermute | solution.py:31
  60.2 2.9 %collective-permute-done.13 = f32[136,256]{1,0:T(8,128)S(1)} collective-permute-done((f32[136,256]{1,0:T(8,128)S(1)}, f32[136,256]{1,0:T(8,128)S(1)}, u32[]{:S(2)}, u32[]{:S(2)}) %collective-permute-start.13) | collective-permute-done | bytes 139296 | tf_op jit(solution)/shard_map/ppermute | solution.py:31
  63.2 4.3 %collective-permute-done.8 = bf16[256,256]{1,0:T(8,128)(2,1)S(1)} collective-permute-done((bf16[256,256]{1,0:T(8,128)(2,1)S(1)}, bf16[256,256]{1,0:T(8,128)(2,1)S(1)}, u32[]{:S(2)}, u32[]{:S(2)}) %collective-permute-start.8) | collective-permute-done | bytes 131104 | tf_op jit(solution)/shard_map/ppermute | solution.py:31
  67.6 0.7 %shard_map.124 = (f32[256,256]{1,0:T(8,128)}, f32[1,256]{1,0:T(1,128)}) custom-call(s32[1,1]{1,0:T(1,128)} %bitcast.5.rep_ref, f32[136,256]{1,0:T(8,128)S(1)} %add.72.mine_ref, f32[136,256]{1,0:T(8,128)S(1)} %collective-permute-done.14.other_ref), custom_call_target="tpu_custom_call" | custom-call | tf_op jit(solution)/shard_map/pallas_call | solution.py:140
  68.4 3.5 %collective-permute-done.9 = bf16[128,256]{1,0:T(8,128)(2,1)S(1)} collective-permute-done((bf16[128,256]{1,0:T(8,128)(2,1)S(1)}, bf16[128,256]{1,0:T(8,128)(2,1)S(1)}, u32[]{:S(2)}, u32[]{:S(2)}) %collective-permute-start.9) | collective-permute-done | bytes 65568 | tf_op jit(solution)/shard_map/ppermute | solution.py:31
  71.9 0.7 add_convert_fusion.2
  (51 shorter events, 5.1 us)
Async XLA Ops:
  0.6 26.7 %copy-start = (s32[1,1,16]{2,1,0:T(1,128)S(1)}, s32[1,1,16]{2,1,0:T(1,128)}, u32[]{:S(2)}) copy-start(s32[1,1,16]{2,1,0:T(1,128)} %param.14) | copy-start | bytes 196
  0.6 13.1 %copy-start.5 = (bf16[128,256]{1,0:T(8,128)(2,1)S(1)}, bf16[128,256]{1,0:T(8,128)(2,1)}, u32[]{:S(2)}) copy-start(bf16[128,256]{1,0:T(8,128)(2,1)} %param.9) | copy-start | bytes 196612
  0.7 6.2 %collective-permute-start = (bf16[128,256]{1,0:T(8,128)(2,1)}, bf16[128,256]{1,0:T(8,128)(2,1)S(1)}, u32[]{:S(2)}, u32[]{:S(2)}) collective-permute-start(bf16[128,256]{1,0:T(8,128)(2,1)} %param.9), channel_id=1, source_target_pairs={{0,8},{1,17},{2,10},{3,19},{4,12},{5,21},{6,14},{7,23},{8,0},{9,25... | collective-permute-start | bytes 196616 | tf_op jit(solution)/shard_map/ppermute | solution.py:31
  7.8 20.5 %copy-start.1 = (bf16[1,1,16,2,128,128]{5,4,3,2,1,0:T(8,128)(2,1)S(1)}, bf16[1,1,16,2,128,128]{5,4,3,2,1,0:T(8,128)(2,1)}, u32[]{:S(2)}) copy-start(bf16[1,1,16,2,128,128]{5,4,3,2,1,0:T(8,128)(2,1)} %param.12) | copy-start | bytes 3145732
  7.8 6.0 %collective-permute-start.1 = (bf16[256,256]{1,0:T(8,128)(2,1)S(1)}, bf16[256,256]{1,0:T(8,128)(2,1)S(1)}, u32[]{:S(2)}, u32[]{:S(2)}) collective-permute-start(bf16[256,256]{1,0:T(8,128)(2,1)S(1)} %pad_maximum_fusion.1), channel_id=1, source_target_pairs={{0,16},{1,9},{2,18},{3,11},{4,20},{5,13},{6,22},{7,15},{8,24},{9,1... | collective-permute-start | bytes 393224 | tf_op jit(solution)/shard_map/ppermute | solution.py:31
  13.8 9.6 %collective-permute-start.2 = (bf16[512,256]{1,0:T(8,128)(2,1)S(1)}, bf16[512,256]{1,0:T(8,128)(2,1)S(1)}, u32[]{:S(2)}, u32[]{:S(2)}) collective-permute-start(bf16[512,256]{1,0:T(8,128)(2,1)S(1)} %pad_maximum_fusion), channel_id=1, source_target_pairs={{0,2},{1,5},{2,0},{3,7},{4,6},{5,1},{6,4},{7,3},{8,10},{9,13},{10,... | collective-permute-start | bytes 786440 | tf_op jit(solution)/shard_map/ppermute | solution.py:31
  16.9 9.1 %copy-start.7 = (s32[16]{0:T(128)S(1)}, s32[16]{0:T(128)}, u32[]{:S(2)}) copy-start(s32[16]{0:T(128)} %constant.60.clone) | copy-start | bytes 196
  16.9 9.1 %copy-start.8 = (s32[16]{0:T(128)S(1)}, s32[16]{0:T(128)}, u32[]{:S(2)}) copy-start(s32[16]{0:T(128)} %constant.61.clone) | copy-start | bytes 196
  23.4 9.7 %collective-permute-start.3 = (bf16[1024,256]{1,0:T(8,128)(2,1)S(1)}, bf16[1024,256]{1,0:T(8,128)(2,1)S(1)}, u32[]{:S(2)}, u32[]{:S(2)}) collective-permute-start(bf16[1024,256]{1,0:T(8,128)(2,1)S(1)} %constant_dynamic-update-slice_fusion.right_ref), channel_id=1, source_target_pairs={{0,4},{1,3},{2,6},{3,1},{4,0},{5,7},{6,2},{7,5},{8,12},{9,11},{10,... | collective-permute-start | bytes 1572872 | tf_op jit(solution)/shard_map/ppermute | solution.py:31
  26.0 0.7 copy-start.6
  33.2 0.8 %copy-start.3 = (bf16[128,256]{1,0:T(8,128)(2,1)S(1)}, bf16[128,256]{1,0:T(8,128)(2,1)}, u32[]{:S(2)}) copy-start(bf16[128,256]{1,0:T(8,128)(2,1)} %own_ref.1) | copy-start | bytes 196612
  33.2 2.1 %copy-start.2 = (bf16[256,256]{1,0:T(8,128)(2,1)S(1)}, bf16[256,256]{1,0:T(8,128)(2,1)}, u32[]{:S(2)}) copy-start(bf16[256,256]{1,0:T(8,128)(2,1)} %weight_ref.1) | copy-start | bytes 393220
  33.6 1.7 %collective-permute-start.4 = (f32[256,256]{1,0:T(8,128)S(1)}, f32[256,256]{1,0:T(8,128)S(1)}, u32[]{:S(2)}, u32[]{:S(2)}) collective-permute-start(f32[256,256]{1,0:T(8,128)S(1)} %shard_map.121.mine_ref), channel_id=1, source_target_pairs={{0,1},{1,0},{2,3},{3,2},{4,5},{5,4},{6,7},{7,6},{8,9},{9,8},{10,11... | collective-permute-start | bytes 786440 | tf_op jit(solution)/shard_map/ppermute | solution.py:35
  34.0 1.3 %collective-permute-start.5 = (bf16[128,256]{1,0:T(8,128)(2,1)S(1)}, bf16[128,256]{1,0:T(8,128)(2,1)S(1)}, u32[]{:S(2)}, u32[]{:S(2)}) collective-permute-start(bf16[128,256]{1,0:T(8,128)(2,1)S(1)} %copy-done.3), channel_id=1, source_target_pairs={{0,1},{1,0},{2,3},{3,2},{4,5},{5,4},{6,7},{7,6},{8,9},{9,8},{10,11... | collective-permute-start | bytes 196616 | tf_op jit(solution)/shard_map/ppermute | solution.py:35
  35.3 0.7 copy-start.4
  36.9 9.6 %collective-permute-start.6 = (bf16[1024,256]{1,0:T(8,128)(2,1)S(1)}, bf16[1024,256]{1,0:T(8,128)(2,1)S(1)}, u32[]{:S(2)}, u32[]{:S(2)}) collective-permute-start(bf16[1024,256]{1,0:T(8,128)(2,1)S(1)} %get-tuple-element.26), channel_id=1, source_target_pairs={{0,4},{1,3},{2,6},{3,1},{4,0},{5,7},{6,2},{7,5},{8,12},{9,11},{10,... | collective-permute-start | bytes 1572872 | tf_op jit(solution)/shard_map/ppermute | solution.py:31
  39.5 7.0 %collective-permute-start.10 = (f32[136,256]{1,0:T(8,128)S(1)}, f32[136,256]{1,0:T(8,128)S(1)}, u32[]{:S(2)}, u32[]{:S(2)}) collective-permute-start(f32[136,256]{1,0:T(8,128)S(1)} %get-tuple-element.27), channel_id=1, source_target_pairs={{0,16},{1,9},{2,18},{3,11},{4,20},{5,13},{6,22},{7,15},{8,24},{9,1... | collective-permute-start | bytes 417800 | tf_op jit(solution)/shard_map/ppermute | solution.py:31
  46.5 5.1 %collective-permute-start.11 = (f32[136,256]{1,0:T(8,128)S(1)}, f32[136,256]{1,0:T(8,128)S(1)}, u32[]{:S(2)}, u32[]{:S(2)}) collective-permute-start(f32[136,256]{1,0:T(8,128)S(1)} %add.69), channel_id=1, source_target_pairs={{0,8},{1,17},{2,10},{3,19},{4,12},{5,21},{6,14},{7,23},{8,0},{9,25... | collective-permute-start | bytes 417800 | tf_op jit(solution)/shard_map/ppermute | solution.py:31
  46.6 13.5 %collective-permute-start.7 = (bf16[512,256]{1,0:T(8,128)(2,1)S(1)}, bf16[512,256]{1,0:T(8,128)(2,1)S(1)}, u32[]{:S(2)}, u32[]{:S(2)}) collective-permute-start(bf16[512,256]{1,0:T(8,128)(2,1)S(1)} %add_convert_fusion), channel_id=1, source_target_pairs={{0,2},{1,5},{2,0},{3,7},{4,6},{5,1},{6,4},{7,3},{8,10},{9,13},{10,... | collective-permute-start | bytes 786440 | tf_op jit(solution)/shard_map/ppermute | solution.py:31
  51.6 5.1 %collective-permute-start.12 = (f32[136,256]{1,0:T(8,128)S(1)}, f32[136,256]{1,0:T(8,128)S(1)}, u32[]{:S(2)}, u32[]{:S(2)}) collective-permute-start(f32[136,256]{1,0:T(8,128)S(1)} %add.70), channel_id=1, source_target_pairs={{0,4},{1,3},{2,6},{3,1},{4,0},{5,7},{6,2},{7,5},{8,12},{9,11},{10,... | collective-permute-start | bytes 417800 | tf_op jit(solution)/shard_map/ppermute | solution.py:31
  56.8 6.3 %collective-permute-start.13 = (f32[136,256]{1,0:T(8,128)S(1)}, f32[136,256]{1,0:T(8,128)S(1)}, u32[]{:S(2)}, u32[]{:S(2)}) collective-permute-start(f32[136,256]{1,0:T(8,128)S(1)} %add.71), channel_id=1, source_target_pairs={{0,2},{1,5},{2,0},{3,7},{4,6},{5,1},{6,4},{7,3},{8,10},{9,13},{10,... | collective-permute-start | bytes 417800 | tf_op jit(solution)/shard_map/ppermute | solution.py:31
  60.1 7.4 %collective-permute-start.8 = (bf16[256,256]{1,0:T(8,128)(2,1)S(1)}, bf16[256,256]{1,0:T(8,128)(2,1)S(1)}, u32[]{:S(2)}, u32[]{:S(2)}) collective-permute-start(bf16[256,256]{1,0:T(8,128)(2,1)S(1)} %add_convert_fusion.1), channel_id=1, source_target_pairs={{0,16},{1,9},{2,18},{3,11},{4,20},{5,13},{6,22},{7,15},{8,24},{9,1... | collective-permute-start | bytes 393224 | tf_op jit(solution)/shard_map/ppermute | solution.py:31
  63.1 4.5 %collective-permute-start.14 = (f32[136,256]{1,0:T(8,128)S(1)}, f32[136,256]{1,0:T(8,128)S(1)}, u32[]{:S(2)}, u32[]{:S(2)}) collective-permute-start(f32[136,256]{1,0:T(8,128)S(1)} %add.72.mine_ref), channel_id=1, source_target_pairs={{0,1},{1,0},{2,3},{3,2},{4,5},{5,4},{6,7},{7,6},{8,9},{9,8},{10,11... | collective-permute-start | bytes 417800 | tf_op jit(solution)/shard_map/ppermute | solution.py:35
  67.5 4.3 %collective-permute-start.9 = (bf16[128,256]{1,0:T(8,128)(2,1)S(1)}, bf16[128,256]{1,0:T(8,128)(2,1)S(1)}, u32[]{:S(2)}, u32[]{:S(2)}) collective-permute-start(bf16[128,256]{1,0:T(8,128)(2,1)S(1)} %add_convert_fusion.3), channel_id=1, source_target_pairs={{0,8},{1,17},{2,10},{3,19},{4,12},{5,21},{6,14},{7,23},{8,0},{9,25... | collective-permute-start | bytes 196616 | tf_op jit(solution)/shard_map/ppermute | solution.py:31

commit v3 on v2

v3 whole, which is shorter than its diff:
```python
from functools import partial

import jax
import jax.numpy as jnp
from jax import lax
from jax.experimental import pallas as pl
from jax.experimental.pallas import tpu as pltpu
from jax.sharding import PartitionSpec as P

BF16 = jnp.bfloat16
F32 = jnp.float32


def dot(left, right, contract=((1,), (0,))):
    return lax.dot_general(left, right, (contract, ((), ())), preferred_element_type=F32)


def axis_order(loop_size):
    bits = [1 << b for b in range(loop_size.bit_length() - 1)]
    low, high = bits[: len(bits) // 2], bits[len(bits) // 2 :]
    return high[::-1] + low


def exchange(value, masks, loop_size, rep_size):
    pairs = []
    for place in range(loop_size):
        for rep in range(rep_size):
            partner = place ^ masks[rep % 2]
            pairs.append((place * rep_size + rep, partner * rep_size + rep))
    return lax.ppermute(value, ("loop", "rep"), pairs)


def swap_rep(value, mask, rep_size):
    return lax.ppermute(value, "rep", [(r, r ^ mask) for r in range(rep_size)])


def partner_masks(order):
    masks = [0]
    for bit in order:
        masks = masks + [m ^ bit for m in masks]
    return masks


def scatter_tiles(word_ref, place_ref, count_ref, masks, tiles_ref, k, out, out_t, first):
    slots, tile = tiles_ref.shape[1], tiles_ref.shape[2]
    panel = out_t.shape[1] // (slots * tile)
    rep = word_ref[0, 1]
    mask = jnp.where(rep == 0, masks[0][k], masks[1][k])
    source = jnp.bitwise_xor(word_ref[0, 0], mask)
    count = count_ref[0, source]
    cols = pl.ds((k - first) * tile, tile)
    for s in range(slots):
        one = tiles_ref[source, s]
        one_t = one.T
        row = jnp.where(s < count, jnp.bitwise_xor(place_ref[source, s], rep), -1)
        for t in range(panel):
            keep = (row == t).astype(BF16)
            rows = pl.ds((s * panel + t) * tile, tile)
            out[rows, cols] = one * keep
            out_t[cols, rows] = one_t * keep


def fold(both):
    half = both.shape[0] // 2
    return both[:half] + both[half:]


def near_kernel(
    word_ref, place_ref, count_ref, tiles_ref, own_ref, come_ref,
    sums_ref, far_ref, near_t_ref, far_t_ref, near_ref, *, masks,
):
    lists = (word_ref, place_ref, count_ref, masks, tiles_ref)
    partners = tiles_ref.shape[0]
    half = partners // 2
    for k in range(half):
        scatter_tiles(*lists, k, near_ref, near_t_ref, 0)
    wide = own_ref.shape[0]
    sums_ref[...] = fold(dot(near_ref[:, :wide], own_ref[...]) + dot(near_ref[:, wide:], come_ref[...]))
    for k in range(half, partners):
        scatter_tiles(*lists, k, far_ref, far_t_ref, half)


def far_kernel(sums_ref, far_ref, own_ref, come_ref, out_ref):
    wide = own_ref.shape[0]
    both = dot(far_ref[:, :wide], own_ref[...]) + dot(far_ref[:, wide:], come_ref[...])
    out_ref[...] = sums_ref[...] + fold(both)


def split(value):
    high = value.astype(BF16)
    return high, (value - high.astype(F32)).astype(BF16)


def exp_less_one(value, grown):
    series = value * (1.0 + value * (1 / 2 + value * (1 / 6 + value * (1 / 24))))
    return jnp.where(value > -0.0625, series, grown - 1.0)


def middle_kernel(
    mine_ref, other_ref, weight_ref, bias_ref, own_ref, pair_ref, far_t_ref,
    message_ref, output_ref, back_ref, grad_ref, sums_ref,
):
    rows = own_ref.shape[0]
    sums_ref[:rows] = mine_ref[:rows] + other_ref[rows:]
    sums_ref[rows:] = mine_ref[rows:] + other_ref[:rows]
    high, low = split(sums_ref[...])
    weight = weight_ref[...]
    preact = dot(high, weight) + dot(low, weight) + bias_ref[...]
    negative = jnp.minimum(preact, 0.0)
    grown = jnp.exp(negative)
    slope = jnp.where(preact > 0, 1.0, grown)
    own = preact[:rows]
    below = exp_less_one(negative[:rows], grown[:rows])
    output_ref[...] = jnp.where(own > 0, own, below).astype(BF16)
    grad_ref[:rows] = (own_ref[...].astype(F32) * slope[:rows]).astype(BF16)
    grad_ref[rows:] = (pair_ref[...].astype(F32) * slope[rows:]).astype(BF16)
    back = dot(grad_ref[...], weight, ((1,), (1,))).astype(BF16)
    back_ref[: 2 * rows] = back
    back_ref[2 * rows :] = back
    wide = message_ref.shape[0]
    message_ref[...] = dot(far_t_ref[wide:], back_ref[...]).astype(BF16)


def message_kernel(near_t_ref, back_ref, message_ref):
    wide = message_ref.shape[0]
    message_ref[...] = dot(near_t_ref[wide:], back_ref[...]).astype(BF16)


def pack_terms(out_ref, weight_term, bias_term):
    share = weight_term.shape[0]
    out_ref[:share] = weight_term.astype(BF16)
    high, low = split(bias_term)
    row = lax.broadcasted_iota(jnp.int32, (16, bias_term.shape[1]), 0)
    low = jnp.where(row == 1, low.astype(F32), 0.0)
    out_ref[share:] = jnp.where(row == 0, high.astype(F32), low).astype(BF16)


def add_packed(mine_ref, other_ref):
    total = mine_ref[...].astype(F32) + other_ref[...].astype(F32)
    share = total.shape[0] - 16
    return total[:share], total[share : share + 1] + total[share + 1 : share + 2]


def repack_kernel(mine_ref, other_ref, out_ref):
    pack_terms(out_ref, *add_packed(mine_ref, other_ref))


def unpack_kernel(mine_ref, other_ref, out_ref):
    weight_term, bias_term = add_packed(mine_ref, other_ref)
    share = weight_term.shape[0]
    out_ref[:share] = weight_term
    out_ref[share:] = jnp.broadcast_to(bias_term, (8, bias_term.shape[1]))


def keep_kernel(word_ref, near_t_ref, far_t_ref, back_ref, grad_ref, sums_ref, near_ref, far_ref, term_ref):
    share = term_ref.shape[0] - 16
    sums = sums_ref[...]
    mine = jnp.where(word_ref[0, 1] == 0, sums[:, :share], sums[:, share:])
    high, low = split(mine)
    grad = grad_ref[...]
    rows = ((0,), (0,))
    own = jnp.sum(grad[: grad.shape[0] // 2].astype(F32), axis=0, keepdims=True)
    pack_terms(term_ref, dot(high, grad, rows) + dot(low, grad, rows), own)
    wide = near_ref.shape[0]
    far_ref[...] = dot(far_t_ref[:wide], back_ref[...])
    near_ref[...] = dot(near_t_ref[:wide], back_ref[...])


def final_kernel(word_ref, mine_ref, other_ref, weight_ref, bias_ref, *, scale):
    share = weight_ref.shape[0] // 2
    mine, other = mine_ref[...] * scale, other_ref[...] * scale
    first = word_ref[0, 1] == 0
    weight_ref[:share] = jnp.where(first, mine[:share], other[:share])
    weight_ref[share:] = jnp.where(first, other[:share], mine[:share])
    bias_ref[...] = mine[share : share + 1] + other[share : share + 1]


def on_chip(kernel, shapes, scratch=(), scalars=0):
    vmem = pl.BlockSpec(memory_space=pltpu.VMEM)
    smem = pl.BlockSpec(memory_space=pltpu.SMEM)

    def call(*operands):
        return pl.pallas_call(
            kernel,
            out_shape=tuple(jax.ShapeDtypeStruct(*shape) for shape in shapes),
            in_specs=[smem] * scalars + [vmem] * (len(operands) - scalars),
            out_specs=(vmem,) * len(shapes),
            scratch_shapes=list(scratch),
            compiler_params=pltpu.CompilerParams(vmem_limit_bytes=40 << 20),
        )(*operands)

    return call


def tile_loop(target, source, partner, tiles, totals, right_of, product_of, place_of):
    slots = tiles.shape[1]

    def one(number, totals):
        k, s = number // slots, number % slots
        product = product_of(tiles[partner[k], s], right_of(k, s))
        product = product * (target[k, s] >= 0).astype(F32)
        start = place_of(k, s)
        earlier = lax.dynamic_slice_in_dim(totals, start, product.shape[0], 0)
        return lax.dynamic_update_slice_in_dim(totals, earlier + product, start, 0)

    return lax.fori_loop(0, target.shape[0] * slots, one, totals)


def slot_targets(tile_place, tile_count, partner, rep, per_side):
    places = tile_place[0, 0][partner]
    target = places // per_side
    target = jnp.bitwise_xor(target // per_side, rep) * per_side + target % per_side
    slots = places.shape[1]
    live = jnp.arange(slots, dtype=jnp.int32)[None, :] < tile_count[0, 0][partner][:, None]
    return jnp.where(live, target, -1), places % per_side


def plus(*parts):
    total = None
    for part, start, size in parts:
        rows = part[start : start + size].astype(F32)
        total = rows if total is None else total + rows
    return total


def after(value, *others):
    return lax.optimization_barrier((value, others))[0]


def dense_body(node_features, weight, bias_vector, tile_values, tile_place, tile_count, cotangent):
    loop_size = lax.axis_size("loop")
    position = lax.axis_index("loop").astype(jnp.int32)
    rep = lax.axis_index("rep").astype(jnp.int32)
    rows_own, width_in = node_features.shape
    width_out = weight.shape[1]
    _, _, partners, slots, tile, _ = tile_values.shape
    share = width_in // 2
    scale_factor = float(rows_own * loop_size * 2) ** (-0.5)
    wide, deep, rows = partners // 2 * tile, slots * 2 * tile, 2 * tile

    def move(value, masks):
        return exchange(value, masks, loop_size, 2)

    far_z, near_z, first, second = (8, 8), (4, 4), (1, 2), (2, 1)
    masks = [
        partner_masks([far_z[core], first[core], second[core], near_z[core]]) for core in range(2)
    ]
    words = jnp.stack([position, rep]).reshape(1, 2)

    own_near = jnp.concatenate([node_features, move(node_features, far_z)], axis=0)
    own_far = move(own_near, near_z)
    own_near = jnp.concatenate([own_near, move(own_near, first)], axis=0)
    come_near = move(own_near, second)
    own_far = jnp.concatenate([own_far, move(own_far, first)], axis=0)
    come_far = move(own_far, second)
    pair_cotangent = swap_rep(cotangent, 1, 2)

    sums, far, near_t, far_t = on_chip(
        partial(near_kernel, masks=masks),
        [((rows, width_in), F32), ((deep, wide), BF16), ((wide, deep), BF16), ((wide, deep), BF16)],
        [pltpu.VMEM((deep, wide), BF16)],
        3,
    )(words, tile_place[0, 0], tile_count[0], tile_values[0, 0], own_near, come_near)
    (sums,) = on_chip(far_kernel, [((rows, width_in), F32)])(sums, far, own_far, come_far)
    far_message, output, back, grad_pre, sums = on_chip(
        middle_kernel,
        [
            ((wide // 2, width_in), BF16),
            ((rows_own, width_out), BF16),
            ((slots * rows, width_in), BF16),
            ((rows, width_out), BF16),
            ((rows, width_in), F32),
        ],
    )(sums, swap_rep(sums, 1, 2), weight, bias_vector.reshape(1, width_out), cotangent, pair_cotangent, far_t)
    (near_message,) = on_chip(message_kernel, [((wide // 2, width_in), BF16)])(near_t, back)
    near_keep, far_keep, term = on_chip(
        keep_kernel,
        [((wide // 2, width_in), F32), ((wide // 2, width_in), F32), ((share + 16, width_out), BF16)],
        (),
        1,
    )(words, near_t, far_t, back, grad_pre, sums)

    far_1 = move(far_message, second)
    near_1 = move(near_message, second)
    (term,) = on_chip(repack_kernel, [(term.shape, BF16)])(term, move(term, (4, 8)))
    half, one = wide // 4, rows_own
    far_message = plus((far_keep, half, half), (far_1, half, half)).astype(BF16)
    far_2 = move(far_message, first)
    near_message = plus((near_keep, half, half), (near_1, half, half)).astype(BF16)
    near_2 = move(near_message, first)
    term = after(term, far_1)
    (term,) = on_chip(unpack_kernel, [((share + 8, width_out), F32)])(term, move(term, (8, 4)))
    z_message = plus((far_keep, 0, half), (far_1, 0, half), (far_2, 0, half)).astype(BF16)
    far_3 = move(z_message, near_z)
    near_parts = (near_keep, near_1, near_2, far_3)
    term = after(term, near_1)
    term = term + move(term, (1, 2))
    last_message = plus(*((part, one, one) for part in near_parts)).astype(BF16)
    last = move(last_message, far_z)
    term = after(term, far_2, near_2)
    term = term + move(term, (2, 1))
    grad_features = plus(*((part, 0, one) for part in near_parts), (last, 0, one)).astype(BF16)

    grad_weight, grad_bias = on_chip(
        partial(final_kernel, scale=scale_factor),
        [((width_in, width_out), F32), ((1, width_out), F32)],
        (),
        1,
    )(words, term, swap_rep(term, 1, 2))
    return (output, grad_features, grad_weight, grad_bias.reshape(width_out))


def general_body(node_features, weight, bias_vector, tile_values, tile_place, tile_count, cotangent):
    loop_size = lax.axis_size("loop")
    rep_size = lax.axis_size("rep")
    position = lax.axis_index("loop").astype(jnp.int32)
    rep = lax.axis_index("rep").astype(jnp.int32)
    rows_own, width_in = node_features.shape
    width_out = weight.shape[1]
    partners, tile = tile_values.shape[2], tile_values.shape[4]
    per_side = rows_own // tile
    panel = rep_size * per_side
    order = axis_order(loop_size)
    half = partners // 2
    share = width_in // rep_size
    scale_factor = float(rows_own * loop_size * rep_size) ** (-0.5)
    tiles = tile_values[0, 0]
    rep_bits = [1 << bit for bit in range(rep_size.bit_length() - 1)]
    partner = jnp.bitwise_xor(position, jnp.array(partner_masks(order), jnp.int32))
    target, source = slot_targets(tile_place, tile_count, partner, rep, per_side)

    def move(value, bit):
        return exchange(value, (bit, bit), loop_size, rep_size)

    gathered = node_features
    for bit in order:
        gathered = jnp.concatenate([gathered, move(gathered, bit)], axis=0)
    cotangent_rows = cotangent
    for bit in rep_bits:
        cotangent_rows = jnp.concatenate(
            [cotangent_rows, swap_rep(cotangent_rows, bit, rep_size)], axis=0
        )
    sums = tile_loop(
        target, source, partner, tiles, jnp.zeros((panel * tile, width_in), F32),
        lambda k, s: lax.dynamic_slice_in_dim(
            gathered, k * rows_own + source[k, s] * tile, tile, 0
        ),
        dot,
        lambda k, s: jnp.maximum(target[k, s], 0) * tile,
    )
    for bit in rep_bits:
        other = swap_rep(sums, bit, rep_size)
        blocks = other.reshape(rep_size, rows_own, width_in)
        blocks = jnp.stack([blocks[t ^ bit] for t in range(rep_size)])
        sums = sums + blocks.reshape(sums.shape)
    high = lax.reduce_precision(sums, 8, 7)
    low = (sums - high).astype(BF16)
    high = high.astype(BF16)
    preact = dot(high, weight) + dot(low, weight) + bias_vector[None, :]
    negative = jnp.minimum(preact, 0.0)
    own = preact[:rows_own]
    output = jnp.where(own > 0, own, jnp.expm1(negative[:rows_own])).astype(BF16)
    slope = jnp.where(preact > 0, 1.0, jnp.exp(negative))
    grad_pre = (cotangent_rows.astype(F32) * slope).astype(BF16)
    back = dot(grad_pre, weight, ((1,), (1,))).astype(BF16)
    start = rep * share
    term = dot(lax.dynamic_slice_in_dim(high, start, share, 1), grad_pre, ((0,), (0,)))
    term = term + dot(lax.dynamic_slice_in_dim(low, start, share, 1), grad_pre, ((0,), (0,)))
    bias_term = jnp.sum(grad_pre[:rows_own].astype(F32), axis=0, keepdims=True)
    term = jnp.concatenate([term, jnp.broadcast_to(bias_term, (8, width_out))], axis=0)
    adjoint = tile_loop(
        target, source, partner, tiles, jnp.zeros((partners * rows_own, width_in), F32),
        lambda k, s: lax.dynamic_slice_in_dim(back, jnp.maximum(target[k, s], 0) * tile, tile, 0),
        lambda left, right: dot(left, right, ((0,), (0,))),
        lambda k, s: k * rows_own + source[k, s] * tile,
    )
    size = half * rows_own
    for bit in order[::-1]:
        term = term + move(term, bit)
        adjoint = adjoint[:size] + move(adjoint[size:].astype(BF16), bit).astype(F32)
        size = size // 2
    shares = term[None] * scale_factor
    for bit in rep_bits:
        shares = jnp.concatenate([shares, swap_rep(shares, bit, rep_size)], axis=0)
    shares = shares[jnp.bitwise_xor(jnp.arange(rep_size, dtype=jnp.int32), rep)]
    grad_weight = shares[:, :share].reshape(width_in, width_out)
    return (output, adjoint.astype(BF16), grad_weight, jnp.sum(shares[:, share], axis=0))


def body(*arrays):
    rows_own, tile_values = arrays[0].shape[0], arrays[3]
    _, _, partners, slots, tile, _ = tile_values.shape
    groups = (lax.axis_size("rep"), partners, slots, rows_own // tile)
    return (dense_body if groups == (2, 16, 2, 1) else general_body)(*arrays)


def solution(mesh):
    return jax.shard_map(
        body,
        mesh=mesh,
        in_specs=(
            P(("loop", "rep"), None),
            P(),
            P(),
            P("loop", "rep", None, None, None, None),
            P("loop", "rep", None, None),
            P("loop", "rep", None),
            P(("loop", "rep"), None),
        ),
        out_specs=(P(("loop", "rep"), None), P(("loop", "rep"), None), P(), P()),
        check_vma=False,
    )
```

time: 72.7 us -> 57.8 us (0.80)
  waiting for transfers between devices: 41.1 us -> 23.3 us
  starting transfers between devices: 21.4 us -> 23.6 us
  Pallas kernels: 4.13 us -> 5.57 us
  other arithmetic: 1.92 us -> 0.95 us
    ppermute x12 -> x16, waiting for transfers between devices: 40 us -> 22.2 us  [exchange(): return lax.ppermute(value, ('loop', 'rep'), pairs)]
    ppermute x12 -> x16, starting transfers between devices: 21.1 us -> 23.3 us  [exchange(): return lax.ppermute(value, ('loop', 'rep'), pairs)]
    unnamed x21 -> x14, local copies, waits for them, and re-layouts: 1.73 us -> 3.22 us
    pallas_call x5 -> x8, Pallas kernels: 4.13 us -> 5.57 us  [call(): pl.pallas_call(kernel, out_shape=tuple((jax.ShapeDtypeStruct(*shape) for...]
    gather x2 -> x0, local copies, waits for them, and re-layouts: 1.22 us -> none  [the longest x1 0.66 us: body(): tile_count[0, 0][partner][:, None]]
    concatenate x3 -> x0, other arithmetic: 0.95 us -> none  [the longest x2 0.87 us: body(): jnp.concatenate([gathered, exchange(gathered, step, orders, loop_size, re...]
  transfers between devices with their start and end apart: 15 -> 19, of which waited for: 11 -> 11; matrix products, arithmetic and copies ran while one was open for 2% -> 3% of each run, Pallas kernels for 4% -> 5%
where the time goes in v3:
time: 57.8 us; the launch traced here: 57.6 us
  starting transfers between devices  23.6 us (41%)
  waiting for transfers between devices  23.3 us (40%)
  Pallas kernels  5.57 us (10%)
  local copies, waits for them, and re-layouts  3.33 us (6%)
  other arithmetic  0.95 us (2%)
  between operations  0.77 us (1%)
    ppermute x16, starting transfers between devices, exchange(): return lax.ppermute(value, ('loop', 'rep'), pairs)  23.3 us
    ppermute x16, waiting for transfers between devices, exchange(): return lax.ppermute(value, ('loop', 'rep'), pairs)  22.2 us
    pallas_call x8, Pallas kernels, call(): pl.pallas_call(kernel, out_shape=tuple((jax.ShapeDtypeStruct(*shape) for...  5.57 us
    unnamed x14, local copies, waits for them, and re-layouts  3.22 us
  transfers between devices with their start and end apart: 19, of which 11 were waited for; matrix products, arithmetic and copies ran while one was open for 3% of the time, Pallas kernels for 5%

profile of v3, /device:TPU:0, one launch (start us, length us, event | category | flops | bytes accessed | tf_op | source)
XLA Modules:
  0.0 57.6 jit_solution(9098670125161465467)
XLA Ops:
  0.6 4.1 %collective-permute-start = (bf16[128,256]{1,0:T(8,128)(2,1)}, bf16[128,256]{1,0:T(8,128)(2,1)S(1)}, u32[]{:S(2)}, u32[]{:S(2)}) collective-permute-start(bf16[128,256]{1,0:T(8,128)(2,1)} %param.7), channel_id=1, source_target_pairs={{0,16},{1,17},{2,18},{3,19},{4,20},{5,21},{6,22},{7,23},{8,24},{9,... | collective-permute-start | bytes 196616 | tf_op jit(solution)/shard_map/ppermute | solution.py:30
  5.6 3.0 %collective-permute-done = bf16[128,256]{1,0:T(8,128)(2,1)S(1)} collective-permute-done((bf16[128,256]{1,0:T(8,128)(2,1)}, bf16[128,256]{1,0:T(8,128)(2,1)S(1)}, u32[]{:S(2)}, u32[]{:S(2)}) %collective-permute-start) | collective-permute-done | bytes 65568 | tf_op jit(solution)/shard_map/ppermute | solution.py:30
  9.4 1.5 %collective-permute-start.1 = (bf16[256,256]{1,0:T(8,128)(2,1)S(1)}, bf16[256,256]{1,0:T(8,128)(2,1)S(1)}, u32[]{:S(2)}, u32[]{:S(2)}) collective-permute-start(bf16[256,256]{1,0:T(8,128)(2,1)S(1)} %get-tuple-element.38), channel_id=1, source_target_pairs={{0,2},{1,5},{2,0},{3,7},{4,6},{5,1},{6,4},{7,3},{8,10},{9,13},{10,... | collective-permute-start | bytes 393224 | tf_op jit(solution)/shard_map/ppermute | solution.py:30
  10.8 2.8 %collective-permute-done.3 = bf16[256,256]{1,0:T(8,128)(2,1)S(1)} collective-permute-done((bf16[256,256]{1,0:T(8,128)(2,1)S(1)}, bf16[256,256]{1,0:T(8,128)(2,1)S(1)}, u32[]{:S(2)}, u32[]{:S(2)}) %collective-permute-start.3) | collective-permute-done | bytes 131104 | tf_op jit(solution)/shard_map/ppermute | solution.py:30
  13.6 1.7 %collective-permute-start.4 = (bf16[256,256]{1,0:T(8,128)(2,1)S(1)}, bf16[256,256]{1,0:T(8,128)(2,1)S(1)}, u32[]{:S(2)}, u32[]{:S(2)}) collective-permute-start(bf16[256,256]{1,0:T(8,128)(2,1)S(1)} %collective-permute-done.3), channel_id=1, source_target_pairs={{0,2},{1,5},{2,0},{3,7},{4,6},{5,1},{6,4},{7,3},{8,10},{9,13},{10,... | collective-permute-start | bytes 393224 | tf_op jit(solution)/shard_map/ppermute | solution.py:30
  15.4 1.6 %collective-permute-start.2 = (bf16[512,256]{1,0:T(8,128)(2,1)S(1)}, bf16[512,256]{1,0:T(8,128)(2,1)S(1)}, u32[]{:S(2)}, u32[]{:S(2)}) collective-permute-start(bf16[512,256]{1,0:T(8,128)(2,1)S(1)} %constant_dynamic-update-slice_fusion.2.own_ref), channel_id=1, source_target_pairs={{0,4},{1,3},{2,6},{3,1},{4,0},{5,7},{6,2},{7,5},{8,12},{9,11},{10,... | collective-permute-start | bytes 786440 | tf_op jit(solution)/shard_map/ppermute | solution.py:30
  17.0 3.1 %collective-permute-done.4 = bf16[256,256]{1,0:T(8,128)(2,1)S(1)} collective-permute-done((bf16[256,256]{1,0:T(8,128)(2,1)S(1)}, bf16[256,256]{1,0:T(8,128)(2,1)S(1)}, u32[]{:S(2)}, u32[]{:S(2)}) %collective-permute-start.4) | collective-permute-done | bytes 131104 | tf_op jit(solution)/shard_map/ppermute | solution.py:30
  20.1 1.8 %collective-permute-start.5 = (bf16[512,256]{1,0:T(8,128)(2,1)S(1)}, bf16[512,256]{1,0:T(8,128)(2,1)S(1)}, u32[]{:S(2)}, u32[]{:S(2)}) collective-permute-start(bf16[512,256]{1,0:T(8,128)(2,1)S(1)} %constant_dynamic-update-slice_fusion.5.own_ref), channel_id=1, source_target_pairs={{0,4},{1,3},{2,6},{3,1},{4,0},{5,7},{6,2},{7,5},{8,12},{9,11},{10,... | collective-permute-start | bytes 786440 | tf_op jit(solution)/shard_map/ppermute | solution.py:30
  23.4 1.5 %shard_map.102 = (f32[256,256]{1,0:T(8,128)S(1)}, bf16[512,1024]{1,0:T(8,128)(2,1)S(1)}, bf16[1024,512]{1,0:T(8,128)(2,1)S(1)}, bf16[1024,512]{1,0:T(8,128)(2,1)S(1)}) custom-call(s32[1,2]{1,0:T(1,128)S(1)} %add_bitcast_fusion.word_ref, s32[16,2]{1,0:T(8,128)S(1)} %copy.11.place_ref, s32[1,16]{1,0:T(1,128)S(1)} %bitcast.11, ...), custom_call_target="tpu_custom_call" | custom-call | tf_op jit(solution)/shard_map/pallas_call | solution.py:183
  24.9 1.6 %collective-permute-done.5.come_ref = bf16[512,256]{1,0:T(8,128)(2,1)S(1)} collective-permute-done((bf16[512,256]{1,0:T(8,128)(2,1)S(1)}, bf16[512,256]{1,0:T(8,128)(2,1)S(1)}, u32[]{:S(2)}, u32[]{:S(2)}) %collective-permute-start.5) | collective-permute-done | bytes 262176 | tf_op jit(solution)/shard_map/ppermute | solution.py:30
  27.6 1.1 %collective-permute-done.7.pair_ref = bf16[128,256]{1,0:T(8,128)(2,1)S(1)} collective-permute-done((bf16[128,256]{1,0:T(8,128)(2,1)S(1)}, bf16[128,256]{1,0:T(8,128)(2,1)S(1)}, u32[]{:S(2)}, u32[]{:S(2)}) %collective-permute-start.7) | collective-permute-done | bytes 65568 | tf_op jit(solution)/shard_map/ppermute | solution.py:34
  30.3 1.7 %collective-permute-start.10 = (bf16[512,256]{1,0:T(8,128)(2,1)S(1)}, bf16[512,256]{1,0:T(8,128)(2,1)S(1)}, u32[]{:S(2)}, u32[]{:S(2)}) collective-permute-start(bf16[512,256]{1,0:T(8,128)(2,1)S(1)} %get-tuple-element.31), channel_id=1, source_target_pairs={{0,4},{1,3},{2,6},{3,1},{4,0},{5,7},{6,2},{7,5},{8,12},{9,11},{10,... | collective-permute-start | bytes 786440 | tf_op jit(solution)/shard_map/ppermute | solution.py:30
  32.0 1.1 %shard_map.105 = (f32[512,256]{1,0:T(8,128)S(1)}, f32[512,256]{1,0:T(8,128)S(1)}, bf16[144,256]{1,0:T(8,128)(2,1)S(1)}) custom-call(s32[1,2]{1,0:T(1,128)S(1)} %add_bitcast_fusion.word_ref, bf16[1024,512]{1,0:T(8,128)(2,1)S(1)} %get-tuple-element.25.near_t_ref, bf16[1024,512]{1,0:T(8,128)(2,1)S(1)} %get-tuple-element.23.far_t_ref, ...), custom_call_target="tpu_custom_call" | custom-call | tf_op jit(solution)/shard_map/pallas_call | solution.py:183
  34.5 3.5 %collective-permute-done.14.other_ref = bf16[144,256]{1,0:T(8,128)(2,1)S(1)} collective-permute-done((bf16[144,256]{1,0:T(8,128)(2,1)S(1)}, bf16[144,256]{1,0:T(8,128)(2,1)S(1)}, u32[]{:S(2)}, u32[]{:S(2)}) %collective-permute-start.14) | collective-permute-done | bytes 73760 | tf_op jit(solution)/shard_map/ppermute | solution.py:30
  38.0 1.7 %collective-permute-start.15 = (bf16[144,256]{1,0:T(8,128)(2,1)S(1)}, bf16[144,256]{1,0:T(8,128)(2,1)S(1)}, u32[]{:S(2)}, u32[]{:S(2)}) collective-permute-start(bf16[144,256]{1,0:T(8,128)(2,1)S(1)} %shard_map.107.mine_ref), channel_id=1, source_target_pairs={{0,16},{1,9},{2,18},{3,11},{4,20},{5,13},{6,22},{7,15},{8,24},{9,1... | collective-permute-start | bytes 221192 | tf_op jit(solution)/shard_map/ppermute | solution.py:30
  39.7 1.5 %collective-permute-start.11 = (bf16[256,256]{1,0:T(8,128)(2,1)S(1)}, bf16[256,256]{1,0:T(8,128)(2,1)S(1)}, u32[]{:S(2)}, u32[]{:S(2)}) collective-permute-start(bf16[256,256]{1,0:T(8,128)(2,1)S(1)} %add_convert_fusion.1), channel_id=1, source_target_pairs={{0,2},{1,5},{2,0},{3,7},{4,6},{5,1},{6,4},{7,3},{8,10},{9,13},{10,... | collective-permute-start | bytes 393224 | tf_op jit(solution)/shard_map/ppermute | solution.py:30
  41.3 1.2 %collective-permute-start.9 = (bf16[256,256]{1,0:T(8,128)(2,1)S(1)}, bf16[256,256]{1,0:T(8,128)(2,1)S(1)}, u32[]{:S(2)}, u32[]{:S(2)}) collective-permute-start(bf16[256,256]{1,0:T(8,128)(2,1)S(1)} %add_convert_fusion.2), channel_id=1, source_target_pairs={{0,2},{1,5},{2,0},{3,7},{4,6},{5,1},{6,4},{7,3},{8,10},{9,13},{10,... | collective-permute-start | bytes 393224 | tf_op jit(solution)/shard_map/ppermute | solution.py:30
  42.5 1.6 %collective-permute-done.15.other_ref = bf16[144,256]{1,0:T(8,128)(2,1)S(1)} collective-permute-done((bf16[144,256]{1,0:T(8,128)(2,1)S(1)}, bf16[144,256]{1,0:T(8,128)(2,1)S(1)}, u32[]{:S(2)}, u32[]{:S(2)}) %collective-permute-start.15) | collective-permute-done | bytes 73760 | tf_op jit(solution)/shard_map/ppermute | solution.py:30
  44.1 1.2 %collective-permute-start.16 = (f32[136,256]{1,0:T(8,128)S(1)}, f32[136,256]{1,0:T(8,128)S(1)}, u32[]{:S(2)}, u32[]{:S(2)}) collective-permute-start(f32[136,256]{1,0:T(8,128)S(1)} %shard_map.108), channel_id=1, source_target_pairs={{0,2},{1,5},{2,0},{3,7},{4,6},{5,1},{6,4},{7,3},{8,10},{9,13},{10,... | collective-permute-start | bytes 417800 | tf_op jit(solution)/shard_map/ppermute | solution.py:30
  45.3 2.0 %collective-permute-start.12 = (bf16[256,256]{1,0:T(8,128)(2,1)S(1)}, bf16[256,256]{1,0:T(8,128)(2,1)S(1)}, u32[]{:S(2)}, u32[]{:S(2)}) collective-permute-start(bf16[256,256]{1,0:T(8,128)(2,1)S(1)} %add_convert_fusion), channel_id=1, source_target_pairs={{0,8},{1,9},{2,10},{3,11},{4,12},{5,13},{6,14},{7,15},{8,0},{9,1},... | collective-permute-start | bytes 393224 | tf_op jit(solution)/shard_map/ppermute | solution.py:30
  47.3 2.3 %collective-permute-done.16 = f32[136,256]{1,0:T(8,128)S(1)} collective-permute-done((f32[136,256]{1,0:T(8,128)S(1)}, f32[136,256]{1,0:T(8,128)S(1)}, u32[]{:S(2)}, u32[]{:S(2)}) %collective-permute-start.16) | collective-permute-done | bytes 139296 | tf_op jit(solution)/shard_map/ppermute | solution.py:30
  50.4 1.5 %collective-permute-start.13 = (bf16[128,256]{1,0:T(8,128)(2,1)S(1)}, bf16[128,256]{1,0:T(8,128)(2,1)S(1)}, u32[]{:S(2)}, u32[]{:S(2)}) collective-permute-start(bf16[128,256]{1,0:T(8,128)(2,1)S(1)} %add_convert_fusion.4), channel_id=1, source_target_pairs={{0,16},{1,17},{2,18},{3,19},{4,20},{5,21},{6,22},{7,23},{8,24},{9,... | collective-permute-start | bytes 196616 | tf_op jit(solution)/shard_map/ppermute | solution.py:30
  51.9 2.8 %collective-permute-done.17 = f32[136,256]{1,0:T(8,128)S(1)} collective-permute-done((f32[136,256]{1,0:T(8,128)S(1)}, f32[136,256]{1,0:T(8,128)S(1)}, u32[]{:S(2)}, u32[]{:S(2)}) %collective-permute-start.17) | collective-permute-done | bytes 139296 | tf_op jit(solution)/shard_map/ppermute | solution.py:30
  56.3 1.3 %shard_map.109 = (f32[256,256]{1,0:T(8,128)}, f32[1,256]{1,0:T(1,128)}) custom-call(s32[1,2]{1,0:T(1,128)S(1)} %add_bitcast_fusion.word_ref, f32[136,256]{1,0:T(8,128)S(1)} %add.51.mine_ref, f32[136,256]{1,0:T(8,128)S(1)} %collective-permute-done.18.other_ref), custom_call_target="tpu_custom_call" | custom-call | tf_op jit(solution)/shard_map/pallas_call | solution.py:183
  (48 shorter events, 9.7 us)
Async XLA Ops:
  0.6 22.1 %copy-start = (bf16[1,1,16,2,128,128]{5,4,3,2,1,0:T(8,128)(2,1)S(1)}, bf16[1,1,16,2,128,128]{5,4,3,2,1,0:T(8,128)(2,1)}, u32[]{:S(2)}) copy-start(bf16[1,1,16,2,128,128]{5,4,3,2,1,0:T(8,128)(2,1)} %param.10) | copy-start | bytes 3145732
  0.6 8.0 %collective-permute-start = (bf16[128,256]{1,0:T(8,128)(2,1)}, bf16[128,256]{1,0:T(8,128)(2,1)S(1)}, u32[]{:S(2)}, u32[]{:S(2)}) collective-permute-start(bf16[128,256]{1,0:T(8,128)(2,1)} %param.7), channel_id=1, source_target_pairs={{0,16},{1,17},{2,18},{3,19},{4,20},{5,21},{6,22},{7,23},{8,24},{9,... | collective-permute-start | bytes 196616 | tf_op jit(solution)/shard_map/ppermute | solution.py:30
  8.6 5.0 %collective-permute-start.3 = (bf16[256,256]{1,0:T(8,128)(2,1)S(1)}, bf16[256,256]{1,0:T(8,128)(2,1)S(1)}, u32[]{:S(2)}, u32[]{:S(2)}) collective-permute-start(bf16[256,256]{1,0:T(8,128)(2,1)S(1)} %get-tuple-element.38), channel_id=1, source_target_pairs={{0,8},{1,9},{2,10},{3,11},{4,12},{5,13},{6,14},{7,15},{8,0},{9,1},... | collective-permute-start | bytes 393224 | tf_op jit(solution)/shard_map/ppermute | solution.py:30
  9.4 6.0 %collective-permute-start.1 = (bf16[256,256]{1,0:T(8,128)(2,1)S(1)}, bf16[256,256]{1,0:T(8,128)(2,1)S(1)}, u32[]{:S(2)}, u32[]{:S(2)}) collective-permute-start(bf16[256,256]{1,0:T(8,128)(2,1)S(1)} %get-tuple-element.38), channel_id=1, source_target_pairs={{0,2},{1,5},{2,0},{3,7},{4,6},{5,1},{6,4},{7,3},{8,10},{9,13},{10,... | collective-permute-start | bytes 393224 | tf_op jit(solution)/shard_map/ppermute | solution.py:30
  13.6 6.4 %collective-permute-start.4 = (bf16[256,256]{1,0:T(8,128)(2,1)S(1)}, bf16[256,256]{1,0:T(8,128)(2,1)S(1)}, u32[]{:S(2)}, u32[]{:S(2)}) collective-permute-start(bf16[256,256]{1,0:T(8,128)(2,1)S(1)} %collective-permute-done.3), channel_id=1, source_target_pairs={{0,2},{1,5},{2,0},{3,7},{4,6},{5,1},{6,4},{7,3},{8,10},{9,13},{10,... | collective-permute-start | bytes 393224 | tf_op jit(solution)/shard_map/ppermute | solution.py:30
  15.4 7.4 %collective-permute-start.2 = (bf16[512,256]{1,0:T(8,128)(2,1)S(1)}, bf16[512,256]{1,0:T(8,128)(2,1)S(1)}, u32[]{:S(2)}, u32[]{:S(2)}) collective-permute-start(bf16[512,256]{1,0:T(8,128)(2,1)S(1)} %constant_dynamic-update-slice_fusion.2.own_ref), channel_id=1, source_target_pairs={{0,4},{1,3},{2,6},{3,1},{4,0},{5,7},{6,2},{7,5},{8,12},{9,11},{10,... | collective-permute-start | bytes 786440 | tf_op jit(solution)/shard_map/ppermute | solution.py:30
  20.1 6.4 %collective-permute-start.5 = (bf16[512,256]{1,0:T(8,128)(2,1)S(1)}, bf16[512,256]{1,0:T(8,128)(2,1)S(1)}, u32[]{:S(2)}, u32[]{:S(2)}) collective-permute-start(bf16[512,256]{1,0:T(8,128)(2,1)S(1)} %constant_dynamic-update-slice_fusion.5.own_ref), channel_id=1, source_target_pairs={{0,4},{1,3},{2,6},{3,1},{4,0},{5,7},{6,2},{7,5},{8,12},{9,11},{10,... | collective-permute-start | bytes 786440 | tf_op jit(solution)/shard_map/ppermute | solution.py:30
  21.9 0.7 %copy-start.5 = (s32[1,1,16,2]{2,3,1,0:T(2,128)S(1)}, s32[1,1,16,2]{2,3,1,0:T(2,128)}, u32[]{:S(2)}) copy-start(s32[1,1,16,2]{2,3,1,0:T(2,128)} %param.11) | copy-start | bytes 388
  26.5 0.8 %copy-start.2 = (bf16[128,256]{1,0:T(8,128)(2,1)S(1)}, bf16[128,256]{1,0:T(8,128)(2,1)}, u32[]{:S(2)}) copy-start(bf16[128,256]{1,0:T(8,128)(2,1)} %own_ref.1) | copy-start | bytes 196612
  26.5 2.1 %copy-start.1 = (bf16[256,256]{1,0:T(8,128)(2,1)S(1)}, bf16[256,256]{1,0:T(8,128)(2,1)}, u32[]{:S(2)}) copy-start(bf16[256,256]{1,0:T(8,128)(2,1)} %weight_ref.1) | copy-start | bytes 393220
  27.0 1.7 %collective-permute-start.6 = (f32[256,256]{1,0:T(8,128)S(1)}, f32[256,256]{1,0:T(8,128)S(1)}, u32[]{:S(2)}, u32[]{:S(2)}) collective-permute-start(f32[256,256]{1,0:T(8,128)S(1)} %shard_map.103.mine_ref), channel_id=1, source_target_pairs={{0,1},{1,0},{2,3},{3,2},{4,5},{5,4},{6,7},{7,6},{8,9},{9,8},{10,11... | collective-permute-start | bytes 786440 | tf_op jit(solution)/shard_map/ppermute | solution.py:34
  27.4 1.3 %collective-permute-start.7 = (bf16[128,256]{1,0:T(8,128)(2,1)S(1)}, bf16[128,256]{1,0:T(8,128)(2,1)S(1)}, u32[]{:S(2)}, u32[]{:S(2)}) collective-permute-start(bf16[128,256]{1,0:T(8,128)(2,1)S(1)} %copy-done.2), channel_id=1, source_target_pairs={{0,1},{1,0},{2,3},{3,2},{4,5},{5,4},{6,7},{7,6},{8,9},{9,8},{10,11... | collective-permute-start | bytes 196616 | tf_op jit(solution)/shard_map/ppermute | solution.py:34
  28.7 0.7 %copy-start.3 = (f32[256]{0:T(256)S(1)}, f32[256]{0:T(256)}, u32[]{:S(2)}) copy-start(f32[256]{0:T(256)} %param.9) | copy-start | bytes 3076
  30.3 7.7 %collective-permute-start.10 = (bf16[512,256]{1,0:T(8,128)(2,1)S(1)}, bf16[512,256]{1,0:T(8,128)(2,1)S(1)}, u32[]{:S(2)}, u32[]{:S(2)}) collective-permute-start(bf16[512,256]{1,0:T(8,128)(2,1)S(1)} %get-tuple-element.31), channel_id=1, source_target_pairs={{0,4},{1,3},{2,6},{3,1},{4,0},{5,7},{6,2},{7,5},{8,12},{9,11},{10,... | collective-permute-start | bytes 786440 | tf_op jit(solution)/shard_map/ppermute | solution.py:30
  33.1 4.8 %collective-permute-start.14 = (bf16[144,256]{1,0:T(8,128)(2,1)S(1)}, bf16[144,256]{1,0:T(8,128)(2,1)S(1)}, u32[]{:S(2)}, u32[]{:S(2)}) collective-permute-start(bf16[144,256]{1,0:T(8,128)(2,1)S(1)} %get-tuple-element.32.mine_ref), channel_id=1, source_target_pairs={{0,8},{1,17},{2,10},{3,19},{4,12},{5,21},{6,14},{7,23},{8,0},{9,25... | collective-permute-start | bytes 221192 | tf_op jit(solution)/shard_map/ppermute | solution.py:30
  33.9 7.3 %collective-permute-start.8 = (bf16[512,256]{1,0:T(8,128)(2,1)S(1)}, bf16[512,256]{1,0:T(8,128)(2,1)S(1)}, u32[]{:S(2)}, u32[]{:S(2)}) collective-permute-start(bf16[512,256]{1,0:T(8,128)(2,1)S(1)} %shard_map.106), channel_id=1, source_target_pairs={{0,4},{1,3},{2,6},{3,1},{4,0},{5,7},{6,2},{7,5},{8,12},{9,11},{10,... | collective-permute-start | bytes 786440 | tf_op jit(solution)/shard_map/ppermute | solution.py:30
  38.0 6.1 %collective-permute-start.15 = (bf16[144,256]{1,0:T(8,128)(2,1)S(1)}, bf16[144,256]{1,0:T(8,128)(2,1)S(1)}, u32[]{:S(2)}, u32[]{:S(2)}) collective-permute-start(bf16[144,256]{1,0:T(8,128)(2,1)S(1)} %shard_map.107.mine_ref), channel_id=1, source_target_pairs={{0,16},{1,9},{2,18},{3,11},{4,20},{5,13},{6,22},{7,15},{8,24},{9,1... | collective-permute-start | bytes 221192 | tf_op jit(solution)/shard_map/ppermute | solution.py:30
  39.7 5.6 %collective-permute-start.11 = (bf16[256,256]{1,0:T(8,128)(2,1)S(1)}, bf16[256,256]{1,0:T(8,128)(2,1)S(1)}, u32[]{:S(2)}, u32[]{:S(2)}) collective-permute-start(bf16[256,256]{1,0:T(8,128)(2,1)S(1)} %add_convert_fusion.1), channel_id=1, source_target_pairs={{0,2},{1,5},{2,0},{3,7},{4,6},{5,1},{6,4},{7,3},{8,10},{9,13},{10,... | collective-permute-start | bytes 393224 | tf_op jit(solution)/shard_map/ppermute | solution.py:30
  41.3 8.3 %collective-permute-start.9 = (bf16[256,256]{1,0:T(8,128)(2,1)S(1)}, bf16[256,256]{1,0:T(8,128)(2,1)S(1)}, u32[]{:S(2)}, u32[]{:S(2)}) collective-permute-start(bf16[256,256]{1,0:T(8,128)(2,1)S(1)} %add_convert_fusion.2), channel_id=1, source_target_pairs={{0,2},{1,5},{2,0},{3,7},{4,6},{5,1},{6,4},{7,3},{8,10},{9,13},{10,... | collective-permute-start | bytes 393224 | tf_op jit(solution)/shard_map/ppermute | solution.py:30
  44.1 5.5 %collective-permute-start.16 = (f32[136,256]{1,0:T(8,128)S(1)}, f32[136,256]{1,0:T(8,128)S(1)}, u32[]{:S(2)}, u32[]{:S(2)}) collective-permute-start(f32[136,256]{1,0:T(8,128)S(1)} %shard_map.108), channel_id=1, source_target_pairs={{0,2},{1,5},{2,0},{3,7},{4,6},{5,1},{6,4},{7,3},{8,10},{9,13},{10,... | collective-permute-start | bytes 417800 | tf_op jit(solution)/shard_map/ppermute | solution.py:30
  45.3 5.0 %collective-permute-start.12 = (bf16[256,256]{1,0:T(8,128)(2,1)S(1)}, bf16[256,256]{1,0:T(8,128)(2,1)S(1)}, u32[]{:S(2)}, u32[]{:S(2)}) collective-permute-start(bf16[256,256]{1,0:T(8,128)(2,1)S(1)} %add_convert_fusion), channel_id=1, source_target_pairs={{0,8},{1,9},{2,10},{3,11},{4,12},{5,13},{6,14},{7,15},{8,0},{9,1},... | collective-permute-start | bytes 393224 | tf_op jit(solution)/shard_map/ppermute | solution.py:30
  49.6 5.1 %collective-permute-start.17 = (f32[136,256]{1,0:T(8,128)S(1)}, f32[136,256]{1,0:T(8,128)S(1)}, u32[]{:S(2)}, u32[]{:S(2)}) collective-permute-start(f32[136,256]{1,0:T(8,128)S(1)} %add.50), channel_id=1, source_target_pairs={{0,4},{1,3},{2,6},{3,1},{4,0},{5,7},{6,2},{7,5},{8,12},{9,11},{10,... | collective-permute-start | bytes 417800 | tf_op jit(solution)/shard_map/ppermute | solution.py:30
  50.4 5.2 %collective-permute-start.13 = (bf16[128,256]{1,0:T(8,128)(2,1)S(1)}, bf16[128,256]{1,0:T(8,128)(2,1)S(1)}, u32[]{:S(2)}, u32[]{:S(2)}) collective-permute-start(bf16[128,256]{1,0:T(8,128)(2,1)S(1)} %add_convert_fusion.4), channel_id=1, source_target_pairs={{0,16},{1,17},{2,18},{3,19},{4,20},{5,21},{6,22},{7,23},{8,24},{9,... | collective-permute-start | bytes 196616 | tf_op jit(solution)/shard_map/ppermute | solution.py:30
  54.7 1.6 %collective-permute-start.18 = (f32[136,256]{1,0:T(8,128)S(1)}, f32[136,256]{1,0:T(8,128)S(1)}, u32[]{:S(2)}, u32[]{:S(2)}) collective-permute-start(f32[136,256]{1,0:T(8,128)S(1)} %add.51.mine_ref), channel_id=1, source_target_pairs={{0,1},{1,0},{2,3},{3,2},{4,5},{5,4},{6,7},{7,6},{8,9},{9,8},{10,11... | collective-permute-start | bytes 417800 | tf_op jit(solution)/shard_map/ppermute | solution.py:34
  (1 other events, 0.7 us)

commit v4 on v3

--- a/solution.py
+++ b/solution.py
@@ -41,12 +41,12 @@
     return masks
 
 
-def scatter_tiles(word_ref, place_ref, count_ref, masks, tiles_ref, k, out, out_t, first):
+def scatter_tiles(position_ref, rep_ref, place_ref, count_ref, masks, tiles_ref, k, out, out_t, first):
     slots, tile = tiles_ref.shape[1], tiles_ref.shape[2]
     panel = out_t.shape[1] // (slots * tile)
-    rep = word_ref[0, 1]
+    rep = rep_ref[0, 0]
     mask = jnp.where(rep == 0, masks[0][k], masks[1][k])
-    source = jnp.bitwise_xor(word_ref[0, 0], mask)
+    source = jnp.bitwise_xor(position_ref[0, 0], mask)
     count = count_ref[0, source]
     cols = pl.ds((k - first) * tile, tile)
     for s in range(slots):
@@ -66,10 +66,11 @@
 
 
 def near_kernel(
-    word_ref, place_ref, count_ref, tiles_ref, own_ref, come_ref,
-    sums_ref, far_ref, near_t_ref, far_t_ref, near_ref, *, masks,
+    position_ref, rep_ref, place_ref, count_ref, tiles_ref, own_ref, come_ref,
+    cotangent_ref, pair_ref, weight_ref, bias_ref,
+    sums_ref, far_ref, near_t_ref, far_t_ref, panel_ref, weight_out_ref, bias_out_ref, near_ref, *, masks,
 ):
-    lists = (word_ref, place_ref, count_ref, masks, tiles_ref)
+    lists = (position_ref, rep_ref, place_ref, count_ref, masks, tiles_ref)
     partners = tiles_ref.shape[0]
     half = partners // 2
     for k in range(half):
@@ -78,6 +79,11 @@
     sums_ref[...] = fold(dot(near_ref[:, :wide], own_ref[...]) + dot(near_ref[:, wide:], come_ref[...]))
     for k in range(half, partners):
         scatter_tiles(*lists, k, far_ref, far_t_ref, half)
+    rows = cotangent_ref.shape[0]
+    panel_ref[:rows] = cotangent_ref[...]
+    panel_ref[rows:] = pair_ref[...]
+    weight_out_ref[...] = weight_ref[...]
+    bias_out_ref[...] = bias_ref[...]
 
 
 def far_kernel(sums_ref, far_ref, own_ref, come_ref, out_ref):
@@ -97,10 +103,10 @@
 
 
 def middle_kernel(
-    mine_ref, other_ref, weight_ref, bias_ref, own_ref, pair_ref, far_t_ref,
+    mine_ref, other_ref, weight_ref, bias_ref, panel_ref, far_t_ref,
     message_ref, output_ref, back_ref, grad_ref, sums_ref,
 ):
-    rows = own_ref.shape[0]
+    rows = output_ref.shape[0]
     sums_ref[:rows] = mine_ref[:rows] + other_ref[rows:]
     sums_ref[rows:] = mine_ref[rows:] + other_ref[:rows]
     high, low = split(sums_ref[...])
@@ -112,8 +118,7 @@
     own = preact[:rows]
     below = exp_less_one(negative[:rows], grown[:rows])
     output_ref[...] = jnp.where(own > 0, own, below).astype(BF16)
-    grad_ref[:rows] = (own_ref[...].astype(F32) * slope[:rows]).astype(BF16)
-    grad_ref[rows:] = (pair_ref[...].astype(F32) * slope[rows:]).astype(BF16)
+    grad_ref[...] = (panel_ref[...].astype(F32) * slope).astype(BF16)
     back = dot(grad_ref[...], weight, ((1,), (1,))).astype(BF16)
     back_ref[: 2 * rows] = back
     back_ref[2 * rows :] = back
@@ -152,10 +157,10 @@
     out_ref[share:] = jnp.broadcast_to(bias_term, (8, bias_term.shape[1]))
 
 
-def keep_kernel(word_ref, near_t_ref, far_t_ref, back_ref, grad_ref, sums_ref, near_ref, far_ref, term_ref):
+def keep_kernel(rep_ref, near_t_ref, far_t_ref, back_ref, grad_ref, sums_ref, near_ref, far_ref, term_ref):
     share = term_ref.shape[0] - 16
     sums = sums_ref[...]
-    mine = jnp.where(word_ref[0, 1] == 0, sums[:, :share], sums[:, share:])
+    mine = jnp.where(rep_ref[0, 0] == 0, sums[:, :share], sums[:, share:])
     high, low = split(mine)
     grad = grad_ref[...]
     rows = ((0,), (0,))
@@ -166,10 +171,10 @@
     near_ref[...] = dot(near_t_ref[:wide], back_ref[...])
 
 
-def final_kernel(word_ref, mine_ref, other_ref, weight_ref, bias_ref, *, scale):
+def final_kernel(rep_ref, mine_ref, other_ref, weight_ref, bias_ref, *, scale):
     share = weight_ref.shape[0] // 2
     mine, other = mine_ref[...] * scale, other_ref[...] * scale
-    first = word_ref[0, 1] == 0
+    first = rep_ref[0, 0] == 0
     weight_ref[:share] = jnp.where(first, mine[:share], other[:share])
     weight_ref[share:] = jnp.where(first, other[:share], mine[:share])
     bias_ref[...] = mine[share : share + 1] + other[share : share + 1]
@@ -241,26 +246,36 @@
     def move(value, masks):
         return exchange(value, masks, loop_size, 2)
 
-    far_z, near_z, first, second = (8, 8), (4, 4), (1, 2), (2, 1)
-    masks = [
-        partner_masks([far_z[core], first[core], second[core], near_z[core]]) for core in range(2)
-    ]
-    words = jnp.stack([position, rep]).reshape(1, 2)
-
-    own_near = jnp.concatenate([node_features, move(node_features, far_z)], axis=0)
-    own_far = move(own_near, near_z)
+    first, second = (1, 2), (2, 1)
+    masks = [partner_masks([4, first[core], second[core], 8]) for core in range(2)]
+    position, rep = position.reshape(1, 1), rep.reshape(1, 1)
+
+    own_near = jnp.concatenate([node_features, move(node_features, (4, 4))], axis=0)
+    own_far = [move(node_features, (z, z)) for z in (8, 12)]
+    own_far = jnp.concatenate(own_far, axis=0)
     own_near = jnp.concatenate([own_near, move(own_near, first)], axis=0)
     come_near = move(own_near, second)
     own_far = jnp.concatenate([own_far, move(own_far, first)], axis=0)
     come_far = move(own_far, second)
     pair_cotangent = swap_rep(cotangent, 1, 2)
 
-    sums, far, near_t, far_t = on_chip(
+    sums, far, near_t, far_t, panel, weight, bias = on_chip(
         partial(near_kernel, masks=masks),
-        [((rows, width_in), F32), ((deep, wide), BF16), ((wide, deep), BF16), ((wide, deep), BF16)],
+        [
+            ((rows, width_in), F32),
+            ((deep, wide), BF16),
+            ((wide, deep), BF16),
+            ((wide, deep), BF16),
+            ((rows, width_out), BF16),
+            ((width_in, width_out), BF16),
+            ((1, width_out), F32),
+        ],
         [pltpu.VMEM((deep, wide), BF16)],
-        3,
-    )(words, tile_place[0, 0], tile_count[0], tile_values[0, 0], own_near, come_near)
+        4,
+    )(
+        position, rep, tile_place[0, 0], tile_count[0], tile_values[0, 0], own_near, come_near,
+        cotangent, pair_cotangent, weight, bias_vector.reshape(1, width_out),
+    )
     (sums,) = on_chip(far_kernel, [((rows, width_in), F32)])(sums, far, own_far, come_far)
     far_message, output, back, grad_pre, sums = on_chip(
         middle_kernel,
@@ -271,42 +286,41 @@
             ((rows, width_out), BF16),
             ((rows, width_in), F32),
         ],
-    )(sums, swap_rep(sums, 1, 2), weight, bias_vector.reshape(1, width_out), cotangent, pair_cotangent, far_t)
+    )(sums, swap_rep(sums, 1, 2), weight, bias, panel, far_t)
     (near_message,) = on_chip(message_kernel, [((wide // 2, width_in), BF16)])(near_t, back)
     near_keep, far_keep, term = on_chip(
         keep_kernel,
         [((wide // 2, width_in), F32), ((wide // 2, width_in), F32), ((share + 16, width_out), BF16)],
         (),
         1,
-    )(words, near_t, far_t, back, grad_pre, sums)
+    )(rep, near_t, far_t, back, grad_pre, sums)
 
     far_1 = move(far_message, second)
     near_1 = move(near_message, second)
+    half, one = wide // 4, rows_own
     (term,) = on_chip(repack_kernel, [(term.shape, BF16)])(term, move(term, (4, 8)))
-    half, one = wide // 4, rows_own
-    far_message = plus((far_keep, half, half), (far_1, half, half)).astype(BF16)
-    far_2 = move(far_message, first)
-    near_message = plus((near_keep, half, half), (near_1, half, half)).astype(BF16)
-    near_2 = move(near_message, first)
+    far_2 = move(plus((far_keep, half, half), (far_1, half, half)).astype(BF16), first)
+    near_2 = move(plus((near_keep, half, half), (near_1, half, half)).astype(BF16), first)
     term = after(term, far_1)
-    (term,) = on_chip(unpack_kernel, [((share + 8, width_out), F32)])(term, move(term, (8, 4)))
-    z_message = plus((far_keep, 0, half), (far_1, 0, half), (far_2, 0, half)).astype(BF16)
-    far_3 = move(z_message, near_z)
-    near_parts = (near_keep, near_1, near_2, far_3)
+    (term,) = on_chip(repack_kernel, [(term.shape, BF16)])(term, move(term, (8, 4)))
+    far_parts = (far_keep, far_1, far_2)
+    near_parts = (near_keep, near_1, near_2)
+    from_8 = move(plus(*((part, 0, one) for part in far_parts)).astype(BF16), (8, 8))
+    from_12 = move(plus(*((part, one, one) for part in far_parts)).astype(BF16), (12, 12))
+    from_4 = move(plus(*((part, one, one) for part in near_parts)).astype(BF16), (4, 4))
     term = after(term, near_1)
-    term = term + move(term, (1, 2))
-    last_message = plus(*((part, one, one) for part in near_parts)).astype(BF16)
-    last = move(last_message, far_z)
+    (term,) = on_chip(repack_kernel, [(term.shape, BF16)])(term, move(term, (1, 2)))
     term = after(term, far_2, near_2)
-    term = term + move(term, (2, 1))
-    grad_features = plus(*((part, 0, one) for part in near_parts), (last, 0, one)).astype(BF16)
+    (term,) = on_chip(unpack_kernel, [((share + 8, width_out), F32)])(term, move(term, (2, 1)))
+    near_parts = near_parts + (from_8, from_12, from_4)
+    grad_features = plus(*((part, 0, one) for part in near_parts)).astype(BF16)
 
     grad_weight, grad_bias = on_chip(
         partial(final_kernel, scale=scale_factor),
         [((width_in, width_out), F32), ((1, width_out), F32)],
         (),
         1,
-    )(words, term, swap_rep(term, 1, 2))
+    )(rep, term, swap_rep(term, 1, 2))
     return (output, grad_features, grad_weight, grad_bias.reshape(width_out))
 
 

time: 57.8 us -> 52.5 us (0.908)
  waiting for transfers between devices: 23.3 us -> 18.9 us
  starting transfers between devices: 23.6 us -> 24.8 us
  Pallas kernels: 5.57 us -> 4.56 us
  local copies, waits for them, and re-layouts: 3.33 us -> 2.4 us
    ppermute x16 -> x18, waiting for transfers between devices: 22.2 us -> 16.9 us  [exchange(): return lax.ppermute(value, ('loop', 'rep'), pairs)]
    ppermute x16 -> x18, starting transfers between devices: 23.3 us -> 24.6 us  [exchange(): return lax.ppermute(value, ('loop', 'rep'), pairs)]
    pallas_call x8 -> x10, Pallas kernels: 5.57 us -> 4.56 us  [call(): pl.pallas_call(kernel, out_shape=tuple((jax.ShapeDtypeStruct(*shape) for...]
    unnamed x14 -> x18, local copies, waits for them, and re-layouts: 3.22 us -> 2.29 us
    ppermute x3, waiting for transfers between devices: 1.12 us -> 2.01 us  [swap_rep(): return lax.ppermute(value, 'rep', [(r, r ^ mask) for r in range(rep_size)])]
  transfers between devices with their start and end apart: 19 -> 21, of which waited for: 11 -> 10; matrix products, arithmetic and copies ran while one was open for 3% -> 4% of each run, Pallas kernels for 5% -> 5%
where the time goes in v4:
time: 52.5 us; the launch traced here: 52.3 us
  starting transfers between devices  24.8 us (47%)
  waiting for transfers between devices  18.9 us (36%)
  Pallas kernels  4.56 us (9%)
  local copies, waits for them, and re-layouts  2.4 us (5%)
  other arithmetic  0.84 us (2%)
  between operations  0.84 us (2%)
    ppermute x18, starting transfers between devices, exchange(): return lax.ppermute(value, ('loop', 'rep'), pairs)  24.6 us
    ppermute x18, waiting for transfers between devices, exchange(): return lax.ppermute(value, ('loop', 'rep'), pairs)  16.9 us
    pallas_call x10, Pallas kernels, call(): pl.pallas_call(kernel, out_shape=tuple((jax.ShapeDtypeStruct(*shape) for...  4.56 us
    unnamed x18, local copies, waits for them, and re-layouts  2.29 us
    ppermute x3, waiting for transfers between devices, swap_rep(): return lax.ppermute(value, 'rep', [(r, r ^ mask) for r in range(rep_size)])  2.01 us
  transfers between devices with their start and end apart: 21, of which 10 were waited for; matrix products, arithmetic and copies ran while one was open for 4% of the time, Pallas kernels for 5%

profile of v4, /device:TPU:0, one launch (start us, length us, event | category | flops | bytes accessed | tf_op | source)
XLA Modules:
  0.0 52.3 jit_solution(4732028279991803937)
XLA Ops:
  0.7 3.1 %collective-permute-start = (bf16[128,256]{1,0:T(8,128)(2,1)}, bf16[128,256]{1,0:T(8,128)(2,1)S(1)}, u32[]{:S(2)}, u32[]{:S(2)}) collective-permute-start(bf16[128,256]{1,0:T(8,128)(2,1)} %param.7), channel_id=1, source_target_pairs={{0,8},{1,9},{2,10},{3,11},{4,12},{5,13},{6,14},{7,15},{8,0},{9,1},... | collective-permute-start | bytes 196616 | tf_op jit(solution)/shard_map/ppermute | solution.py:30
  3.7 2.6 %collective-permute-start.4 = (bf16[128,256]{1,0:T(8,128)(2,1)}, bf16[128,256]{1,0:T(8,128)(2,1)S(1)}, u32[]{:S(2)}, u32[]{:S(2)}) collective-permute-start(bf16[128,256]{1,0:T(8,128)(2,1)} %param.7), channel_id=1, source_target_pairs={{0,16},{1,17},{2,18},{3,19},{4,20},{5,21},{6,22},{7,23},{8,24},{9,... | collective-permute-start | bytes 196616 | tf_op jit(solution)/shard_map/ppermute | solution.py:30
  6.3 0.9 %constant_dynamic-update-slice_fusion.2 = bf16[512,256]{1,0:T(8,128)(2,1)S(1)} fusion(bf16[128,256]{1,0:T(8,128)(2,1)} %param.7), kind=kLoop, calls=%fused_computation.10 | loop fusion | bytes 131072
  7.3 1.7 %collective-permute-start.1 = (bf16[256,256]{1,0:T(8,128)(2,1)S(1)}, bf16[256,256]{1,0:T(8,128)(2,1)S(1)}, u32[]{:S(2)}, u32[]{:S(2)}) collective-permute-start(bf16[256,256]{1,0:T(8,128)(2,1)S(1)} %pad_maximum_fusion), channel_id=1, source_target_pairs={{0,2},{1,5},{2,0},{3,7},{4,6},{5,1},{6,4},{7,3},{8,10},{9,13},{10,... | collective-permute-start | bytes 393224 | tf_op jit(solution)/shard_map/ppermute | solution.py:30
  9.0 2.2 %collective-permute-done.4 = bf16[128,256]{1,0:T(8,128)(2,1)S(1)} collective-permute-done((bf16[128,256]{1,0:T(8,128)(2,1)}, bf16[128,256]{1,0:T(8,128)(2,1)S(1)}, u32[]{:S(2)}, u32[]{:S(2)}) %collective-permute-start.4) | collective-permute-done | bytes 65568 | tf_op jit(solution)/shard_map/ppermute | solution.py:30
  11.2 1.4 %collective-permute-done.5 = bf16[128,256]{1,0:T(8,128)(2,1)S(1)} collective-permute-done((bf16[128,256]{1,0:T(8,128)(2,1)}, bf16[128,256]{1,0:T(8,128)(2,1)S(1)}, u32[]{:S(2)}, u32[]{:S(2)}) %collective-permute-start.5) | collective-permute-done | bytes 65568 | tf_op jit(solution)/shard_map/ppermute | solution.py:30
  12.6 1.6 %collective-permute-start.6 = (bf16[256,256]{1,0:T(8,128)(2,1)S(1)}, bf16[256,256]{1,0:T(8,128)(2,1)S(1)}, u32[]{:S(2)}, u32[]{:S(2)}) collective-permute-start(bf16[256,256]{1,0:T(8,128)(2,1)S(1)} %pad_maximum_fusion.1), channel_id=1, source_target_pairs={{0,2},{1,5},{2,0},{3,7},{4,6},{5,1},{6,4},{7,3},{8,10},{9,13},{10,... | collective-permute-start | bytes 393224 | tf_op jit(solution)/shard_map/ppermute | solution.py:30
  14.3 1.6 %collective-permute-start.2 = (bf16[512,256]{1,0:T(8,128)(2,1)S(1)}, bf16[512,256]{1,0:T(8,128)(2,1)S(1)}, u32[]{:S(2)}, u32[]{:S(2)}) collective-permute-start(bf16[512,256]{1,0:T(8,128)(2,1)S(1)} %constant_dynamic-update-slice_fusion.own_ref), channel_id=1, source_target_pairs={{0,4},{1,3},{2,6},{3,1},{4,0},{5,7},{6,2},{7,5},{8,12},{9,11},{10,... | collective-permute-start | bytes 786440 | tf_op jit(solution)/shard_map/ppermute | solution.py:30
  15.9 3.3 %collective-permute-done.6 = bf16[256,256]{1,0:T(8,128)(2,1)S(1)} collective-permute-done((bf16[256,256]{1,0:T(8,128)(2,1)S(1)}, bf16[256,256]{1,0:T(8,128)(2,1)S(1)}, u32[]{:S(2)}, u32[]{:S(2)}) %collective-permute-start.6) | collective-permute-done | bytes 131104 | tf_op jit(solution)/shard_map/ppermute | solution.py:30
  19.1 1.2 %collective-permute-start.7 = (bf16[512,256]{1,0:T(8,128)(2,1)S(1)}, bf16[512,256]{1,0:T(8,128)(2,1)S(1)}, u32[]{:S(2)}, u32[]{:S(2)}) collective-permute-start(bf16[512,256]{1,0:T(8,128)(2,1)S(1)} %constant_dynamic-update-slice_fusion.3.own_ref), channel_id=1, source_target_pairs={{0,4},{1,3},{2,6},{3,1},{4,0},{5,7},{6,2},{7,5},{8,12},{9,11},{10,... | collective-permute-start | bytes 786440 | tf_op jit(solution)/shard_map/ppermute | solution.py:30
  22.3 1.5 %shard_map.102 = (f32[256,256]{1,0:T(8,128)S(1)}, bf16[512,1024]{1,0:T(8,128)(2,1)S(1)}, bf16[1024,512]{1,0:T(8,128)(2,1)S(1)}, bf16[1024,512]{1,0:T(8,128)(2,1)...) custom-call(s32[1,1]{1,0:T(1,128)} %bitcast.position_ref, ...), custom_call_target="tpu_custom_call" | custom-call | tf_op jit(solution)/shard_map/pallas_call | solution.py:188
  23.8 1.7 %collective-permute-done.7.come_ref = bf16[512,256]{1,0:T(8,128)(2,1)S(1)} collective-permute-done((bf16[512,256]{1,0:T(8,128)(2,1)S(1)}, bf16[512,256]{1,0:T(8,128)(2,1)S(1)}, u32[]{:S(2)}, u32[]{:S(2)}) %collective-permute-start.7) | collective-permute-done | bytes 262176 | tf_op jit(solution)/shard_map/ppermute | solution.py:30
  26.1 1.5 %collective-permute-done.8.other_ref = f32[256,256]{1,0:T(8,128)S(1)} collective-permute-done((f32[256,256]{1,0:T(8,128)S(1)}, f32[256,256]{1,0:T(8,128)S(1)}, u32[]{:S(2)}, u32[]{:S(2)}) %collective-permute-start.8) | collective-permute-done | bytes 262176 | tf_op jit(solution)/shard_map/ppermute | solution.py:34
  27.6 0.9 %shard_map.104 = (bf16[512,256]{1,0:T(8,128)(2,1)S(1)}, bf16[128,256]{1,0:T(8,128)(2,1)}, bf16[512,256]{1,0:T(8,128)(2,1)S(1)}, bf16[256,256]{1,0:T(8,128)(2,1)S(1)}, f32[256,256]{1,0:T(8,128)S(1)}) custom-call(f32[256,256]{1,0:T(8,128)S(1)} %shard_map.103.mine_ref, f32[256,256]{1,0:T(8,128)S(1)} %collective-permute-done.8.other_ref, ...), custom_call_target="tpu_custom_call" | custom-call | tf_op jit(solution)/shard_map/pallas_call | solution.py:188
  28.6 1.1 %collective-permute-start.11 = (bf16[512,256]{1,0:T(8,128)(2,1)S(1)}, bf16[512,256]{1,0:T(8,128)(2,1)S(1)}, u32[]{:S(2)}, u32[]{:S(2)}) collective-permute-start(bf16[512,256]{1,0:T(8,128)(2,1)S(1)} %get-tuple-element.37), channel_id=1, source_target_pairs={{0,4},{1,3},{2,6},{3,1},{4,0},{5,7},{6,2},{7,5},{8,12},{9,11},{10,... | collective-permute-start | bytes 786440 | tf_op jit(solution)/shard_map/ppermute | solution.py:30
  31.6 3.9 %collective-permute-done.16.other_ref = bf16[144,256]{1,0:T(8,128)(2,1)S(1)} collective-permute-done((bf16[144,256]{1,0:T(8,128)(2,1)S(1)}, bf16[144,256]{1,0:T(8,128)(2,1)S(1)}, u32[]{:S(2)}, u32[]{:S(2)}) %collective-permute-start.16) | collective-permute-done | bytes 73760 | tf_op jit(solution)/shard_map/ppermute | solution.py:30
  35.5 1.2 %collective-permute-start.17 = (bf16[144,256]{1,0:T(8,128)(2,1)S(1)}, bf16[144,256]{1,0:T(8,128)(2,1)S(1)}, u32[]{:S(2)}, u32[]{:S(2)}) collective-permute-start(bf16[144,256]{1,0:T(8,128)(2,1)S(1)} %shard_map.107.mine_ref), channel_id=1, source_target_pairs={{0,16},{1,9},{2,18},{3,11},{4,20},{5,13},{6,22},{7,15},{8,24},{9,1... | collective-permute-start | bytes 221192 | tf_op jit(solution)/shard_map/ppermute | solution.py:30
  36.7 1.6 %collective-permute-start.12 = (bf16[256,256]{1,0:T(8,128)(2,1)S(1)}, bf16[256,256]{1,0:T(8,128)(2,1)S(1)}, u32[]{:S(2)}, u32[]{:S(2)}) collective-permute-start(bf16[256,256]{1,0:T(8,128)(2,1)S(1)} %add_convert_fusion), channel_id=1, source_target_pairs={{0,2},{1,5},{2,0},{3,7},{4,6},{5,1},{6,4},{7,3},{8,10},{9,13},{10,... | collective-permute-start | bytes 393224 | tf_op jit(solution)/shard_map/ppermute | solution.py:30
  38.3 1.8 %collective-permute-start.10 = (bf16[256,256]{1,0:T(8,128)(2,1)S(1)}, bf16[256,256]{1,0:T(8,128)(2,1)S(1)}, u32[]{:S(2)}, u32[]{:S(2)}) collective-permute-start(bf16[256,256]{1,0:T(8,128)(2,1)S(1)} %add_convert_fusion.1), channel_id=1, source_target_pairs={{0,2},{1,5},{2,0},{3,7},{4,6},{5,1},{6,4},{7,3},{8,10},{9,13},{10,... | collective-permute-start | bytes 393224 | tf_op jit(solution)/shard_map/ppermute | solution.py:30
  41.0 1.4 %collective-permute-start.18 = (bf16[144,256]{1,0:T(8,128)(2,1)S(1)}, bf16[144,256]{1,0:T(8,128)(2,1)S(1)}, u32[]{:S(2)}, u32[]{:S(2)}) collective-permute-start(bf16[144,256]{1,0:T(8,128)(2,1)S(1)} %shard_map.108.mine_ref), channel_id=1, source_target_pairs={{0,2},{1,5},{2,0},{3,7},{4,6},{5,1},{6,4},{7,3},{8,10},{9,13},{10,... | collective-permute-start | bytes 221192 | tf_op jit(solution)/shard_map/ppermute | solution.py:30
  42.5 1.3 %collective-permute-start.13 = (bf16[128,256]{1,0:T(8,128)(2,1)S(1)}, bf16[128,256]{1,0:T(8,128)(2,1)S(1)}, u32[]{:S(2)}, u32[]{:S(2)}) collective-permute-start(bf16[128,256]{1,0:T(8,128)(2,1)S(1)} %get-tuple-element.44), channel_id=1, source_target_pairs={{0,16},{1,17},{2,18},{3,19},{4,20},{5,21},{6,22},{7,23},{8,24},{9,... | collective-permute-start | bytes 196616 | tf_op jit(solution)/shard_map/ppermute | solution.py:30
  43.7 1.8 %collective-permute-start.14 = (bf16[128,256]{1,0:T(8,128)(2,1)S(1)}, bf16[128,256]{1,0:T(8,128)(2,1)S(1)}, u32[]{:S(2)}, u32[]{:S(2)}) collective-permute-start(bf16[128,256]{1,0:T(8,128)(2,1)S(1)} %get-tuple-element.45), channel_id=1, source_target_pairs={{0,24},{1,25},{2,26},{3,27},{4,28},{5,29},{6,30},{7,31},{8,16},{9,... | collective-permute-start | bytes 196616 | tf_op jit(solution)/shard_map/ppermute | solution.py:30
  45.6 0.9 %collective-permute-start.19 = (bf16[144,256]{1,0:T(8,128)(2,1)S(1)}, bf16[144,256]{1,0:T(8,128)(2,1)S(1)}, u32[]{:S(2)}, u32[]{:S(2)}) collective-permute-start(bf16[144,256]{1,0:T(8,128)(2,1)S(1)} %shard_map.109.mine_ref), channel_id=1, source_target_pairs={{0,4},{1,3},{2,6},{3,1},{4,0},{5,7},{6,2},{7,5},{8,12},{9,11},{10,... | collective-permute-start | bytes 221192 | tf_op jit(solution)/shard_map/ppermute | solution.py:30
  47.2 2.7 %collective-permute-done.19.other_ref = bf16[144,256]{1,0:T(8,128)(2,1)S(1)} collective-permute-done((bf16[144,256]{1,0:T(8,128)(2,1)S(1)}, bf16[144,256]{1,0:T(8,128)(2,1)S(1)}, u32[]{:S(2)}, u32[]{:S(2)}) %collective-permute-start.19) | collective-permute-done | bytes 73760 | tf_op jit(solution)/shard_map/ppermute | solution.py:30
  (56 shorter events, 8.4 us)
Async XLA Ops:
  0.6 6.6 %copy-start.5 = (bf16[128,256]{1,0:T(8,128)(2,1)S(1)}, bf16[128,256]{1,0:T(8,128)(2,1)}, u32[]{:S(2)}) copy-start(bf16[128,256]{1,0:T(8,128)(2,1)} %param.7) | copy-start | bytes 196612
  0.6 21.0 %copy-start = (bf16[1,1,16,2,128,128]{5,4,3,2,1,0:T(8,128)(2,1)S(1)}, bf16[1,1,16,2,128,128]{5,4,3,2,1,0:T(8,128)(2,1)}, u32[]{:S(2)}) copy-start(bf16[1,1,16,2,128,128]{5,4,3,2,1,0:T(8,128)(2,1)} %param.10) | copy-start | bytes 3145732
  0.7 6.6 %collective-permute-start = (bf16[128,256]{1,0:T(8,128)(2,1)}, bf16[128,256]{1,0:T(8,128)(2,1)S(1)}, u32[]{:S(2)}, u32[]{:S(2)}) collective-permute-start(bf16[128,256]{1,0:T(8,128)(2,1)} %param.7), channel_id=1, source_target_pairs={{0,8},{1,9},{2,10},{3,11},{4,12},{5,13},{6,14},{7,15},{8,0},{9,1},... | collective-permute-start | bytes 196616 | tf_op jit(solution)/shard_map/ppermute | solution.py:30
  3.7 7.5 %collective-permute-start.4 = (bf16[128,256]{1,0:T(8,128)(2,1)}, bf16[128,256]{1,0:T(8,128)(2,1)S(1)}, u32[]{:S(2)}, u32[]{:S(2)}) collective-permute-start(bf16[128,256]{1,0:T(8,128)(2,1)} %param.7), channel_id=1, source_target_pairs={{0,16},{1,17},{2,18},{3,19},{4,20},{5,21},{6,22},{7,23},{8,24},{9,... | collective-permute-start | bytes 196616 | tf_op jit(solution)/shard_map/ppermute | solution.py:30
  6.3 6.3 %collective-permute-start.5 = (bf16[128,256]{1,0:T(8,128)(2,1)}, bf16[128,256]{1,0:T(8,128)(2,1)S(1)}, u32[]{:S(2)}, u32[]{:S(2)}) collective-permute-start(bf16[128,256]{1,0:T(8,128)(2,1)} %param.7), channel_id=1, source_target_pairs={{0,24},{1,25},{2,26},{3,27},{4,28},{5,29},{6,30},{7,31},{8,16},{9,... | collective-permute-start | bytes 196616 | tf_op jit(solution)/shard_map/ppermute | solution.py:30
  7.3 7.0 %collective-permute-start.1 = (bf16[256,256]{1,0:T(8,128)(2,1)S(1)}, bf16[256,256]{1,0:T(8,128)(2,1)S(1)}, u32[]{:S(2)}, u32[]{:S(2)}) collective-permute-start(bf16[256,256]{1,0:T(8,128)(2,1)S(1)} %pad_maximum_fusion), channel_id=1, source_target_pairs={{0,2},{1,5},{2,0},{3,7},{4,6},{5,1},{6,4},{7,3},{8,10},{9,13},{10,... | collective-permute-start | bytes 393224 | tf_op jit(solution)/shard_map/ppermute | solution.py:30
  12.6 6.5 %collective-permute-start.6 = (bf16[256,256]{1,0:T(8,128)(2,1)S(1)}, bf16[256,256]{1,0:T(8,128)(2,1)S(1)}, u32[]{:S(2)}, u32[]{:S(2)}) collective-permute-start(bf16[256,256]{1,0:T(8,128)(2,1)S(1)} %pad_maximum_fusion.1), channel_id=1, source_target_pairs={{0,2},{1,5},{2,0},{3,7},{4,6},{5,1},{6,4},{7,3},{8,10},{9,13},{10,... | collective-permute-start | bytes 393224 | tf_op jit(solution)/shard_map/ppermute | solution.py:30
  14.3 7.4 %copy-start.1 = (bf16[256,256]{1,0:T(8,128)(2,1)S(1)}, bf16[256,256]{1,0:T(8,128)(2,1)}, u32[]{:S(2)}) copy-start(bf16[256,256]{1,0:T(8,128)(2,1)} %weight_ref.1) | copy-start | bytes 393220
  14.3 7.3 %collective-permute-start.2 = (bf16[512,256]{1,0:T(8,128)(2,1)S(1)}, bf16[512,256]{1,0:T(8,128)(2,1)S(1)}, u32[]{:S(2)}, u32[]{:S(2)}) collective-permute-start(bf16[512,256]{1,0:T(8,128)(2,1)S(1)} %constant_dynamic-update-slice_fusion.own_ref), channel_id=1, source_target_pairs={{0,4},{1,3},{2,6},{3,1},{4,0},{5,7},{6,2},{7,5},{8,12},{9,11},{10,... | collective-permute-start | bytes 786440 | tf_op jit(solution)/shard_map/ppermute | solution.py:30
  19.1 6.4 %collective-permute-start.7 = (bf16[512,256]{1,0:T(8,128)(2,1)S(1)}, bf16[512,256]{1,0:T(8,128)(2,1)S(1)}, u32[]{:S(2)}, u32[]{:S(2)}) collective-permute-start(bf16[512,256]{1,0:T(8,128)(2,1)S(1)} %constant_dynamic-update-slice_fusion.3.own_ref), channel_id=1, source_target_pairs={{0,4},{1,3},{2,6},{3,1},{4,0},{5,7},{6,2},{7,5},{8,12},{9,11},{10,... | collective-permute-start | bytes 786440 | tf_op jit(solution)/shard_map/ppermute | solution.py:30
  20.4 1.3 %collective-permute-start.3 = (bf16[128,256]{1,0:T(8,128)(2,1)S(1)}, bf16[128,256]{1,0:T(8,128)(2,1)S(1)}, u32[]{:S(2)}, u32[]{:S(2)}) collective-permute-start(bf16[128,256]{1,0:T(8,128)(2,1)S(1)} %copy-done.2), channel_id=1, source_target_pairs={{0,1},{1,0},{2,3},{3,2},{4,5},{5,4},{6,7},{7,6},{8,9},{9,8},{10,11... | collective-permute-start | bytes 196616 | tf_op jit(solution)/shard_map/ppermute | solution.py:34
  26.0 1.6 %collective-permute-start.8 = (f32[256,256]{1,0:T(8,128)S(1)}, f32[256,256]{1,0:T(8,128)S(1)}, u32[]{:S(2)}, u32[]{:S(2)}) collective-permute-start(f32[256,256]{1,0:T(8,128)S(1)} %shard_map.103.mine_ref), channel_id=1, source_target_pairs={{0,1},{1,0},{2,3},{3,2},{4,5},{5,4},{6,7},{7,6},{8,9},{9,8},{10,11... | collective-permute-start | bytes 786440 | tf_op jit(solution)/shard_map/ppermute | solution.py:34
  28.6 6.9 %collective-permute-start.11 = (bf16[512,256]{1,0:T(8,128)(2,1)S(1)}, bf16[512,256]{1,0:T(8,128)(2,1)S(1)}, u32[]{:S(2)}, u32[]{:S(2)}) collective-permute-start(bf16[512,256]{1,0:T(8,128)(2,1)S(1)} %get-tuple-element.37), channel_id=1, source_target_pairs={{0,4},{1,3},{2,6},{3,1},{4,0},{5,7},{6,2},{7,5},{8,12},{9,11},{10,... | collective-permute-start | bytes 786440 | tf_op jit(solution)/shard_map/ppermute | solution.py:30
  30.2 5.2 %collective-permute-start.16 = (bf16[144,256]{1,0:T(8,128)(2,1)S(1)}, bf16[144,256]{1,0:T(8,128)(2,1)S(1)}, u32[]{:S(2)}, u32[]{:S(2)}) collective-permute-start(bf16[144,256]{1,0:T(8,128)(2,1)S(1)} %get-tuple-element.38.mine_ref), channel_id=1, source_target_pairs={{0,8},{1,17},{2,10},{3,19},{4,12},{5,21},{6,14},{7,23},{8,0},{9,25... | collective-permute-start | bytes 221192 | tf_op jit(solution)/shard_map/ppermute | solution.py:30
  30.9 7.4 %collective-permute-start.9 = (bf16[512,256]{1,0:T(8,128)(2,1)S(1)}, bf16[512,256]{1,0:T(8,128)(2,1)S(1)}, u32[]{:S(2)}, u32[]{:S(2)}) collective-permute-start(bf16[512,256]{1,0:T(8,128)(2,1)S(1)} %shard_map.106), channel_id=1, source_target_pairs={{0,4},{1,3},{2,6},{3,1},{4,0},{5,7},{6,2},{7,5},{8,12},{9,11},{10,... | collective-permute-start | bytes 786440 | tf_op jit(solution)/shard_map/ppermute | solution.py:30
  35.5 5.4 %collective-permute-start.17 = (bf16[144,256]{1,0:T(8,128)(2,1)S(1)}, bf16[144,256]{1,0:T(8,128)(2,1)S(1)}, u32[]{:S(2)}, u32[]{:S(2)}) collective-permute-start(bf16[144,256]{1,0:T(8,128)(2,1)S(1)} %shard_map.107.mine_ref), channel_id=1, source_target_pairs={{0,16},{1,9},{2,18},{3,11},{4,20},{5,13},{6,22},{7,15},{8,24},{9,1... | collective-permute-start | bytes 221192 | tf_op jit(solution)/shard_map/ppermute | solution.py:30
  36.7 5.7 %collective-permute-start.12 = (bf16[256,256]{1,0:T(8,128)(2,1)S(1)}, bf16[256,256]{1,0:T(8,128)(2,1)S(1)}, u32[]{:S(2)}, u32[]{:S(2)}) collective-permute-start(bf16[256,256]{1,0:T(8,128)(2,1)S(1)} %add_convert_fusion), channel_id=1, source_target_pairs={{0,2},{1,5},{2,0},{3,7},{4,6},{5,1},{6,4},{7,3},{8,10},{9,13},{10,... | collective-permute-start | bytes 393224 | tf_op jit(solution)/shard_map/ppermute | solution.py:30
  38.3 7.2 %collective-permute-start.10 = (bf16[256,256]{1,0:T(8,128)(2,1)S(1)}, bf16[256,256]{1,0:T(8,128)(2,1)S(1)}, u32[]{:S(2)}, u32[]{:S(2)}) collective-permute-start(bf16[256,256]{1,0:T(8,128)(2,1)S(1)} %add_convert_fusion.1), channel_id=1, source_target_pairs={{0,2},{1,5},{2,0},{3,7},{4,6},{5,1},{6,4},{7,3},{8,10},{9,13},{10,... | collective-permute-start | bytes 393224 | tf_op jit(solution)/shard_map/ppermute | solution.py:30
  41.0 4.5 %collective-permute-start.18 = (bf16[144,256]{1,0:T(8,128)(2,1)S(1)}, bf16[144,256]{1,0:T(8,128)(2,1)S(1)}, u32[]{:S(2)}, u32[]{:S(2)}) collective-permute-start(bf16[144,256]{1,0:T(8,128)(2,1)S(1)} %shard_map.108.mine_ref), channel_id=1, source_target_pairs={{0,2},{1,5},{2,0},{3,7},{4,6},{5,1},{6,4},{7,3},{8,10},{9,13},{10,... | collective-permute-start | bytes 221192 | tf_op jit(solution)/shard_map/ppermute | solution.py:30
  42.5 7.6 %collective-permute-start.13 = (bf16[128,256]{1,0:T(8,128)(2,1)S(1)}, bf16[128,256]{1,0:T(8,128)(2,1)S(1)}, u32[]{:S(2)}, u32[]{:S(2)}) collective-permute-start(bf16[128,256]{1,0:T(8,128)(2,1)S(1)} %get-tuple-element.44), channel_id=1, source_target_pairs={{0,16},{1,17},{2,18},{3,19},{4,20},{5,21},{6,22},{7,23},{8,24},{9,... | collective-permute-start | bytes 196616 | tf_op jit(solution)/shard_map/ppermute | solution.py:30
  43.7 6.4 %collective-permute-start.14 = (bf16[128,256]{1,0:T(8,128)(2,1)S(1)}, bf16[128,256]{1,0:T(8,128)(2,1)S(1)}, u32[]{:S(2)}, u32[]{:S(2)}) collective-permute-start(bf16[128,256]{1,0:T(8,128)(2,1)S(1)} %get-tuple-element.45), channel_id=1, source_target_pairs={{0,24},{1,25},{2,26},{3,27},{4,28},{5,29},{6,30},{7,31},{8,16},{9,... | collective-permute-start | bytes 196616 | tf_op jit(solution)/shard_map/ppermute | solution.py:30
  45.6 4.4 %collective-permute-start.19 = (bf16[144,256]{1,0:T(8,128)(2,1)S(1)}, bf16[144,256]{1,0:T(8,128)(2,1)S(1)}, u32[]{:S(2)}, u32[]{:S(2)}) collective-permute-start(bf16[144,256]{1,0:T(8,128)(2,1)S(1)} %shard_map.109.mine_ref), channel_id=1, source_target_pairs={{0,4},{1,3},{2,6},{3,1},{4,0},{5,7},{6,2},{7,5},{8,12},{9,11},{10,... | collective-permute-start | bytes 221192 | tf_op jit(solution)/shard_map/ppermute | solution.py:30
  46.5 4.3 %collective-permute-start.15 = (bf16[128,256]{1,0:T(8,128)(2,1)S(1)}, bf16[128,256]{1,0:T(8,128)(2,1)S(1)}, u32[]{:S(2)}, u32[]{:S(2)}) collective-permute-start(bf16[128,256]{1,0:T(8,128)(2,1)S(1)} %add_convert_fusion.3), channel_id=1, source_target_pairs={{0,8},{1,9},{2,10},{3,11},{4,12},{5,13},{6,14},{7,15},{8,0},{9,1},... | collective-permute-start | bytes 196616 | tf_op jit(solution)/shard_map/ppermute | solution.py:30
  50.0 1.5 %collective-permute-start.20 = (f32[136,256]{1,0:T(8,128)S(1)}, f32[136,256]{1,0:T(8,128)S(1)}, u32[]{:S(2)}, u32[]{:S(2)}) collective-permute-start(f32[136,256]{1,0:T(8,128)S(1)} %shard_map.110.mine_ref), channel_id=1, source_target_pairs={{0,1},{1,0},{2,3},{3,2},{4,5},{5,4},{6,7},{7,6},{8,9},{9,8},{10,11... | collective-permute-start | bytes 417800 | tf_op jit(solution)/shard_map/ppermute | solution.py:34
  (4 other events, 8.1 us)

commit v5 on v4

--- a/solution.py
+++ b/solution.py
@@ -66,7 +66,7 @@
 
 
 def near_kernel(
-    position_ref, rep_ref, place_ref, count_ref, tiles_ref, own_ref, come_ref,
+    position_ref, rep_ref, place_ref, count_ref, tiles_ref, own_ref, come_ref, far_own_ref,
     cotangent_ref, pair_ref, weight_ref, bias_ref,
     sums_ref, far_ref, near_t_ref, far_t_ref, panel_ref, weight_out_ref, bias_out_ref, near_ref, *, masks,
 ):
@@ -75,10 +75,11 @@
     half = partners // 2
     for k in range(half):
         scatter_tiles(*lists, k, near_ref, near_t_ref, 0)
-    wide = own_ref.shape[0]
-    sums_ref[...] = fold(dot(near_ref[:, :wide], own_ref[...]) + dot(near_ref[:, wide:], come_ref[...]))
     for k in range(half, partners):
         scatter_tiles(*lists, k, far_ref, far_t_ref, half)
+    wide = own_ref.shape[0]
+    both = dot(near_ref[:, :wide], own_ref[...]) + dot(near_ref[:, wide:], come_ref[...])
+    sums_ref[...] = fold(both + dot(far_ref[:, :wide], far_own_ref[...]))
     rows = cotangent_ref.shape[0]
     panel_ref[:rows] = cotangent_ref[...]
     panel_ref[rows:] = pair_ref[...]
@@ -86,10 +87,9 @@
     bias_out_ref[...] = bias_ref[...]
 
 
-def far_kernel(sums_ref, far_ref, own_ref, come_ref, out_ref):
-    wide = own_ref.shape[0]
-    both = dot(far_ref[:, :wide], own_ref[...]) + dot(far_ref[:, wide:], come_ref[...])
-    out_ref[...] = sums_ref[...] + fold(both)
+def far_kernel(sums_ref, far_ref, come_ref, out_ref):
+    wide = come_ref.shape[0]
+    out_ref[...] = sums_ref[...] + fold(dot(far_ref[:, wide:], come_ref[...]))
 
 
 def split(value):
@@ -251,9 +251,10 @@
     position, rep = position.reshape(1, 1), rep.reshape(1, 1)
 
     own_near = jnp.concatenate([node_features, move(node_features, (4, 4))], axis=0)
-    own_far = [move(node_features, (z, z)) for z in (8, 12)]
+    own_far = [after(move(node_features, (z, z)), own_near) for z in (8, 12)]
     own_far = jnp.concatenate(own_far, axis=0)
-    own_near = jnp.concatenate([own_near, move(own_near, first)], axis=0)
+    come = after(move(own_near, first), own_far)
+    own_near = jnp.concatenate([own_near, come], axis=0)
     come_near = move(own_near, second)
     own_far = jnp.concatenate([own_far, move(own_far, first)], axis=0)
     come_far = move(own_far, second)
@@ -273,10 +274,10 @@
         [pltpu.VMEM((deep, wide), BF16)],
         4,
     )(
-        position, rep, tile_place[0, 0], tile_count[0], tile_values[0, 0], own_near, come_near,
+        position, rep, tile_place[0, 0], tile_count[0], tile_values[0, 0], own_near, come_near, own_far,
         cotangent, pair_cotangent, weight, bias_vector.reshape(1, width_out),
     )
-    (sums,) = on_chip(far_kernel, [((rows, width_in), F32)])(sums, far, own_far, come_far)
+    (sums,) = on_chip(far_kernel, [((rows, width_in), F32)])(sums, far, come_far)
     far_message, output, back, grad_pre, sums = on_chip(
         middle_kernel,
         [

time: 52.5 us -> 52.3 us (level)
    unnamed x18 -> x15, local copies, waits for them, and re-layouts: 2.29 us -> 2.29 us
where the time goes in v5:
time: 52.3 us; the launch traced here: 52.1 us
  starting transfers between devices  24.8 us (47%)
  waiting for transfers between devices  18.8 us (36%)
  Pallas kernels  4.51 us (9%)
  local copies, waits for them, and re-layouts  2.4 us (5%)
  other arithmetic  0.82 us (2%)
  between operations  0.81 us (2%)
    ppermute x18, starting transfers between devices, exchange(): return lax.ppermute(value, ('loop', 'rep'), pairs)  24.6 us
    ppermute x18, waiting for transfers between devices, exchange(): return lax.ppermute(value, ('loop', 'rep'), pairs)  16.7 us
    pallas_call x10, Pallas kernels, call(): pl.pallas_call(kernel, out_shape=tuple((jax.ShapeDtypeStruct(*shape) for...  4.51 us
    unnamed x15, local copies, waits for them, and re-layouts  2.29 us
    ppermute x3, waiting for transfers between devices, swap_rep(): return lax.ppermute(value, 'rep', [(r, r ^ mask) for r in range(rep_size)])  2.01 us
  transfers between devices with their start and end apart: 21, of which 10 were waited for; matrix products, arithmetic and copies ran while one was open for 4% of the time, Pallas kernels for 5%

profile of v5, /device:TPU:0, one launch (start us, length us, event | category | flops | bytes accessed | tf_op | source)
XLA Modules:
  0.0 52.1 jit_solution(17932871754824219177)
XLA Ops:
  0.6 3.1 %collective-permute-start = (bf16[128,256]{1,0:T(8,128)(2,1)}, bf16[128,256]{1,0:T(8,128)(2,1)S(1)}, u32[]{:S(2)}, u32[]{:S(2)}) collective-permute-start(bf16[128,256]{1,0:T(8,128)(2,1)} %param.7), channel_id=1, source_target_pairs={{0,8},{1,9},{2,10},{3,11},{4,12},{5,13},{6,14},{7,15},{8,0},{9,1},... | collective-permute-start | bytes 196616 | tf_op jit(solution)/shard_map/ppermute | solution.py:30
  3.7 2.6 %collective-permute-start.2 = (bf16[128,256]{1,0:T(8,128)(2,1)}, bf16[128,256]{1,0:T(8,128)(2,1)S(1)}, u32[]{:S(2)}, u32[]{:S(2)}) collective-permute-start(bf16[128,256]{1,0:T(8,128)(2,1)} %param.7), channel_id=1, source_target_pairs={{0,16},{1,17},{2,18},{3,19},{4,20},{5,21},{6,22},{7,23},{8,24},{9,... | collective-permute-start | bytes 196616 | tf_op jit(solution)/shard_map/ppermute | solution.py:30
  6.3 0.9 %constant_dynamic-update-slice_fusion.1 = (bf16[256,256]{1,0:T(8,128)(2,1)S(1)}, bf16[512,256]{1,0:T(8,128)(2,1)S(1)}) fusion(bf16[128,256]{1,0:T(8,128)(2,1)} %param.7), kind=kLoop, calls=%fused_computation.7 | loop fusion | bytes 196608
  7.3 1.7 %collective-permute-start.1 = (bf16[256,256]{1,0:T(8,128)(2,1)S(1)}, bf16[256,256]{1,0:T(8,128)(2,1)S(1)}, u32[]{:S(2)}, u32[]{:S(2)}) collective-permute-start(bf16[256,256]{1,0:T(8,128)(2,1)S(1)} %get-tuple-element.56), channel_id=1, source_target_pairs={{0,2},{1,5},{2,0},{3,7},{4,6},{5,1},{6,4},{7,3},{8,10},{9,13},{10,... | collective-permute-start | bytes 393224 | tf_op jit(solution)/shard_map/ppermute | solution.py:30
  9.0 2.2 %collective-permute-done.2 = bf16[128,256]{1,0:T(8,128)(2,1)S(1)} collective-permute-done((bf16[128,256]{1,0:T(8,128)(2,1)}, bf16[128,256]{1,0:T(8,128)(2,1)S(1)}, u32[]{:S(2)}, u32[]{:S(2)}) %collective-permute-start.2) | collective-permute-done | bytes 65568 | tf_op jit(solution)/shard_map/ppermute | solution.py:30
  11.2 1.4 %collective-permute-done.3 = bf16[128,256]{1,0:T(8,128)(2,1)S(1)} collective-permute-done((bf16[128,256]{1,0:T(8,128)(2,1)}, bf16[128,256]{1,0:T(8,128)(2,1)S(1)}, u32[]{:S(2)}, u32[]{:S(2)}) %collective-permute-start.3) | collective-permute-done | bytes 65568 | tf_op jit(solution)/shard_map/ppermute | solution.py:30
  12.6 1.6 %collective-permute-start.5 = (bf16[256,256]{1,0:T(8,128)(2,1)S(1)}, bf16[256,256]{1,0:T(8,128)(2,1)S(1)}, u32[]{:S(2)}, u32[]{:S(2)}) collective-permute-start(bf16[256,256]{1,0:T(8,128)(2,1)S(1)} %get-tuple-element.53), channel_id=1, source_target_pairs={{0,2},{1,5},{2,0},{3,7},{4,6},{5,1},{6,4},{7,3},{8,10},{9,13},{10,... | collective-permute-start | bytes 393224 | tf_op jit(solution)/shard_map/ppermute | solution.py:30
  14.2 1.6 %collective-permute-start.4 = (bf16[512,256]{1,0:T(8,128)(2,1)S(1)}, bf16[512,256]{1,0:T(8,128)(2,1)S(1)}, u32[]{:S(2)}, u32[]{:S(2)}) collective-permute-start(bf16[512,256]{1,0:T(8,128)(2,1)S(1)} %constant_dynamic-update-slice_fusion.4.own_ref), channel_id=1, source_target_pairs={{0,4},{1,3},{2,6},{3,1},{4,0},{5,7},{6,2},{7,5},{8,12},{9,11},{10,... | collective-permute-start | bytes 786440 | tf_op jit(solution)/shard_map/ppermute | solution.py:30
  15.8 3.3 %collective-permute-done.5 = bf16[256,256]{1,0:T(8,128)(2,1)S(1)} collective-permute-done((bf16[256,256]{1,0:T(8,128)(2,1)S(1)}, bf16[256,256]{1,0:T(8,128)(2,1)S(1)}, u32[]{:S(2)}, u32[]{:S(2)}) %collective-permute-start.5) | collective-permute-done | bytes 131104 | tf_op jit(solution)/shard_map/ppermute | solution.py:30
  19.1 1.1 %collective-permute-start.7 = (bf16[512,256]{1,0:T(8,128)(2,1)S(1)}, bf16[512,256]{1,0:T(8,128)(2,1)S(1)}, u32[]{:S(2)}, u32[]{:S(2)}) collective-permute-start(bf16[512,256]{1,0:T(8,128)(2,1)S(1)} %constant_dynamic-update-slice_fusion.7.far_own_ref), channel_id=1, source_target_pairs={{0,4},{1,3},{2,6},{3,1},{4,0},{5,7},{6,2},{7,5},{8,12},{9,11},{10,... | collective-permute-start | bytes 786440 | tf_op jit(solution)/shard_map/ppermute | solution.py:30
  22.2 1.6 %shard_map.102 = (f32[256,256]{1,0:T(8,128)S(1)}, bf16[512,1024]{1,0:T(8,128)(2,1)S(1)}, bf16[1024,512]{1,0:T(8,128)(2,1)S(1)}, bf16[1024,512]{1,0:T(8,128)(2,1)...) custom-call(s32[1,1]{1,0:T(1,128)} %bitcast.position_ref, ...), custom_call_target="tpu_custom_call" | custom-call | tf_op jit(solution)/shard_map/pallas_call | solution.py:188
  23.8 1.8 %collective-permute-done.7.come_ref = bf16[512,256]{1,0:T(8,128)(2,1)S(1)} collective-permute-done((bf16[512,256]{1,0:T(8,128)(2,1)S(1)}, bf16[512,256]{1,0:T(8,128)(2,1)S(1)}, u32[]{:S(2)}, u32[]{:S(2)}) %collective-permute-start.7) | collective-permute-done | bytes 262176 | tf_op jit(solution)/shard_map/ppermute | solution.py:30
  26.0 1.5 %collective-permute-done.8.other_ref = f32[256,256]{1,0:T(8,128)S(1)} collective-permute-done((f32[256,256]{1,0:T(8,128)S(1)}, f32[256,256]{1,0:T(8,128)S(1)}, u32[]{:S(2)}, u32[]{:S(2)}) %collective-permute-start.8) | collective-permute-done | bytes 262176 | tf_op jit(solution)/shard_map/ppermute | solution.py:34
  27.5 0.9 %shard_map.104 = (bf16[512,256]{1,0:T(8,128)(2,1)S(1)}, bf16[128,256]{1,0:T(8,128)(2,1)}, bf16[512,256]{1,0:T(8,128)(2,1)S(1)}, bf16[256,256]{1,0:T(8,128)(2,1)S(1)}, f32[256,256]{1,0:T(8,128)S(1)}) custom-call(f32[256,256]{1,0:T(8,128)S(1)} %shard_map.103.mine_ref, f32[256,256]{1,0:T(8,128)S(1)} %collective-permute-done.8.other_ref, ...), custom_call_target="tpu_custom_call" | custom-call | tf_op jit(solution)/shard_map/pallas_call | solution.py:188
  28.4 1.0 %collective-permute-start.11 = (bf16[512,256]{1,0:T(8,128)(2,1)S(1)}, bf16[512,256]{1,0:T(8,128)(2,1)S(1)}, u32[]{:S(2)}, u32[]{:S(2)}) collective-permute-start(bf16[512,256]{1,0:T(8,128)(2,1)S(1)} %get-tuple-element.43), channel_id=1, source_target_pairs={{0,4},{1,3},{2,6},{3,1},{4,0},{5,7},{6,2},{7,5},{8,12},{9,11},{10,... | collective-permute-start | bytes 786440 | tf_op jit(solution)/shard_map/ppermute | solution.py:30
  31.4 3.7 %collective-permute-done.16.other_ref = bf16[144,256]{1,0:T(8,128)(2,1)S(1)} collective-permute-done((bf16[144,256]{1,0:T(8,128)(2,1)S(1)}, bf16[144,256]{1,0:T(8,128)(2,1)S(1)}, u32[]{:S(2)}, u32[]{:S(2)}) %collective-permute-start.16) | collective-permute-done | bytes 73760 | tf_op jit(solution)/shard_map/ppermute | solution.py:30
  35.2 1.2 %collective-permute-start.17 = (bf16[144,256]{1,0:T(8,128)(2,1)S(1)}, bf16[144,256]{1,0:T(8,128)(2,1)S(1)}, u32[]{:S(2)}, u32[]{:S(2)}) collective-permute-start(bf16[144,256]{1,0:T(8,128)(2,1)S(1)} %shard_map.107.mine_ref), channel_id=1, source_target_pairs={{0,16},{1,9},{2,18},{3,11},{4,20},{5,13},{6,22},{7,15},{8,24},{9,1... | collective-permute-start | bytes 221192 | tf_op jit(solution)/shard_map/ppermute | solution.py:30
  36.5 1.6 %collective-permute-start.12 = (bf16[256,256]{1,0:T(8,128)(2,1)S(1)}, bf16[256,256]{1,0:T(8,128)(2,1)S(1)}, u32[]{:S(2)}, u32[]{:S(2)}) collective-permute-start(bf16[256,256]{1,0:T(8,128)(2,1)S(1)} %add_convert_fusion), channel_id=1, source_target_pairs={{0,2},{1,5},{2,0},{3,7},{4,6},{5,1},{6,4},{7,3},{8,10},{9,13},{10,... | collective-permute-start | bytes 393224 | tf_op jit(solution)/shard_map/ppermute | solution.py:30
  38.1 1.9 %collective-permute-start.10 = (bf16[256,256]{1,0:T(8,128)(2,1)S(1)}, bf16[256,256]{1,0:T(8,128)(2,1)S(1)}, u32[]{:S(2)}, u32[]{:S(2)}) collective-permute-start(bf16[256,256]{1,0:T(8,128)(2,1)S(1)} %add_convert_fusion.1), channel_id=1, source_target_pairs={{0,2},{1,5},{2,0},{3,7},{4,6},{5,1},{6,4},{7,3},{8,10},{9,13},{10,... | collective-permute-start | bytes 393224 | tf_op jit(solution)/shard_map/ppermute | solution.py:30
  40.8 1.4 %collective-permute-start.18 = (bf16[144,256]{1,0:T(8,128)(2,1)S(1)}, bf16[144,256]{1,0:T(8,128)(2,1)S(1)}, u32[]{:S(2)}, u32[]{:S(2)}) collective-permute-start(bf16[144,256]{1,0:T(8,128)(2,1)S(1)} %shard_map.108.mine_ref), channel_id=1, source_target_pairs={{0,2},{1,5},{2,0},{3,7},{4,6},{5,1},{6,4},{7,3},{8,10},{9,13},{10,... | collective-permute-start | bytes 221192 | tf_op jit(solution)/shard_map/ppermute | solution.py:30
  42.3 1.2 %collective-permute-start.13 = (bf16[128,256]{1,0:T(8,128)(2,1)S(1)}, bf16[128,256]{1,0:T(8,128)(2,1)S(1)}, u32[]{:S(2)}, u32[]{:S(2)}) collective-permute-start(bf16[128,256]{1,0:T(8,128)(2,1)S(1)} %get-tuple-element.50), channel_id=1, source_target_pairs={{0,16},{1,17},{2,18},{3,19},{4,20},{5,21},{6,22},{7,23},{8,24},{9,... | collective-permute-start | bytes 196616 | tf_op jit(solution)/shard_map/ppermute | solution.py:30
  43.5 1.9 %collective-permute-start.14 = (bf16[128,256]{1,0:T(8,128)(2,1)S(1)}, bf16[128,256]{1,0:T(8,128)(2,1)S(1)}, u32[]{:S(2)}, u32[]{:S(2)}) collective-permute-start(bf16[128,256]{1,0:T(8,128)(2,1)S(1)} %get-tuple-element.51), channel_id=1, source_target_pairs={{0,24},{1,25},{2,26},{3,27},{4,28},{5,29},{6,30},{7,31},{8,16},{9,... | collective-permute-start | bytes 196616 | tf_op jit(solution)/shard_map/ppermute | solution.py:30
  45.4 0.8 %collective-permute-start.19 = (bf16[144,256]{1,0:T(8,128)(2,1)S(1)}, bf16[144,256]{1,0:T(8,128)(2,1)S(1)}, u32[]{:S(2)}, u32[]{:S(2)}) collective-permute-start(bf16[144,256]{1,0:T(8,128)(2,1)S(1)} %shard_map.109.mine_ref), channel_id=1, source_target_pairs={{0,4},{1,3},{2,6},{3,1},{4,0},{5,7},{6,2},{7,5},{8,12},{9,11},{10,... | collective-permute-start | bytes 221192 | tf_op jit(solution)/shard_map/ppermute | solution.py:30
  47.1 2.8 %collective-permute-done.19.other_ref = bf16[144,256]{1,0:T(8,128)(2,1)S(1)} collective-permute-done((bf16[144,256]{1,0:T(8,128)(2,1)S(1)}, bf16[144,256]{1,0:T(8,128)(2,1)S(1)}, u32[]{:S(2)}, u32[]{:S(2)}) %collective-permute-start.19) | collective-permute-done | bytes 73760 | tf_op jit(solution)/shard_map/ppermute | solution.py:30
  (52 shorter events, 8.3 us)
Async XLA Ops:
  0.6 20.9 %copy-start = (bf16[1,1,16,2,128,128]{5,4,3,2,1,0:T(8,128)(2,1)S(1)}, bf16[1,1,16,2,128,128]{5,4,3,2,1,0:T(8,128)(2,1)}, u32[]{:S(2)}) copy-start(bf16[1,1,16,2,128,128]{5,4,3,2,1,0:T(8,128)(2,1)} %param.10) | copy-start | bytes 3145732
  0.6 6.6 %collective-permute-start = (bf16[128,256]{1,0:T(8,128)(2,1)}, bf16[128,256]{1,0:T(8,128)(2,1)S(1)}, u32[]{:S(2)}, u32[]{:S(2)}) collective-permute-start(bf16[128,256]{1,0:T(8,128)(2,1)} %param.7), channel_id=1, source_target_pairs={{0,8},{1,9},{2,10},{3,11},{4,12},{5,13},{6,14},{7,15},{8,0},{9,1},... | collective-permute-start | bytes 196616 | tf_op jit(solution)/shard_map/ppermute | solution.py:30
  3.7 7.5 %collective-permute-start.2 = (bf16[128,256]{1,0:T(8,128)(2,1)}, bf16[128,256]{1,0:T(8,128)(2,1)S(1)}, u32[]{:S(2)}, u32[]{:S(2)}) collective-permute-start(bf16[128,256]{1,0:T(8,128)(2,1)} %param.7), channel_id=1, source_target_pairs={{0,16},{1,17},{2,18},{3,19},{4,20},{5,21},{6,22},{7,23},{8,24},{9,... | collective-permute-start | bytes 196616 | tf_op jit(solution)/shard_map/ppermute | solution.py:30
  6.3 6.3 %collective-permute-start.3 = (bf16[128,256]{1,0:T(8,128)(2,1)}, bf16[128,256]{1,0:T(8,128)(2,1)S(1)}, u32[]{:S(2)}, u32[]{:S(2)}) collective-permute-start(bf16[128,256]{1,0:T(8,128)(2,1)} %param.7), channel_id=1, source_target_pairs={{0,24},{1,25},{2,26},{3,27},{4,28},{5,29},{6,30},{7,31},{8,16},{9,... | collective-permute-start | bytes 196616 | tf_op jit(solution)/shard_map/ppermute | solution.py:30
  7.3 6.9 %collective-permute-start.1 = (bf16[256,256]{1,0:T(8,128)(2,1)S(1)}, bf16[256,256]{1,0:T(8,128)(2,1)S(1)}, u32[]{:S(2)}, u32[]{:S(2)}) collective-permute-start(bf16[256,256]{1,0:T(8,128)(2,1)S(1)} %get-tuple-element.56), channel_id=1, source_target_pairs={{0,2},{1,5},{2,0},{3,7},{4,6},{5,1},{6,4},{7,3},{8,10},{9,13},{10,... | collective-permute-start | bytes 393224 | tf_op jit(solution)/shard_map/ppermute | solution.py:30
  12.6 6.5 %collective-permute-start.5 = (bf16[256,256]{1,0:T(8,128)(2,1)S(1)}, bf16[256,256]{1,0:T(8,128)(2,1)S(1)}, u32[]{:S(2)}, u32[]{:S(2)}) collective-permute-start(bf16[256,256]{1,0:T(8,128)(2,1)S(1)} %get-tuple-element.53), channel_id=1, source_target_pairs={{0,2},{1,5},{2,0},{3,7},{4,6},{5,1},{6,4},{7,3},{8,10},{9,13},{10,... | collective-permute-start | bytes 393224 | tf_op jit(solution)/shard_map/ppermute | solution.py:30
  14.2 7.3 %collective-permute-start.4 = (bf16[512,256]{1,0:T(8,128)(2,1)S(1)}, bf16[512,256]{1,0:T(8,128)(2,1)S(1)}, u32[]{:S(2)}, u32[]{:S(2)}) collective-permute-start(bf16[512,256]{1,0:T(8,128)(2,1)S(1)} %constant_dynamic-update-slice_fusion.4.own_ref), channel_id=1, source_target_pairs={{0,4},{1,3},{2,6},{3,1},{4,0},{5,7},{6,2},{7,5},{8,12},{9,11},{10,... | collective-permute-start | bytes 786440 | tf_op jit(solution)/shard_map/ppermute | solution.py:30
  19.1 1.1 %copy-start.2 = (bf16[128,256]{1,0:T(8,128)(2,1)S(1)}, bf16[128,256]{1,0:T(8,128)(2,1)}, u32[]{:S(2)}) copy-start(bf16[128,256]{1,0:T(8,128)(2,1)} %cotangent_ref.1) | copy-start | bytes 196612
  19.1 2.4 %copy-start.1 = (bf16[256,256]{1,0:T(8,128)(2,1)S(1)}, bf16[256,256]{1,0:T(8,128)(2,1)}, u32[]{:S(2)}) copy-start(bf16[256,256]{1,0:T(8,128)(2,1)} %weight_ref.1) | copy-start | bytes 393220
  19.1 6.4 %collective-permute-start.7 = (bf16[512,256]{1,0:T(8,128)(2,1)S(1)}, bf16[512,256]{1,0:T(8,128)(2,1)S(1)}, u32[]{:S(2)}, u32[]{:S(2)}) collective-permute-start(bf16[512,256]{1,0:T(8,128)(2,1)S(1)} %constant_dynamic-update-slice_fusion.7.far_own_ref), channel_id=1, source_target_pairs={{0,4},{1,3},{2,6},{3,1},{4,0},{5,7},{6,2},{7,5},{8,12},{9,11},{10,... | collective-permute-start | bytes 786440 | tf_op jit(solution)/shard_map/ppermute | solution.py:30
  20.2 1.3 %collective-permute-start.6 = (bf16[128,256]{1,0:T(8,128)(2,1)S(1)}, bf16[128,256]{1,0:T(8,128)(2,1)S(1)}, u32[]{:S(2)}, u32[]{:S(2)}) collective-permute-start(bf16[128,256]{1,0:T(8,128)(2,1)S(1)} %copy-done.2), channel_id=1, source_target_pairs={{0,1},{1,0},{2,3},{3,2},{4,5},{5,4},{6,7},{7,6},{8,9},{9,8},{10,11... | collective-permute-start | bytes 196616 | tf_op jit(solution)/shard_map/ppermute | solution.py:34
  25.9 1.6 %collective-permute-start.8 = (f32[256,256]{1,0:T(8,128)S(1)}, f32[256,256]{1,0:T(8,128)S(1)}, u32[]{:S(2)}, u32[]{:S(2)}) collective-permute-start(f32[256,256]{1,0:T(8,128)S(1)} %shard_map.103.mine_ref), channel_id=1, source_target_pairs={{0,1},{1,0},{2,3},{3,2},{4,5},{5,4},{6,7},{7,6},{8,9},{9,8},{10,11... | collective-permute-start | bytes 786440 | tf_op jit(solution)/shard_map/ppermute | solution.py:34
  28.4 6.8 %collective-permute-start.11 = (bf16[512,256]{1,0:T(8,128)(2,1)S(1)}, bf16[512,256]{1,0:T(8,128)(2,1)S(1)}, u32[]{:S(2)}, u32[]{:S(2)}) collective-permute-start(bf16[512,256]{1,0:T(8,128)(2,1)S(1)} %get-tuple-element.43), channel_id=1, source_target_pairs={{0,4},{1,3},{2,6},{3,1},{4,0},{5,7},{6,2},{7,5},{8,12},{9,11},{10,... | collective-permute-start | bytes 786440 | tf_op jit(solution)/shard_map/ppermute | solution.py:30
  30.0 5.2 %collective-permute-start.16 = (bf16[144,256]{1,0:T(8,128)(2,1)S(1)}, bf16[144,256]{1,0:T(8,128)(2,1)S(1)}, u32[]{:S(2)}, u32[]{:S(2)}) collective-permute-start(bf16[144,256]{1,0:T(8,128)(2,1)S(1)} %get-tuple-element.44.mine_ref), channel_id=1, source_target_pairs={{0,8},{1,17},{2,10},{3,19},{4,12},{5,21},{6,14},{7,23},{8,0},{9,25... | collective-permute-start | bytes 221192 | tf_op jit(solution)/shard_map/ppermute | solution.py:30
  30.7 7.3 %collective-permute-start.9 = (bf16[512,256]{1,0:T(8,128)(2,1)S(1)}, bf16[512,256]{1,0:T(8,128)(2,1)S(1)}, u32[]{:S(2)}, u32[]{:S(2)}) collective-permute-start(bf16[512,256]{1,0:T(8,128)(2,1)S(1)} %shard_map.106), channel_id=1, source_target_pairs={{0,4},{1,3},{2,6},{3,1},{4,0},{5,7},{6,2},{7,5},{8,12},{9,11},{10,... | collective-permute-start | bytes 786440 | tf_op jit(solution)/shard_map/ppermute | solution.py:30
  35.2 5.6 %collective-permute-start.17 = (bf16[144,256]{1,0:T(8,128)(2,1)S(1)}, bf16[144,256]{1,0:T(8,128)(2,1)S(1)}, u32[]{:S(2)}, u32[]{:S(2)}) collective-permute-start(bf16[144,256]{1,0:T(8,128)(2,1)S(1)} %shard_map.107.mine_ref), channel_id=1, source_target_pairs={{0,16},{1,9},{2,18},{3,11},{4,20},{5,13},{6,22},{7,15},{8,24},{9,1... | collective-permute-start | bytes 221192 | tf_op jit(solution)/shard_map/ppermute | solution.py:30
  36.5 5.8 %collective-permute-start.12 = (bf16[256,256]{1,0:T(8,128)(2,1)S(1)}, bf16[256,256]{1,0:T(8,128)(2,1)S(1)}, u32[]{:S(2)}, u32[]{:S(2)}) collective-permute-start(bf16[256,256]{1,0:T(8,128)(2,1)S(1)} %add_convert_fusion), channel_id=1, source_target_pairs={{0,2},{1,5},{2,0},{3,7},{4,6},{5,1},{6,4},{7,3},{8,10},{9,13},{10,... | collective-permute-start | bytes 393224 | tf_op jit(solution)/shard_map/ppermute | solution.py:30
  38.1 7.4 %collective-permute-start.10 = (bf16[256,256]{1,0:T(8,128)(2,1)S(1)}, bf16[256,256]{1,0:T(8,128)(2,1)S(1)}, u32[]{:S(2)}, u32[]{:S(2)}) collective-permute-start(bf16[256,256]{1,0:T(8,128)(2,1)S(1)} %add_convert_fusion.1), channel_id=1, source_target_pairs={{0,2},{1,5},{2,0},{3,7},{4,6},{5,1},{6,4},{7,3},{8,10},{9,13},{10,... | collective-permute-start | bytes 393224 | tf_op jit(solution)/shard_map/ppermute | solution.py:30
  40.8 4.6 %collective-permute-start.18 = (bf16[144,256]{1,0:T(8,128)(2,1)S(1)}, bf16[144,256]{1,0:T(8,128)(2,1)S(1)}, u32[]{:S(2)}, u32[]{:S(2)}) collective-permute-start(bf16[144,256]{1,0:T(8,128)(2,1)S(1)} %shard_map.108.mine_ref), channel_id=1, source_target_pairs={{0,2},{1,5},{2,0},{3,7},{4,6},{5,1},{6,4},{7,3},{8,10},{9,13},{10,... | collective-permute-start | bytes 221192 | tf_op jit(solution)/shard_map/ppermute | solution.py:30
  42.3 7.7 %collective-permute-start.13 = (bf16[128,256]{1,0:T(8,128)(2,1)S(1)}, bf16[128,256]{1,0:T(8,128)(2,1)S(1)}, u32[]{:S(2)}, u32[]{:S(2)}) collective-permute-start(bf16[128,256]{1,0:T(8,128)(2,1)S(1)} %get-tuple-element.50), channel_id=1, source_target_pairs={{0,16},{1,17},{2,18},{3,19},{4,20},{5,21},{6,22},{7,23},{8,24},{9,... | collective-permute-start | bytes 196616 | tf_op jit(solution)/shard_map/ppermute | solution.py:30
  43.5 6.5 %collective-permute-start.14 = (bf16[128,256]{1,0:T(8,128)(2,1)S(1)}, bf16[128,256]{1,0:T(8,128)(2,1)S(1)}, u32[]{:S(2)}, u32[]{:S(2)}) collective-permute-start(bf16[128,256]{1,0:T(8,128)(2,1)S(1)} %get-tuple-element.51), channel_id=1, source_target_pairs={{0,24},{1,25},{2,26},{3,27},{4,28},{5,29},{6,30},{7,31},{8,16},{9,... | collective-permute-start | bytes 196616 | tf_op jit(solution)/shard_map/ppermute | solution.py:30
  45.4 4.4 %collective-permute-start.19 = (bf16[144,256]{1,0:T(8,128)(2,1)S(1)}, bf16[144,256]{1,0:T(8,128)(2,1)S(1)}, u32[]{:S(2)}, u32[]{:S(2)}) collective-permute-start(bf16[144,256]{1,0:T(8,128)(2,1)S(1)} %shard_map.109.mine_ref), channel_id=1, source_target_pairs={{0,4},{1,3},{2,6},{3,1},{4,0},{5,7},{6,2},{7,5},{8,12},{9,11},{10,... | collective-permute-start | bytes 221192 | tf_op jit(solution)/shard_map/ppermute | solution.py:30
  46.3 4.3 %collective-permute-start.15 = (bf16[128,256]{1,0:T(8,128)(2,1)S(1)}, bf16[128,256]{1,0:T(8,128)(2,1)S(1)}, u32[]{:S(2)}, u32[]{:S(2)}) collective-permute-start(bf16[128,256]{1,0:T(8,128)(2,1)S(1)} %add_convert_fusion.3), channel_id=1, source_target_pairs={{0,8},{1,9},{2,10},{3,11},{4,12},{5,13},{6,14},{7,15},{8,0},{9,1},... | collective-permute-start | bytes 196616 | tf_op jit(solution)/shard_map/ppermute | solution.py:30
  49.9 1.4 %collective-permute-start.20 = (f32[136,256]{1,0:T(8,128)S(1)}, f32[136,256]{1,0:T(8,128)S(1)}, u32[]{:S(2)}, u32[]{:S(2)}) collective-permute-start(f32[136,256]{1,0:T(8,128)S(1)} %shard_map.110.mine_ref), channel_id=1, source_target_pairs={{0,1},{1,0},{2,3},{3,2},{4,5},{5,4},{6,7},{7,6},{8,9},{9,8},{10,11... | collective-permute-start | bytes 417800 | tf_op jit(solution)/shard_map/ppermute | solution.py:34
  (3 other events, 2.0 us)

commit v6 on v5

--- a/solution.py
+++ b/solution.py
@@ -104,20 +104,17 @@
 
 def middle_kernel(
     mine_ref, other_ref, weight_ref, bias_ref, panel_ref, far_t_ref,
-    message_ref, output_ref, back_ref, grad_ref, sums_ref,
+    message_ref, preact_ref, back_ref, grad_ref, sums_ref,
 ):
-    rows = output_ref.shape[0]
+    rows = preact_ref.shape[0]
     sums_ref[:rows] = mine_ref[:rows] + other_ref[rows:]
     sums_ref[rows:] = mine_ref[rows:] + other_ref[:rows]
     high, low = split(sums_ref[...])
     weight = weight_ref[...]
     preact = dot(high, weight) + dot(low, weight) + bias_ref[...]
     negative = jnp.minimum(preact, 0.0)
-    grown = jnp.exp(negative)
-    slope = jnp.where(preact > 0, 1.0, grown)
-    own = preact[:rows]
-    below = exp_less_one(negative[:rows], grown[:rows])
-    output_ref[...] = jnp.where(own > 0, own, below).astype(BF16)
+    slope = jnp.where(preact > 0, 1.0, jnp.exp(negative))
+    preact_ref[...] = preact[:rows]
     grad_ref[...] = (panel_ref[...].astype(F32) * slope).astype(BF16)
     back = dot(grad_ref[...], weight, ((1,), (1,))).astype(BF16)
     back_ref[: 2 * rows] = back
@@ -157,7 +154,7 @@
     out_ref[share:] = jnp.broadcast_to(bias_term, (8, bias_term.shape[1]))
 
 
-def keep_kernel(rep_ref, near_t_ref, far_t_ref, back_ref, grad_ref, sums_ref, near_ref, far_ref, term_ref):
+def term_kernel(rep_ref, grad_ref, sums_ref, term_ref):
     share = term_ref.shape[0] - 16
     sums = sums_ref[...]
     mine = jnp.where(rep_ref[0, 0] == 0, sums[:, :share], sums[:, share:])
@@ -166,9 +163,16 @@
     rows = ((0,), (0,))
     own = jnp.sum(grad[: grad.shape[0] // 2].astype(F32), axis=0, keepdims=True)
     pack_terms(term_ref, dot(high, grad, rows) + dot(low, grad, rows), own)
+
+
+def keep_kernel(near_t_ref, far_t_ref, back_ref, preact_ref, near_ref, far_ref, output_ref):
     wide = near_ref.shape[0]
     far_ref[...] = dot(far_t_ref[:wide], back_ref[...])
     near_ref[...] = dot(near_t_ref[:wide], back_ref[...])
+    own = preact_ref[...]
+    negative = jnp.minimum(own, 0.0)
+    below = exp_less_one(negative, jnp.exp(negative))
+    output_ref[...] = jnp.where(own > 0, own, below).astype(BF16)
 
 
 def final_kernel(rep_ref, mine_ref, other_ref, weight_ref, bias_ref, *, scale):
@@ -278,23 +282,22 @@
         cotangent, pair_cotangent, weight, bias_vector.reshape(1, width_out),
     )
     (sums,) = on_chip(far_kernel, [((rows, width_in), F32)])(sums, far, come_far)
-    far_message, output, back, grad_pre, sums = on_chip(
+    far_message, preact, back, grad_pre, sums = on_chip(
         middle_kernel,
         [
             ((wide // 2, width_in), BF16),
-            ((rows_own, width_out), BF16),
+            ((rows_own, width_out), F32),
             ((slots * rows, width_in), BF16),
             ((rows, width_out), BF16),
             ((rows, width_in), F32),
         ],
     )(sums, swap_rep(sums, 1, 2), weight, bias, panel, far_t)
     (near_message,) = on_chip(message_kernel, [((wide // 2, width_in), BF16)])(near_t, back)
-    near_keep, far_keep, term = on_chip(
+    (term,) = on_chip(term_kernel, [((share + 16, width_out), BF16)], (), 1)(rep, grad_pre, sums)
+    near_keep, far_keep, output = on_chip(
         keep_kernel,
-        [((wide // 2, width_in), F32), ((wide // 2, width_in), F32), ((share + 16, width_out), BF16)],
-        (),
-        1,
-    )(rep, near_t, far_t, back, grad_pre, sums)
+        [((wide // 2, width_in), F32), ((wide // 2, width_in), F32), ((rows_own, width_out), BF16)],
+    )(near_t, far_t, back, preact)
 
     far_1 = move(far_message, second)
     near_1 = move(near_message, second)

time: 52.3 us -> 52.1 us (level)
  waiting for transfers between devices: 18.8 us -> 17.5 us
  Pallas kernels: 4.51 us -> 5.09 us
    ppermute x18, waiting for transfers between devices: 16.7 us -> 15.5 us  [exchange(): return lax.ppermute(value, ('loop', 'rep'), pairs)]
    pallas_call x10 -> x11, Pallas kernels: 4.51 us -> 5.09 us  [call(): pl.pallas_call(kernel, out_shape=tuple((jax.ShapeDtypeStruct(*shape) for...]
  transfers between devices with their start and end apart: 21 -> 21, of which waited for: 10 -> 11; matrix products, arithmetic and copies ran while one was open for 4% -> 4% of each run, Pallas kernels for 5% -> 6%
where the time goes in v6:
time: 52.1 us; the launch traced here: 51.9 us
  starting transfers between devices  25.2 us (48%)
  waiting for transfers between devices  17.5 us (34%)
  Pallas kernels  5.09 us (10%)
  local copies, waits for them, and re-layouts  2.4 us (5%)
  other arithmetic  0.83 us (2%)
  between operations  0.82 us (2%)
    ppermute x18, starting transfers between devices, exchange(): return lax.ppermute(value, ('loop', 'rep'), pairs)  25.1 us
    ppermute x18, waiting for transfers between devices, exchange(): return lax.ppermute(value, ('loop', 'rep'), pairs)  15.5 us
    pallas_call x11, Pallas kernels, call(): pl.pallas_call(kernel, out_shape=tuple((jax.ShapeDtypeStruct(*shape) for...  5.09 us
    unnamed x15, local copies, waits for them, and re-layouts  2.29 us
    ppermute x3, waiting for transfers between devices, swap_rep(): return lax.ppermute(value, 'rep', [(r, r ^ mask) for r in range(rep_size)])  2.01 us
  transfers between devices with their start and end apart: 21, of which 11 were waited for; matrix products, arithmetic and copies ran while one was open for 4% of the time, Pallas kernels for 6%

profile of v6, /device:TPU:0, one launch (start us, length us, event | category | flops | bytes accessed | tf_op | source)
XLA Modules:
  0.0 51.9 jit_solution(12189878095167233342)
XLA Ops:
  0.6 3.1 %collective-permute-start = (bf16[128,256]{1,0:T(8,128)(2,1)}, bf16[128,256]{1,0:T(8,128)(2,1)S(1)}, u32[]{:S(2)}, u32[]{:S(2)}) collective-permute-start(bf16[128,256]{1,0:T(8,128)(2,1)} %param.7), channel_id=1, source_target_pairs={{0,8},{1,9},{2,10},{3,11},{4,12},{5,13},{6,14},{7,15},{8,0},{9,1},... | collective-permute-start | bytes 196616 | tf_op jit(solution)/shard_map/ppermute | solution.py:30
  3.7 2.6 %collective-permute-start.2 = (bf16[128,256]{1,0:T(8,128)(2,1)}, bf16[128,256]{1,0:T(8,128)(2,1)S(1)}, u32[]{:S(2)}, u32[]{:S(2)}) collective-permute-start(bf16[128,256]{1,0:T(8,128)(2,1)} %param.7), channel_id=1, source_target_pairs={{0,16},{1,17},{2,18},{3,19},{4,20},{5,21},{6,22},{7,23},{8,24},{9,... | collective-permute-start | bytes 196616 | tf_op jit(solution)/shard_map/ppermute | solution.py:30
  7.3 1.7 %collective-permute-start.1 = (bf16[256,256]{1,0:T(8,128)(2,1)S(1)}, bf16[256,256]{1,0:T(8,128)(2,1)S(1)}, u32[]{:S(2)}, u32[]{:S(2)}) collective-permute-start(bf16[256,256]{1,0:T(8,128)(2,1)S(1)} %get-tuple-element.56), channel_id=1, source_target_pairs={{0,2},{1,5},{2,0},{3,7},{4,6},{5,1},{6,4},{7,3},{8,10},{9,13},{10,... | collective-permute-start | bytes 393224 | tf_op jit(solution)/shard_map/ppermute | solution.py:30
  9.0 2.2 %collective-permute-done.2 = bf16[128,256]{1,0:T(8,128)(2,1)S(1)} collective-permute-done((bf16[128,256]{1,0:T(8,128)(2,1)}, bf16[128,256]{1,0:T(8,128)(2,1)S(1)}, u32[]{:S(2)}, u32[]{:S(2)}) %collective-permute-start.2) | collective-permute-done | bytes 65568 | tf_op jit(solution)/shard_map/ppermute | solution.py:30
  11.2 1.4 %collective-permute-done.3 = bf16[128,256]{1,0:T(8,128)(2,1)S(1)} collective-permute-done((bf16[128,256]{1,0:T(8,128)(2,1)}, bf16[128,256]{1,0:T(8,128)(2,1)S(1)}, u32[]{:S(2)}, u32[]{:S(2)}) %collective-permute-start.3) | collective-permute-done | bytes 65568 | tf_op jit(solution)/shard_map/ppermute | solution.py:30
  12.6 1.6 %collective-permute-start.5 = (bf16[256,256]{1,0:T(8,128)(2,1)S(1)}, bf16[256,256]{1,0:T(8,128)(2,1)S(1)}, u32[]{:S(2)}, u32[]{:S(2)}) collective-permute-start(bf16[256,256]{1,0:T(8,128)(2,1)S(1)} %get-tuple-element.53), channel_id=1, source_target_pairs={{0,2},{1,5},{2,0},{3,7},{4,6},{5,1},{6,4},{7,3},{8,10},{9,13},{10,... | collective-permute-start | bytes 393224 | tf_op jit(solution)/shard_map/ppermute | solution.py:30
  14.2 1.6 %collective-permute-start.4 = (bf16[512,256]{1,0:T(8,128)(2,1)S(1)}, bf16[512,256]{1,0:T(8,128)(2,1)S(1)}, u32[]{:S(2)}, u32[]{:S(2)}) collective-permute-start(bf16[512,256]{1,0:T(8,128)(2,1)S(1)} %constant_dynamic-update-slice_fusion.4.own_ref), channel_id=1, source_target_pairs={{0,4},{1,3},{2,6},{3,1},{4,0},{5,7},{6,2},{7,5},{8,12},{9,11},{10,... | collective-permute-start | bytes 786440 | tf_op jit(solution)/shard_map/ppermute | solution.py:30
  15.8 3.3 %collective-permute-done.5 = bf16[256,256]{1,0:T(8,128)(2,1)S(1)} collective-permute-done((bf16[256,256]{1,0:T(8,128)(2,1)S(1)}, bf16[256,256]{1,0:T(8,128)(2,1)S(1)}, u32[]{:S(2)}, u32[]{:S(2)}) %collective-permute-start.5) | collective-permute-done | bytes 131104 | tf_op jit(solution)/shard_map/ppermute | solution.py:30
  19.1 1.1 %collective-permute-start.7 = (bf16[512,256]{1,0:T(8,128)(2,1)S(1)}, bf16[512,256]{1,0:T(8,128)(2,1)S(1)}, u32[]{:S(2)}, u32[]{:S(2)}) collective-permute-start(bf16[512,256]{1,0:T(8,128)(2,1)S(1)} %constant_dynamic-update-slice_fusion.7.far_own_ref), channel_id=1, source_target_pairs={{0,4},{1,3},{2,6},{3,1},{4,0},{5,7},{6,2},{7,5},{8,12},{9,11},{10,... | collective-permute-start | bytes 786440 | tf_op jit(solution)/shard_map/ppermute | solution.py:30
  22.2 1.6 %shard_map.102 = (f32[256,256]{1,0:T(8,128)S(1)}, bf16[512,1024]{1,0:T(8,128)(2,1)S(1)}, bf16[1024,512]{1,0:T(8,128)(2,1)S(1)}, bf16[1024,512]{1,0:T(8,128)(2,1)...) custom-call(s32[1,1]{1,0:T(1,128)} %bitcast.position_ref, ...), custom_call_target="tpu_custom_call" | custom-call | tf_op jit(solution)/shard_map/pallas_call | solution.py:192
  23.8 1.8 %collective-permute-done.7.come_ref = bf16[512,256]{1,0:T(8,128)(2,1)S(1)} collective-permute-done((bf16[512,256]{1,0:T(8,128)(2,1)S(1)}, bf16[512,256]{1,0:T(8,128)(2,1)S(1)}, u32[]{:S(2)}, u32[]{:S(2)}) %collective-permute-start.7) | collective-permute-done | bytes 262176 | tf_op jit(solution)/shard_map/ppermute | solution.py:30
  26.0 1.5 %collective-permute-done.8.other_ref = f32[256,256]{1,0:T(8,128)S(1)} collective-permute-done((f32[256,256]{1,0:T(8,128)S(1)}, f32[256,256]{1,0:T(8,128)S(1)}, u32[]{:S(2)}, u32[]{:S(2)}) %collective-permute-start.8) | collective-permute-done | bytes 262176 | tf_op jit(solution)/shard_map/ppermute | solution.py:34
  28.2 1.1 %collective-permute-start.11 = (bf16[512,256]{1,0:T(8,128)(2,1)S(1)}, bf16[512,256]{1,0:T(8,128)(2,1)S(1)}, u32[]{:S(2)}, u32[]{:S(2)}) collective-permute-start(bf16[512,256]{1,0:T(8,128)(2,1)S(1)} %get-tuple-element.42), channel_id=1, source_target_pairs={{0,4},{1,3},{2,6},{3,1},{4,0},{5,7},{6,2},{7,5},{8,12},{9,11},{10,... | collective-permute-start | bytes 786440 | tf_op jit(solution)/shard_map/ppermute | solution.py:30
  31.0 1.1 %shard_map.105 = (f32[512,256]{1,0:T(8,128)S(1)}, f32[512,256]{1,0:T(8,128)S(1)}, bf16[128,256]{1,0:T(8,128)(2,1)}) custom-call(bf16[1024,512]{1,0:T(8,128)(2,1)S(1)} %get-tuple-element.30.near_t_ref, bf16[1024,512]{1,0:T(8,128)(2,1)S(1)} %get-tuple-element.31.far_t_ref, bf16[512,256]{1,0:T(8,128)(2,1)S(1)} %get-tuple-element.37.back_ref, ...), custom_call_target="tpu_custom_call" | custom-call | tf_op jit(solution)/shard_map/pallas_call | solution.py:192
  32.1 2.7 %collective-permute-done.16.other_ref = bf16[144,256]{1,0:T(8,128)(2,1)S(1)} collective-permute-done((bf16[144,256]{1,0:T(8,128)(2,1)S(1)}, bf16[144,256]{1,0:T(8,128)(2,1)S(1)}, u32[]{:S(2)}, u32[]{:S(2)}) %collective-permute-start.16) | collective-permute-done | bytes 73760 | tf_op jit(solution)/shard_map/ppermute | solution.py:30
  34.8 1.4 %collective-permute-start.17 = (bf16[144,256]{1,0:T(8,128)(2,1)S(1)}, bf16[144,256]{1,0:T(8,128)(2,1)S(1)}, u32[]{:S(2)}, u32[]{:S(2)}) collective-permute-start(bf16[144,256]{1,0:T(8,128)(2,1)S(1)} %shard_map.108.mine_ref), channel_id=1, source_target_pairs={{0,16},{1,9},{2,18},{3,11},{4,20},{5,13},{6,22},{7,15},{8,24},{9,1... | collective-permute-start | bytes 221192 | tf_op jit(solution)/shard_map/ppermute | solution.py:30
  36.2 1.6 %collective-permute-start.12 = (bf16[256,256]{1,0:T(8,128)(2,1)S(1)}, bf16[256,256]{1,0:T(8,128)(2,1)S(1)}, u32[]{:S(2)}, u32[]{:S(2)}) collective-permute-start(bf16[256,256]{1,0:T(8,128)(2,1)S(1)} %add_convert_fusion), channel_id=1, source_target_pairs={{0,2},{1,5},{2,0},{3,7},{4,6},{5,1},{6,4},{7,3},{8,10},{9,13},{10,... | collective-permute-start | bytes 393224 | tf_op jit(solution)/shard_map/ppermute | solution.py:30
  37.9 1.9 %collective-permute-start.10 = (bf16[256,256]{1,0:T(8,128)(2,1)S(1)}, bf16[256,256]{1,0:T(8,128)(2,1)S(1)}, u32[]{:S(2)}, u32[]{:S(2)}) collective-permute-start(bf16[256,256]{1,0:T(8,128)(2,1)S(1)} %add_convert_fusion.1), channel_id=1, source_target_pairs={{0,2},{1,5},{2,0},{3,7},{4,6},{5,1},{6,4},{7,3},{8,10},{9,13},{10,... | collective-permute-start | bytes 393224 | tf_op jit(solution)/shard_map/ppermute | solution.py:30
  40.4 1.4 %collective-permute-start.18 = (bf16[144,256]{1,0:T(8,128)(2,1)S(1)}, bf16[144,256]{1,0:T(8,128)(2,1)S(1)}, u32[]{:S(2)}, u32[]{:S(2)}) collective-permute-start(bf16[144,256]{1,0:T(8,128)(2,1)S(1)} %shard_map.109.mine_ref), channel_id=1, source_target_pairs={{0,2},{1,5},{2,0},{3,7},{4,6},{5,1},{6,4},{7,3},{8,10},{9,13},{10,... | collective-permute-start | bytes 221192 | tf_op jit(solution)/shard_map/ppermute | solution.py:30
  41.9 1.3 %collective-permute-start.13 = (bf16[128,256]{1,0:T(8,128)(2,1)S(1)}, bf16[128,256]{1,0:T(8,128)(2,1)S(1)}, u32[]{:S(2)}, u32[]{:S(2)}) collective-permute-start(bf16[128,256]{1,0:T(8,128)(2,1)S(1)} %get-tuple-element.50), channel_id=1, source_target_pairs={{0,16},{1,17},{2,18},{3,19},{4,20},{5,21},{6,22},{7,23},{8,24},{9,... | collective-permute-start | bytes 196616 | tf_op jit(solution)/shard_map/ppermute | solution.py:30
  43.2 1.8 %collective-permute-start.14 = (bf16[128,256]{1,0:T(8,128)(2,1)S(1)}, bf16[128,256]{1,0:T(8,128)(2,1)S(1)}, u32[]{:S(2)}, u32[]{:S(2)}) collective-permute-start(bf16[128,256]{1,0:T(8,128)(2,1)S(1)} %get-tuple-element.51), channel_id=1, source_target_pairs={{0,24},{1,25},{2,26},{3,27},{4,28},{5,29},{6,30},{7,31},{8,16},{9,... | collective-permute-start | bytes 196616 | tf_op jit(solution)/shard_map/ppermute | solution.py:30
  45.0 1.1 %collective-permute-start.19 = (bf16[144,256]{1,0:T(8,128)(2,1)S(1)}, bf16[144,256]{1,0:T(8,128)(2,1)S(1)}, u32[]{:S(2)}, u32[]{:S(2)}) collective-permute-start(bf16[144,256]{1,0:T(8,128)(2,1)S(1)} %shard_map.110.mine_ref), channel_id=1, source_target_pairs={{0,4},{1,3},{2,6},{3,1},{4,0},{5,7},{6,2},{7,5},{8,12},{9,11},{10,... | collective-permute-start | bytes 221192 | tf_op jit(solution)/shard_map/ppermute | solution.py:30
  46.9 2.5 %collective-permute-done.19.other_ref = bf16[144,256]{1,0:T(8,128)(2,1)S(1)} collective-permute-done((bf16[144,256]{1,0:T(8,128)(2,1)S(1)}, bf16[144,256]{1,0:T(8,128)(2,1)S(1)}, u32[]{:S(2)}, u32[]{:S(2)}) %collective-permute-start.19) | collective-permute-done | bytes 73760 | tf_op jit(solution)/shard_map/ppermute | solution.py:30
  49.5 1.0 %collective-permute-done.15 = bf16[128,256]{1,0:T(8,128)(2,1)S(1)} collective-permute-done((bf16[128,256]{1,0:T(8,128)(2,1)S(1)}, bf16[128,256]{1,0:T(8,128)(2,1)S(1)}, u32[]{:S(2)}, u32[]{:S(2)}) %collective-permute-start.15) | collective-permute-done | bytes 65568 | tf_op jit(solution)/shard_map/ppermute | solution.py:30
  (53 shorter events, 8.9 us)
Async XLA Ops:
  0.6 20.9 %copy-start = (bf16[1,1,16,2,128,128]{5,4,3,2,1,0:T(8,128)(2,1)S(1)}, bf16[1,1,16,2,128,128]{5,4,3,2,1,0:T(8,128)(2,1)}, u32[]{:S(2)}) copy-start(bf16[1,1,16,2,128,128]{5,4,3,2,1,0:T(8,128)(2,1)} %param.10) | copy-start | bytes 3145732
  0.6 6.6 %collective-permute-start = (bf16[128,256]{1,0:T(8,128)(2,1)}, bf16[128,256]{1,0:T(8,128)(2,1)S(1)}, u32[]{:S(2)}, u32[]{:S(2)}) collective-permute-start(bf16[128,256]{1,0:T(8,128)(2,1)} %param.7), channel_id=1, source_target_pairs={{0,8},{1,9},{2,10},{3,11},{4,12},{5,13},{6,14},{7,15},{8,0},{9,1},... | collective-permute-start | bytes 196616 | tf_op jit(solution)/shard_map/ppermute | solution.py:30
  3.7 7.5 %collective-permute-start.2 = (bf16[128,256]{1,0:T(8,128)(2,1)}, bf16[128,256]{1,0:T(8,128)(2,1)S(1)}, u32[]{:S(2)}, u32[]{:S(2)}) collective-permute-start(bf16[128,256]{1,0:T(8,128)(2,1)} %param.7), channel_id=1, source_target_pairs={{0,16},{1,17},{2,18},{3,19},{4,20},{5,21},{6,22},{7,23},{8,24},{9,... | collective-permute-start | bytes 196616 | tf_op jit(solution)/shard_map/ppermute | solution.py:30
  6.3 6.3 %collective-permute-start.3 = (bf16[128,256]{1,0:T(8,128)(2,1)}, bf16[128,256]{1,0:T(8,128)(2,1)S(1)}, u32[]{:S(2)}, u32[]{:S(2)}) collective-permute-start(bf16[128,256]{1,0:T(8,128)(2,1)} %param.7), channel_id=1, source_target_pairs={{0,24},{1,25},{2,26},{3,27},{4,28},{5,29},{6,30},{7,31},{8,16},{9,... | collective-permute-start | bytes 196616 | tf_op jit(solution)/shard_map/ppermute | solution.py:30
  7.3 6.9 %collective-permute-start.1 = (bf16[256,256]{1,0:T(8,128)(2,1)S(1)}, bf16[256,256]{1,0:T(8,128)(2,1)S(1)}, u32[]{:S(2)}, u32[]{:S(2)}) collective-permute-start(bf16[256,256]{1,0:T(8,128)(2,1)S(1)} %get-tuple-element.56), channel_id=1, source_target_pairs={{0,2},{1,5},{2,0},{3,7},{4,6},{5,1},{6,4},{7,3},{8,10},{9,13},{10,... | collective-permute-start | bytes 393224 | tf_op jit(solution)/shard_map/ppermute | solution.py:30
  12.6 6.5 %collective-permute-start.5 = (bf16[256,256]{1,0:T(8,128)(2,1)S(1)}, bf16[256,256]{1,0:T(8,128)(2,1)S(1)}, u32[]{:S(2)}, u32[]{:S(2)}) collective-permute-start(bf16[256,256]{1,0:T(8,128)(2,1)S(1)} %get-tuple-element.53), channel_id=1, source_target_pairs={{0,2},{1,5},{2,0},{3,7},{4,6},{5,1},{6,4},{7,3},{8,10},{9,13},{10,... | collective-permute-start | bytes 393224 | tf_op jit(solution)/shard_map/ppermute | solution.py:30
  14.2 7.3 %collective-permute-start.4 = (bf16[512,256]{1,0:T(8,128)(2,1)S(1)}, bf16[512,256]{1,0:T(8,128)(2,1)S(1)}, u32[]{:S(2)}, u32[]{:S(2)}) collective-permute-start(bf16[512,256]{1,0:T(8,128)(2,1)S(1)} %constant_dynamic-update-slice_fusion.4.own_ref), channel_id=1, source_target_pairs={{0,4},{1,3},{2,6},{3,1},{4,0},{5,7},{6,2},{7,5},{8,12},{9,11},{10,... | collective-permute-start | bytes 786440 | tf_op jit(solution)/shard_map/ppermute | solution.py:30
  19.1 1.1 %copy-start.2 = (bf16[128,256]{1,0:T(8,128)(2,1)S(1)}, bf16[128,256]{1,0:T(8,128)(2,1)}, u32[]{:S(2)}) copy-start(bf16[128,256]{1,0:T(8,128)(2,1)} %cotangent_ref.1) | copy-start | bytes 196612
  19.1 2.4 %copy-start.1 = (bf16[256,256]{1,0:T(8,128)(2,1)S(1)}, bf16[256,256]{1,0:T(8,128)(2,1)}, u32[]{:S(2)}) copy-start(bf16[256,256]{1,0:T(8,128)(2,1)} %weight_ref.1) | copy-start | bytes 393220
  19.1 6.4 %collective-permute-start.7 = (bf16[512,256]{1,0:T(8,128)(2,1)S(1)}, bf16[512,256]{1,0:T(8,128)(2,1)S(1)}, u32[]{:S(2)}, u32[]{:S(2)}) collective-permute-start(bf16[512,256]{1,0:T(8,128)(2,1)S(1)} %constant_dynamic-update-slice_fusion.7.far_own_ref), channel_id=1, source_target_pairs={{0,4},{1,3},{2,6},{3,1},{4,0},{5,7},{6,2},{7,5},{8,12},{9,11},{10,... | collective-permute-start | bytes 786440 | tf_op jit(solution)/shard_map/ppermute | solution.py:30
  20.2 1.3 %collective-permute-start.6 = (bf16[128,256]{1,0:T(8,128)(2,1)S(1)}, bf16[128,256]{1,0:T(8,128)(2,1)S(1)}, u32[]{:S(2)}, u32[]{:S(2)}) collective-permute-start(bf16[128,256]{1,0:T(8,128)(2,1)S(1)} %copy-done.2), channel_id=1, source_target_pairs={{0,1},{1,0},{2,3},{3,2},{4,5},{5,4},{6,7},{7,6},{8,9},{9,8},{10,11... | collective-permute-start | bytes 196616 | tf_op jit(solution)/shard_map/ppermute | solution.py:34
  25.9 1.6 %collective-permute-start.8 = (f32[256,256]{1,0:T(8,128)S(1)}, f32[256,256]{1,0:T(8,128)S(1)}, u32[]{:S(2)}, u32[]{:S(2)}) collective-permute-start(f32[256,256]{1,0:T(8,128)S(1)} %shard_map.103.mine_ref), channel_id=1, source_target_pairs={{0,1},{1,0},{2,3},{3,2},{4,5},{5,4},{6,7},{7,6},{8,9},{9,8},{10,11... | collective-permute-start | bytes 786440 | tf_op jit(solution)/shard_map/ppermute | solution.py:34
  28.2 6.6 %collective-permute-start.11 = (bf16[512,256]{1,0:T(8,128)(2,1)S(1)}, bf16[512,256]{1,0:T(8,128)(2,1)S(1)}, u32[]{:S(2)}, u32[]{:S(2)}) collective-permute-start(bf16[512,256]{1,0:T(8,128)(2,1)S(1)} %get-tuple-element.42), channel_id=1, source_target_pairs={{0,4},{1,3},{2,6},{3,1},{4,0},{5,7},{6,2},{7,5},{8,12},{9,11},{10,... | collective-permute-start | bytes 786440 | tf_op jit(solution)/shard_map/ppermute | solution.py:30
  29.5 5.2 %collective-permute-start.16 = (bf16[144,256]{1,0:T(8,128)(2,1)S(1)}, bf16[144,256]{1,0:T(8,128)(2,1)S(1)}, u32[]{:S(2)}, u32[]{:S(2)}) collective-permute-start(bf16[144,256]{1,0:T(8,128)(2,1)S(1)} %shard_map.107.mine_ref), channel_id=1, source_target_pairs={{0,8},{1,17},{2,10},{3,19},{4,12},{5,21},{6,14},{7,23},{8,0},{9,25... | collective-permute-start | bytes 221192 | tf_op jit(solution)/shard_map/ppermute | solution.py:30
  30.3 7.6 %collective-permute-start.9 = (bf16[512,256]{1,0:T(8,128)(2,1)S(1)}, bf16[512,256]{1,0:T(8,128)(2,1)S(1)}, u32[]{:S(2)}, u32[]{:S(2)}) collective-permute-start(bf16[512,256]{1,0:T(8,128)(2,1)S(1)} %shard_map.106), channel_id=1, source_target_pairs={{0,4},{1,3},{2,6},{3,1},{4,0},{5,7},{6,2},{7,5},{8,12},{9,11},{10,... | collective-permute-start | bytes 786440 | tf_op jit(solution)/shard_map/ppermute | solution.py:30
  34.8 5.6 %collective-permute-start.17 = (bf16[144,256]{1,0:T(8,128)(2,1)S(1)}, bf16[144,256]{1,0:T(8,128)(2,1)S(1)}, u32[]{:S(2)}, u32[]{:S(2)}) collective-permute-start(bf16[144,256]{1,0:T(8,128)(2,1)S(1)} %shard_map.108.mine_ref), channel_id=1, source_target_pairs={{0,16},{1,9},{2,18},{3,11},{4,20},{5,13},{6,22},{7,15},{8,24},{9,1... | collective-permute-start | bytes 221192 | tf_op jit(solution)/shard_map/ppermute | solution.py:30
  36.2 5.6 %collective-permute-start.12 = (bf16[256,256]{1,0:T(8,128)(2,1)S(1)}, bf16[256,256]{1,0:T(8,128)(2,1)S(1)}, u32[]{:S(2)}, u32[]{:S(2)}) collective-permute-start(bf16[256,256]{1,0:T(8,128)(2,1)S(1)} %add_convert_fusion), channel_id=1, source_target_pairs={{0,2},{1,5},{2,0},{3,7},{4,6},{5,1},{6,4},{7,3},{8,10},{9,13},{10,... | collective-permute-start | bytes 393224 | tf_op jit(solution)/shard_map/ppermute | solution.py:30
  37.9 7.1 %collective-permute-start.10 = (bf16[256,256]{1,0:T(8,128)(2,1)S(1)}, bf16[256,256]{1,0:T(8,128)(2,1)S(1)}, u32[]{:S(2)}, u32[]{:S(2)}) collective-permute-start(bf16[256,256]{1,0:T(8,128)(2,1)S(1)} %add_convert_fusion.1), channel_id=1, source_target_pairs={{0,2},{1,5},{2,0},{3,7},{4,6},{5,1},{6,4},{7,3},{8,10},{9,13},{10,... | collective-permute-start | bytes 393224 | tf_op jit(solution)/shard_map/ppermute | solution.py:30
  40.4 4.6 %collective-permute-start.18 = (bf16[144,256]{1,0:T(8,128)(2,1)S(1)}, bf16[144,256]{1,0:T(8,128)(2,1)S(1)}, u32[]{:S(2)}, u32[]{:S(2)}) collective-permute-start(bf16[144,256]{1,0:T(8,128)(2,1)S(1)} %shard_map.109.mine_ref), channel_id=1, source_target_pairs={{0,2},{1,5},{2,0},{3,7},{4,6},{5,1},{6,4},{7,3},{8,10},{9,13},{10,... | collective-permute-start | bytes 221192 | tf_op jit(solution)/shard_map/ppermute | solution.py:30
  41.9 7.7 %collective-permute-start.13 = (bf16[128,256]{1,0:T(8,128)(2,1)S(1)}, bf16[128,256]{1,0:T(8,128)(2,1)S(1)}, u32[]{:S(2)}, u32[]{:S(2)}) collective-permute-start(bf16[128,256]{1,0:T(8,128)(2,1)S(1)} %get-tuple-element.50), channel_id=1, source_target_pairs={{0,16},{1,17},{2,18},{3,19},{4,20},{5,21},{6,22},{7,23},{8,24},{9,... | collective-permute-start | bytes 196616 | tf_op jit(solution)/shard_map/ppermute | solution.py:30
  43.2 6.3 %collective-permute-start.14 = (bf16[128,256]{1,0:T(8,128)(2,1)S(1)}, bf16[128,256]{1,0:T(8,128)(2,1)S(1)}, u32[]{:S(2)}, u32[]{:S(2)}) collective-permute-start(bf16[128,256]{1,0:T(8,128)(2,1)S(1)} %get-tuple-element.51), channel_id=1, source_target_pairs={{0,24},{1,25},{2,26},{3,27},{4,28},{5,29},{6,30},{7,31},{8,16},{9,... | collective-permute-start | bytes 196616 | tf_op jit(solution)/shard_map/ppermute | solution.py:30
  45.0 4.4 %collective-permute-start.19 = (bf16[144,256]{1,0:T(8,128)(2,1)S(1)}, bf16[144,256]{1,0:T(8,128)(2,1)S(1)}, u32[]{:S(2)}, u32[]{:S(2)}) collective-permute-start(bf16[144,256]{1,0:T(8,128)(2,1)S(1)} %shard_map.110.mine_ref), channel_id=1, source_target_pairs={{0,4},{1,3},{2,6},{3,1},{4,0},{5,7},{6,2},{7,5},{8,12},{9,11},{10,... | collective-permute-start | bytes 221192 | tf_op jit(solution)/shard_map/ppermute | solution.py:30
  46.2 4.3 %collective-permute-start.15 = (bf16[128,256]{1,0:T(8,128)(2,1)S(1)}, bf16[128,256]{1,0:T(8,128)(2,1)S(1)}, u32[]{:S(2)}, u32[]{:S(2)}) collective-permute-start(bf16[128,256]{1,0:T(8,128)(2,1)S(1)} %add_convert_fusion.3), channel_id=1, source_target_pairs={{0,8},{1,9},{2,10},{3,11},{4,12},{5,13},{6,14},{7,15},{8,0},{9,1},... | collective-permute-start | bytes 196616 | tf_op jit(solution)/shard_map/ppermute | solution.py:30
  49.4 1.7 %collective-permute-start.20 = (f32[136,256]{1,0:T(8,128)S(1)}, f32[136,256]{1,0:T(8,128)S(1)}, u32[]{:S(2)}, u32[]{:S(2)}) collective-permute-start(f32[136,256]{1,0:T(8,128)S(1)} %shard_map.111.mine_ref), channel_id=1, source_target_pairs={{0,1},{1,0},{2,3},{3,2},{4,5},{5,4},{6,7},{7,6},{8,9},{9,8},{10,11... | collective-permute-start | bytes 417800 | tf_op jit(solution)/shard_map/ppermute | solution.py:34
  (3 other events, 2.0 us)

commit v7 on v6

--- a/solution.py
+++ b/solution.py
@@ -87,9 +87,11 @@
     bias_out_ref[...] = bias_ref[...]
 
 
-def far_kernel(sums_ref, far_ref, come_ref, out_ref):
+def far_kernel(sums_ref, far_ref, come_ref, out_ref, last_ref):
     wide = come_ref.shape[0]
-    out_ref[...] = sums_ref[...] + fold(dot(far_ref[:, wide:], come_ref[...]))
+    last = fold(dot(far_ref[:, wide:], come_ref[...]))
+    out_ref[...] = sums_ref[...] + last
+    last_ref[...] = last.astype(BF16)
 
 
 def split(value):
@@ -103,12 +105,13 @@
 
 
 def middle_kernel(
-    mine_ref, other_ref, weight_ref, bias_ref, panel_ref, far_t_ref,
+    mine_ref, early_ref, last_ref, weight_ref, bias_ref, panel_ref, far_t_ref,
     message_ref, preact_ref, back_ref, grad_ref, sums_ref,
 ):
     rows = preact_ref.shape[0]
-    sums_ref[:rows] = mine_ref[:rows] + other_ref[rows:]
-    sums_ref[rows:] = mine_ref[rows:] + other_ref[:rows]
+    other = early_ref[...] + last_ref[...].astype(F32)
+    sums_ref[:rows] = mine_ref[:rows] + other[rows:]
+    sums_ref[rows:] = mine_ref[rows:] + other[:rows]
     high, low = split(sums_ref[...])
     weight = weight_ref[...]
     preact = dot(high, weight) + dot(low, weight) + bias_ref[...]
@@ -281,7 +284,8 @@
         position, rep, tile_place[0, 0], tile_count[0], tile_values[0, 0], own_near, come_near, own_far,
         cotangent, pair_cotangent, weight, bias_vector.reshape(1, width_out),
     )
-    (sums,) = on_chip(far_kernel, [((rows, width_in), F32)])(sums, far, come_far)
+    early = swap_rep(sums, 1, 2)
+    sums, last = on_chip(far_kernel, [((rows, width_in), F32), ((rows, width_in), BF16)])(sums, far, come_far)
     far_message, preact, back, grad_pre, sums = on_chip(
         middle_kernel,
         [
@@ -291,7 +295,7 @@
             ((rows, width_out), BF16),
             ((rows, width_in), F32),
         ],
-    )(sums, swap_rep(sums, 1, 2), weight, bias, panel, far_t)
+    )(sums, early, swap_rep(last, 1, 2), weight, bias, panel, far_t)
     (near_message,) = on_chip(message_kernel, [((wide // 2, width_in), BF16)])(near_t, back)
     (term,) = on_chip(term_kernel, [((share + 16, width_out), BF16)], (), 1)(rep, grad_pre, sums)
     near_keep, far_keep, output = on_chip(

time: 52.1 us -> 51.9 us (level)
    ppermute x3 -> x4, waiting for transfers between devices: 2.01 us -> 1.83 us  [swap_rep(): return lax.ppermute(value, 'rep', [(r, r ^ mask) for r in range(rep_size)])]
  transfers between devices with their start and end apart: 21 -> 22, of which waited for: 11 -> 11; matrix products, arithmetic and copies ran while one was open for 4% -> 4% of each run, Pallas kernels for 6% -> 7%
where the time goes in v7:
time: 51.9 us; the launch traced here: 51.7 us
  starting transfers between devices  25.5 us (49%)
  waiting for transfers between devices  17.2 us (33%)
  Pallas kernels  5.08 us (10%)
  local copies, waits for them, and re-layouts  2.4 us (5%)
  between operations  0.82 us (2%)
  other arithmetic  0.81 us (2%)
    ppermute x18, starting transfers between devices, exchange(): return lax.ppermute(value, ('loop', 'rep'), pairs)  25.1 us
    ppermute x18, waiting for transfers between devices, exchange(): return lax.ppermute(value, ('loop', 'rep'), pairs)  15.3 us
    pallas_call x11, Pallas kernels, call(): pl.pallas_call(kernel, out_shape=tuple((jax.ShapeDtypeStruct(*shape) for...  5.08 us
    unnamed x15, local copies, waits for them, and re-layouts  2.29 us
    ppermute x4, waiting for transfers between devices, swap_rep(): return lax.ppermute(value, 'rep', [(r, r ^ mask) for r in range(rep_size)])  1.83 us
  transfers between devices with their start and end apart: 22, of which 11 were waited for; matrix products, arithmetic and copies ran while one was open for 4% of the time, Pallas kernels for 7%

profile of v7, /device:TPU:0, one launch (start us, length us, event | category | flops | bytes accessed | tf_op | source)
XLA Modules:
  0.0 51.7 jit_solution(13975214106449780730)
XLA Ops:
  0.6 3.1 %collective-permute-start = (bf16[128,256]{1,0:T(8,128)(2,1)}, bf16[128,256]{1,0:T(8,128)(2,1)S(1)}, u32[]{:S(2)}, u32[]{:S(2)}) collective-permute-start(bf16[128,256]{1,0:T(8,128)(2,1)} %param.7), channel_id=1, source_target_pairs={{0,8},{1,9},{2,10},{3,11},{4,12},{5,13},{6,14},{7,15},{8,0},{9,1},... | collective-permute-start | bytes 196616 | tf_op jit(solution)/shard_map/ppermute | solution.py:30
  3.7 2.6 %collective-permute-start.2 = (bf16[128,256]{1,0:T(8,128)(2,1)}, bf16[128,256]{1,0:T(8,128)(2,1)S(1)}, u32[]{:S(2)}, u32[]{:S(2)}) collective-permute-start(bf16[128,256]{1,0:T(8,128)(2,1)} %param.7), channel_id=1, source_target_pairs={{0,16},{1,17},{2,18},{3,19},{4,20},{5,21},{6,22},{7,23},{8,24},{9,... | collective-permute-start | bytes 196616 | tf_op jit(solution)/shard_map/ppermute | solution.py:30
  7.3 1.7 %collective-permute-start.1 = (bf16[256,256]{1,0:T(8,128)(2,1)S(1)}, bf16[256,256]{1,0:T(8,128)(2,1)S(1)}, u32[]{:S(2)}, u32[]{:S(2)}) collective-permute-start(bf16[256,256]{1,0:T(8,128)(2,1)S(1)} %get-tuple-element.60), channel_id=1, source_target_pairs={{0,2},{1,5},{2,0},{3,7},{4,6},{5,1},{6,4},{7,3},{8,10},{9,13},{10,... | collective-permute-start | bytes 393224 | tf_op jit(solution)/shard_map/ppermute | solution.py:30
  9.0 2.2 %collective-permute-done.2 = bf16[128,256]{1,0:T(8,128)(2,1)S(1)} collective-permute-done((bf16[128,256]{1,0:T(8,128)(2,1)}, bf16[128,256]{1,0:T(8,128)(2,1)S(1)}, u32[]{:S(2)}, u32[]{:S(2)}) %collective-permute-start.2) | collective-permute-done | bytes 65568 | tf_op jit(solution)/shard_map/ppermute | solution.py:30
  11.2 1.4 %collective-permute-done.3 = bf16[128,256]{1,0:T(8,128)(2,1)S(1)} collective-permute-done((bf16[128,256]{1,0:T(8,128)(2,1)}, bf16[128,256]{1,0:T(8,128)(2,1)S(1)}, u32[]{:S(2)}, u32[]{:S(2)}) %collective-permute-start.3) | collective-permute-done | bytes 65568 | tf_op jit(solution)/shard_map/ppermute | solution.py:30
  12.6 1.6 %collective-permute-start.5 = (bf16[256,256]{1,0:T(8,128)(2,1)S(1)}, bf16[256,256]{1,0:T(8,128)(2,1)S(1)}, u32[]{:S(2)}, u32[]{:S(2)}) collective-permute-start(bf16[256,256]{1,0:T(8,128)(2,1)S(1)} %get-tuple-element.57), channel_id=1, source_target_pairs={{0,2},{1,5},{2,0},{3,7},{4,6},{5,1},{6,4},{7,3},{8,10},{9,13},{10,... | collective-permute-start | bytes 393224 | tf_op jit(solution)/shard_map/ppermute | solution.py:30
  14.2 1.6 %collective-permute-start.4 = (bf16[512,256]{1,0:T(8,128)(2,1)S(1)}, bf16[512,256]{1,0:T(8,128)(2,1)S(1)}, u32[]{:S(2)}, u32[]{:S(2)}) collective-permute-start(bf16[512,256]{1,0:T(8,128)(2,1)S(1)} %constant_dynamic-update-slice_fusion.4.own_ref), channel_id=1, source_target_pairs={{0,4},{1,3},{2,6},{3,1},{4,0},{5,7},{6,2},{7,5},{8,12},{9,11},{10,... | collective-permute-start | bytes 786440 | tf_op jit(solution)/shard_map/ppermute | solution.py:30
  15.8 3.3 %collective-permute-done.5 = bf16[256,256]{1,0:T(8,128)(2,1)S(1)} collective-permute-done((bf16[256,256]{1,0:T(8,128)(2,1)S(1)}, bf16[256,256]{1,0:T(8,128)(2,1)S(1)}, u32[]{:S(2)}, u32[]{:S(2)}) %collective-permute-start.5) | collective-permute-done | bytes 131104 | tf_op jit(solution)/shard_map/ppermute | solution.py:30
  19.1 1.1 %collective-permute-start.7 = (bf16[512,256]{1,0:T(8,128)(2,1)S(1)}, bf16[512,256]{1,0:T(8,128)(2,1)S(1)}, u32[]{:S(2)}, u32[]{:S(2)}) collective-permute-start(bf16[512,256]{1,0:T(8,128)(2,1)S(1)} %constant_dynamic-update-slice_fusion.7.far_own_ref), channel_id=1, source_target_pairs={{0,4},{1,3},{2,6},{3,1},{4,0},{5,7},{6,2},{7,5},{8,12},{9,11},{10,... | collective-permute-start | bytes 786440 | tf_op jit(solution)/shard_map/ppermute | solution.py:30
  22.2 1.6 %shard_map.102 = (f32[256,256]{1,0:T(8,128)S(1)}, bf16[512,1024]{1,0:T(8,128)(2,1)S(1)}, bf16[1024,512]{1,0:T(8,128)(2,1)S(1)}, bf16[1024,512]{1,0:T(8,128)(2,1)...) custom-call(s32[1,1]{1,0:T(1,128)} %bitcast.position_ref, ...), custom_call_target="tpu_custom_call" | custom-call | tf_op jit(solution)/shard_map/pallas_call | solution.py:195
  24.0 1.6 %collective-permute-done.7.come_ref = bf16[512,256]{1,0:T(8,128)(2,1)S(1)} collective-permute-done((bf16[512,256]{1,0:T(8,128)(2,1)S(1)}, bf16[512,256]{1,0:T(8,128)(2,1)S(1)}, u32[]{:S(2)}, u32[]{:S(2)}) %collective-permute-start.7) | collective-permute-done | bytes 262176 | tf_op jit(solution)/shard_map/ppermute | solution.py:30
  26.0 1.3 %collective-permute-done.9.last_ref = bf16[256,256]{1,0:T(8,128)(2,1)S(1)} collective-permute-done((bf16[256,256]{1,0:T(8,128)(2,1)S(1)}, bf16[256,256]{1,0:T(8,128)(2,1)S(1)}, u32[]{:S(2)}, u32[]{:S(2)}) %collective-permute-start.9) | collective-permute-done | bytes 131104 | tf_op jit(solution)/shard_map/ppermute | solution.py:34
  28.0 1.1 %collective-permute-start.12 = (bf16[512,256]{1,0:T(8,128)(2,1)S(1)}, bf16[512,256]{1,0:T(8,128)(2,1)S(1)}, u32[]{:S(2)}, u32[]{:S(2)}) collective-permute-start(bf16[512,256]{1,0:T(8,128)(2,1)S(1)} %get-tuple-element.46), channel_id=1, source_target_pairs={{0,4},{1,3},{2,6},{3,1},{4,0},{5,7},{6,2},{7,5},{8,12},{9,11},{10,... | collective-permute-start | bytes 786440 | tf_op jit(solution)/shard_map/ppermute | solution.py:30
  30.8 1.1 %shard_map.105 = (f32[512,256]{1,0:T(8,128)S(1)}, f32[512,256]{1,0:T(8,128)S(1)}, bf16[128,256]{1,0:T(8,128)(2,1)}) custom-call(bf16[1024,512]{1,0:T(8,128)(2,1)S(1)} %get-tuple-element.32.near_t_ref, bf16[1024,512]{1,0:T(8,128)(2,1)S(1)} %get-tuple-element.33.far_t_ref, bf16[512,256]{1,0:T(8,128)(2,1)S(1)} %get-tuple-element.41.back_ref, ...), custom_call_target="tpu_custom_call" | custom-call | tf_op jit(solution)/shard_map/pallas_call | solution.py:195
  31.9 2.7 %collective-permute-done.17.other_ref = bf16[144,256]{1,0:T(8,128)(2,1)S(1)} collective-permute-done((bf16[144,256]{1,0:T(8,128)(2,1)S(1)}, bf16[144,256]{1,0:T(8,128)(2,1)S(1)}, u32[]{:S(2)}, u32[]{:S(2)}) %collective-permute-start.17) | collective-permute-done | bytes 73760 | tf_op jit(solution)/shard_map/ppermute | solution.py:30
  34.6 1.4 %collective-permute-start.18 = (bf16[144,256]{1,0:T(8,128)(2,1)S(1)}, bf16[144,256]{1,0:T(8,128)(2,1)S(1)}, u32[]{:S(2)}, u32[]{:S(2)}) collective-permute-start(bf16[144,256]{1,0:T(8,128)(2,1)S(1)} %shard_map.108.mine_ref), channel_id=1, source_target_pairs={{0,16},{1,9},{2,18},{3,11},{4,20},{5,13},{6,22},{7,15},{8,24},{9,1... | collective-permute-start | bytes 221192 | tf_op jit(solution)/shard_map/ppermute | solution.py:30
  36.0 1.6 %collective-permute-start.13 = (bf16[256,256]{1,0:T(8,128)(2,1)S(1)}, bf16[256,256]{1,0:T(8,128)(2,1)S(1)}, u32[]{:S(2)}, u32[]{:S(2)}) collective-permute-start(bf16[256,256]{1,0:T(8,128)(2,1)S(1)} %add_convert_fusion), channel_id=1, source_target_pairs={{0,2},{1,5},{2,0},{3,7},{4,6},{5,1},{6,4},{7,3},{8,10},{9,13},{10,... | collective-permute-start | bytes 393224 | tf_op jit(solution)/shard_map/ppermute | solution.py:30
  37.7 1.9 %collective-permute-start.11 = (bf16[256,256]{1,0:T(8,128)(2,1)S(1)}, bf16[256,256]{1,0:T(8,128)(2,1)S(1)}, u32[]{:S(2)}, u32[]{:S(2)}) collective-permute-start(bf16[256,256]{1,0:T(8,128)(2,1)S(1)} %add_convert_fusion.1), channel_id=1, source_target_pairs={{0,2},{1,5},{2,0},{3,7},{4,6},{5,1},{6,4},{7,3},{8,10},{9,13},{10,... | collective-permute-start | bytes 393224 | tf_op jit(solution)/shard_map/ppermute | solution.py:30
  40.2 1.4 %collective-permute-start.19 = (bf16[144,256]{1,0:T(8,128)(2,1)S(1)}, bf16[144,256]{1,0:T(8,128)(2,1)S(1)}, u32[]{:S(2)}, u32[]{:S(2)}) collective-permute-start(bf16[144,256]{1,0:T(8,128)(2,1)S(1)} %shard_map.109.mine_ref), channel_id=1, source_target_pairs={{0,2},{1,5},{2,0},{3,7},{4,6},{5,1},{6,4},{7,3},{8,10},{9,13},{10,... | collective-permute-start | bytes 221192 | tf_op jit(solution)/shard_map/ppermute | solution.py:30
  41.7 1.3 %collective-permute-start.14 = (bf16[128,256]{1,0:T(8,128)(2,1)S(1)}, bf16[128,256]{1,0:T(8,128)(2,1)S(1)}, u32[]{:S(2)}, u32[]{:S(2)}) collective-permute-start(bf16[128,256]{1,0:T(8,128)(2,1)S(1)} %get-tuple-element.54), channel_id=1, source_target_pairs={{0,16},{1,17},{2,18},{3,19},{4,20},{5,21},{6,22},{7,23},{8,24},{9,... | collective-permute-start | bytes 196616 | tf_op jit(solution)/shard_map/ppermute | solution.py:30
  43.0 1.8 %collective-permute-start.15 = (bf16[128,256]{1,0:T(8,128)(2,1)S(1)}, bf16[128,256]{1,0:T(8,128)(2,1)S(1)}, u32[]{:S(2)}, u32[]{:S(2)}) collective-permute-start(bf16[128,256]{1,0:T(8,128)(2,1)S(1)} %get-tuple-element.55), channel_id=1, source_target_pairs={{0,24},{1,25},{2,26},{3,27},{4,28},{5,29},{6,30},{7,31},{8,16},{9,... | collective-permute-start | bytes 196616 | tf_op jit(solution)/shard_map/ppermute | solution.py:30
  44.8 1.1 %collective-permute-start.20 = (bf16[144,256]{1,0:T(8,128)(2,1)S(1)}, bf16[144,256]{1,0:T(8,128)(2,1)S(1)}, u32[]{:S(2)}, u32[]{:S(2)}) collective-permute-start(bf16[144,256]{1,0:T(8,128)(2,1)S(1)} %shard_map.110.mine_ref), channel_id=1, source_target_pairs={{0,4},{1,3},{2,6},{3,1},{4,0},{5,7},{6,2},{7,5},{8,12},{9,11},{10,... | collective-permute-start | bytes 221192 | tf_op jit(solution)/shard_map/ppermute | solution.py:30
  46.7 2.5 %collective-permute-done.20.other_ref = bf16[144,256]{1,0:T(8,128)(2,1)S(1)} collective-permute-done((bf16[144,256]{1,0:T(8,128)(2,1)S(1)}, bf16[144,256]{1,0:T(8,128)(2,1)S(1)}, u32[]{:S(2)}, u32[]{:S(2)}) %collective-permute-start.20) | collective-permute-done | bytes 73760 | tf_op jit(solution)/shard_map/ppermute | solution.py:30
  49.4 0.9 %collective-permute-done.16 = bf16[128,256]{1,0:T(8,128)(2,1)S(1)} collective-permute-done((bf16[128,256]{1,0:T(8,128)(2,1)S(1)}, bf16[128,256]{1,0:T(8,128)(2,1)S(1)}, u32[]{:S(2)}, u32[]{:S(2)}) %collective-permute-start.16) | collective-permute-done | bytes 65568 | tf_op jit(solution)/shard_map/ppermute | solution.py:30
  (55 shorter events, 9.1 us)
Async XLA Ops:
  0.6 20.9 %copy-start = (bf16[1,1,16,2,128,128]{5,4,3,2,1,0:T(8,128)(2,1)S(1)}, bf16[1,1,16,2,128,128]{5,4,3,2,1,0:T(8,128)(2,1)}, u32[]{:S(2)}) copy-start(bf16[1,1,16,2,128,128]{5,4,3,2,1,0:T(8,128)(2,1)} %param.10) | copy-start | bytes 3145732
  0.6 6.6 %collective-permute-start = (bf16[128,256]{1,0:T(8,128)(2,1)}, bf16[128,256]{1,0:T(8,128)(2,1)S(1)}, u32[]{:S(2)}, u32[]{:S(2)}) collective-permute-start(bf16[128,256]{1,0:T(8,128)(2,1)} %param.7), channel_id=1, source_target_pairs={{0,8},{1,9},{2,10},{3,11},{4,12},{5,13},{6,14},{7,15},{8,0},{9,1},... | collective-permute-start | bytes 196616 | tf_op jit(solution)/shard_map/ppermute | solution.py:30
  3.7 7.5 %collective-permute-start.2 = (bf16[128,256]{1,0:T(8,128)(2,1)}, bf16[128,256]{1,0:T(8,128)(2,1)S(1)}, u32[]{:S(2)}, u32[]{:S(2)}) collective-permute-start(bf16[128,256]{1,0:T(8,128)(2,1)} %param.7), channel_id=1, source_target_pairs={{0,16},{1,17},{2,18},{3,19},{4,20},{5,21},{6,22},{7,23},{8,24},{9,... | collective-permute-start | bytes 196616 | tf_op jit(solution)/shard_map/ppermute | solution.py:30
  6.3 6.3 %collective-permute-start.3 = (bf16[128,256]{1,0:T(8,128)(2,1)}, bf16[128,256]{1,0:T(8,128)(2,1)S(1)}, u32[]{:S(2)}, u32[]{:S(2)}) collective-permute-start(bf16[128,256]{1,0:T(8,128)(2,1)} %param.7), channel_id=1, source_target_pairs={{0,24},{1,25},{2,26},{3,27},{4,28},{5,29},{6,30},{7,31},{8,16},{9,... | collective-permute-start | bytes 196616 | tf_op jit(solution)/shard_map/ppermute | solution.py:30
  7.3 6.9 %collective-permute-start.1 = (bf16[256,256]{1,0:T(8,128)(2,1)S(1)}, bf16[256,256]{1,0:T(8,128)(2,1)S(1)}, u32[]{:S(2)}, u32[]{:S(2)}) collective-permute-start(bf16[256,256]{1,0:T(8,128)(2,1)S(1)} %get-tuple-element.60), channel_id=1, source_target_pairs={{0,2},{1,5},{2,0},{3,7},{4,6},{5,1},{6,4},{7,3},{8,10},{9,13},{10,... | collective-permute-start | bytes 393224 | tf_op jit(solution)/shard_map/ppermute | solution.py:30
  12.6 6.5 %collective-permute-start.5 = (bf16[256,256]{1,0:T(8,128)(2,1)S(1)}, bf16[256,256]{1,0:T(8,128)(2,1)S(1)}, u32[]{:S(2)}, u32[]{:S(2)}) collective-permute-start(bf16[256,256]{1,0:T(8,128)(2,1)S(1)} %get-tuple-element.57), channel_id=1, source_target_pairs={{0,2},{1,5},{2,0},{3,7},{4,6},{5,1},{6,4},{7,3},{8,10},{9,13},{10,... | collective-permute-start | bytes 393224 | tf_op jit(solution)/shard_map/ppermute | solution.py:30
  14.2 7.3 %collective-permute-start.4 = (bf16[512,256]{1,0:T(8,128)(2,1)S(1)}, bf16[512,256]{1,0:T(8,128)(2,1)S(1)}, u32[]{:S(2)}, u32[]{:S(2)}) collective-permute-start(bf16[512,256]{1,0:T(8,128)(2,1)S(1)} %constant_dynamic-update-slice_fusion.4.own_ref), channel_id=1, source_target_pairs={{0,4},{1,3},{2,6},{3,1},{4,0},{5,7},{6,2},{7,5},{8,12},{9,11},{10,... | collective-permute-start | bytes 786440 | tf_op jit(solution)/shard_map/ppermute | solution.py:30
  19.1 2.4 %copy-start.1 = (bf16[256,256]{1,0:T(8,128)(2,1)S(1)}, bf16[256,256]{1,0:T(8,128)(2,1)}, u32[]{:S(2)}) copy-start(bf16[256,256]{1,0:T(8,128)(2,1)} %weight_ref.1) | copy-start | bytes 393220
  19.1 6.4 %collective-permute-start.7 = (bf16[512,256]{1,0:T(8,128)(2,1)S(1)}, bf16[512,256]{1,0:T(8,128)(2,1)S(1)}, u32[]{:S(2)}, u32[]{:S(2)}) collective-permute-start(bf16[512,256]{1,0:T(8,128)(2,1)S(1)} %constant_dynamic-update-slice_fusion.7.far_own_ref), channel_id=1, source_target_pairs={{0,4},{1,3},{2,6},{3,1},{4,0},{5,7},{6,2},{7,5},{8,12},{9,11},{10,... | collective-permute-start | bytes 786440 | tf_op jit(solution)/shard_map/ppermute | solution.py:30
  20.2 1.3 %collective-permute-start.6 = (bf16[128,256]{1,0:T(8,128)(2,1)S(1)}, bf16[128,256]{1,0:T(8,128)(2,1)S(1)}, u32[]{:S(2)}, u32[]{:S(2)}) collective-permute-start(bf16[128,256]{1,0:T(8,128)(2,1)S(1)} %copy-done.2), channel_id=1, source_target_pairs={{0,1},{1,0},{2,3},{3,2},{4,5},{5,4},{6,7},{7,6},{8,9},{9,8},{10,11... | collective-permute-start | bytes 196616 | tf_op jit(solution)/shard_map/ppermute | solution.py:34
  23.8 3.5 %collective-permute-start.8 = (f32[256,256]{1,0:T(8,128)S(1)}, f32[256,256]{1,0:T(8,128)S(1)}, u32[]{:S(2)}, u32[]{:S(2)}) collective-permute-start(f32[256,256]{1,0:T(8,128)S(1)} %get-tuple-element.34.sums_ref), channel_id=1, source_target_pairs={{0,1},{1,0},{2,3},{3,2},{4,5},{5,4},{6,7},{7,6},{8,9},{9,8},{10,11... | collective-permute-start | bytes 786440 | tf_op jit(solution)/shard_map/ppermute | solution.py:34
  25.9 1.4 %collective-permute-start.9 = (bf16[256,256]{1,0:T(8,128)(2,1)S(1)}, bf16[256,256]{1,0:T(8,128)(2,1)S(1)}, u32[]{:S(2)}, u32[]{:S(2)}) collective-permute-start(bf16[256,256]{1,0:T(8,128)(2,1)S(1)} %get-tuple-element.37), channel_id=1, source_target_pairs={{0,1},{1,0},{2,3},{3,2},{4,5},{5,4},{6,7},{7,6},{8,9},{9,8},{10,11... | collective-permute-start | bytes 393224 | tf_op jit(solution)/shard_map/ppermute | solution.py:34
  28.0 6.6 %collective-permute-start.12 = (bf16[512,256]{1,0:T(8,128)(2,1)S(1)}, bf16[512,256]{1,0:T(8,128)(2,1)S(1)}, u32[]{:S(2)}, u32[]{:S(2)}) collective-permute-start(bf16[512,256]{1,0:T(8,128)(2,1)S(1)} %get-tuple-element.46), channel_id=1, source_target_pairs={{0,4},{1,3},{2,6},{3,1},{4,0},{5,7},{6,2},{7,5},{8,12},{9,11},{10,... | collective-permute-start | bytes 786440 | tf_op jit(solution)/shard_map/ppermute | solution.py:30
  29.3 5.2 %collective-permute-start.17 = (bf16[144,256]{1,0:T(8,128)(2,1)S(1)}, bf16[144,256]{1,0:T(8,128)(2,1)S(1)}, u32[]{:S(2)}, u32[]{:S(2)}) collective-permute-start(bf16[144,256]{1,0:T(8,128)(2,1)S(1)} %shard_map.107.mine_ref), channel_id=1, source_target_pairs={{0,8},{1,17},{2,10},{3,19},{4,12},{5,21},{6,14},{7,23},{8,0},{9,25... | collective-permute-start | bytes 221192 | tf_op jit(solution)/shard_map/ppermute | solution.py:30
  30.1 7.6 %collective-permute-start.10 = (bf16[512,256]{1,0:T(8,128)(2,1)S(1)}, bf16[512,256]{1,0:T(8,128)(2,1)S(1)}, u32[]{:S(2)}, u32[]{:S(2)}) collective-permute-start(bf16[512,256]{1,0:T(8,128)(2,1)S(1)} %shard_map.106), channel_id=1, source_target_pairs={{0,4},{1,3},{2,6},{3,1},{4,0},{5,7},{6,2},{7,5},{8,12},{9,11},{10,... | collective-permute-start | bytes 786440 | tf_op jit(solution)/shard_map/ppermute | solution.py:30
  34.6 5.6 %collective-permute-start.18 = (bf16[144,256]{1,0:T(8,128)(2,1)S(1)}, bf16[144,256]{1,0:T(8,128)(2,1)S(1)}, u32[]{:S(2)}, u32[]{:S(2)}) collective-permute-start(bf16[144,256]{1,0:T(8,128)(2,1)S(1)} %shard_map.108.mine_ref), channel_id=1, source_target_pairs={{0,16},{1,9},{2,18},{3,11},{4,20},{5,13},{6,22},{7,15},{8,24},{9,1... | collective-permute-start | bytes 221192 | tf_op jit(solution)/shard_map/ppermute | solution.py:30
  36.0 5.7 %collective-permute-start.13 = (bf16[256,256]{1,0:T(8,128)(2,1)S(1)}, bf16[256,256]{1,0:T(8,128)(2,1)S(1)}, u32[]{:S(2)}, u32[]{:S(2)}) collective-permute-start(bf16[256,256]{1,0:T(8,128)(2,1)S(1)} %add_convert_fusion), channel_id=1, source_target_pairs={{0,2},{1,5},{2,0},{3,7},{4,6},{5,1},{6,4},{7,3},{8,10},{9,13},{10,... | collective-permute-start | bytes 393224 | tf_op jit(solution)/shard_map/ppermute | solution.py:30
  37.7 7.1 %collective-permute-start.11 = (bf16[256,256]{1,0:T(8,128)(2,1)S(1)}, bf16[256,256]{1,0:T(8,128)(2,1)S(1)}, u32[]{:S(2)}, u32[]{:S(2)}) collective-permute-start(bf16[256,256]{1,0:T(8,128)(2,1)S(1)} %add_convert_fusion.1), channel_id=1, source_target_pairs={{0,2},{1,5},{2,0},{3,7},{4,6},{5,1},{6,4},{7,3},{8,10},{9,13},{10,... | collective-permute-start | bytes 393224 | tf_op jit(solution)/shard_map/ppermute | solution.py:30
  40.2 4.6 %collective-permute-start.19 = (bf16[144,256]{1,0:T(8,128)(2,1)S(1)}, bf16[144,256]{1,0:T(8,128)(2,1)S(1)}, u32[]{:S(2)}, u32[]{:S(2)}) collective-permute-start(bf16[144,256]{1,0:T(8,128)(2,1)S(1)} %shard_map.109.mine_ref), channel_id=1, source_target_pairs={{0,2},{1,5},{2,0},{3,7},{4,6},{5,1},{6,4},{7,3},{8,10},{9,13},{10,... | collective-permute-start | bytes 221192 | tf_op jit(solution)/shard_map/ppermute | solution.py:30
  41.7 7.7 %collective-permute-start.14 = (bf16[128,256]{1,0:T(8,128)(2,1)S(1)}, bf16[128,256]{1,0:T(8,128)(2,1)S(1)}, u32[]{:S(2)}, u32[]{:S(2)}) collective-permute-start(bf16[128,256]{1,0:T(8,128)(2,1)S(1)} %get-tuple-element.54), channel_id=1, source_target_pairs={{0,16},{1,17},{2,18},{3,19},{4,20},{5,21},{6,22},{7,23},{8,24},{9,... | collective-permute-start | bytes 196616 | tf_op jit(solution)/shard_map/ppermute | solution.py:30
  43.0 6.3 %collective-permute-start.15 = (bf16[128,256]{1,0:T(8,128)(2,1)S(1)}, bf16[128,256]{1,0:T(8,128)(2,1)S(1)}, u32[]{:S(2)}, u32[]{:S(2)}) collective-permute-start(bf16[128,256]{1,0:T(8,128)(2,1)S(1)} %get-tuple-element.55), channel_id=1, source_target_pairs={{0,24},{1,25},{2,26},{3,27},{4,28},{5,29},{6,30},{7,31},{8,16},{9,... | collective-permute-start | bytes 196616 | tf_op jit(solution)/shard_map/ppermute | solution.py:30
  44.8 4.4 %collective-permute-start.20 = (bf16[144,256]{1,0:T(8,128)(2,1)S(1)}, bf16[144,256]{1,0:T(8,128)(2,1)S(1)}, u32[]{:S(2)}, u32[]{:S(2)}) collective-permute-start(bf16[144,256]{1,0:T(8,128)(2,1)S(1)} %shard_map.110.mine_ref), channel_id=1, source_target_pairs={{0,4},{1,3},{2,6},{3,1},{4,0},{5,7},{6,2},{7,5},{8,12},{9,11},{10,... | collective-permute-start | bytes 221192 | tf_op jit(solution)/shard_map/ppermute | solution.py:30
  46.0 4.3 %collective-permute-start.16 = (bf16[128,256]{1,0:T(8,128)(2,1)S(1)}, bf16[128,256]{1,0:T(8,128)(2,1)S(1)}, u32[]{:S(2)}, u32[]{:S(2)}) collective-permute-start(bf16[128,256]{1,0:T(8,128)(2,1)S(1)} %add_convert_fusion.3), channel_id=1, source_target_pairs={{0,8},{1,9},{2,10},{3,11},{4,12},{5,13},{6,14},{7,15},{8,0},{9,1},... | collective-permute-start | bytes 196616 | tf_op jit(solution)/shard_map/ppermute | solution.py:30
  49.3 1.7 %collective-permute-start.21 = (f32[136,256]{1,0:T(8,128)S(1)}, f32[136,256]{1,0:T(8,128)S(1)}, u32[]{:S(2)}, u32[]{:S(2)}) collective-permute-start(f32[136,256]{1,0:T(8,128)S(1)} %shard_map.111.mine_ref), channel_id=1, source_target_pairs={{0,1},{1,0},{2,3},{3,2},{4,5},{5,4},{6,7},{7,6},{8,9},{9,8},{10,11... | collective-permute-start | bytes 417800 | tf_op jit(solution)/shard_map/ppermute | solution.py:34
  (4 other events, 3.1 us)

commit v8 on v6

--- a/solution.py
+++ b/solution.py
@@ -255,8 +255,8 @@
     position, rep = position.reshape(1, 1), rep.reshape(1, 1)
 
     own_near = jnp.concatenate([node_features, move(node_features, (4, 4))], axis=0)
-    own_far = [after(move(node_features, (z, z)), own_near) for z in (8, 12)]
-    own_far = jnp.concatenate(own_far, axis=0)
+    own_far = [after(move(node_features, (z, z)), own_near) for z in (12, 8)]
+    own_far = jnp.concatenate(own_far[::-1], axis=0)
     come = after(move(own_near, first), own_far)
     own_near = jnp.concatenate([own_near, come], axis=0)
     come_near = move(own_near, second)

time: 52.1 us -> 52.1 us (level)
  no operation moved by 1% of the time
where the time goes in v8:
time: 52.1 us; the launch traced here: 51.9 us
  starting transfers between devices  25.2 us (48%)
  waiting for transfers between devices  17.5 us (34%)
  Pallas kernels  5.09 us (10%)
  local copies, waits for them, and re-layouts  2.4 us (5%)
  other arithmetic  0.83 us (2%)
  between operations  0.82 us (2%)
    ppermute x18, starting transfers between devices, exchange(): return lax.ppermute(value, ('loop', 'rep'), pairs)  25.1 us
    ppermute x18, waiting for transfers between devices, exchange(): return lax.ppermute(value, ('loop', 'rep'), pairs)  15.5 us
    pallas_call x11, Pallas kernels, call(): pl.pallas_call(kernel, out_shape=tuple((jax.ShapeDtypeStruct(*shape) for...  5.09 us
    unnamed x15, local copies, waits for them, and re-layouts  2.29 us
    ppermute x3, waiting for transfers between devices, swap_rep(): return lax.ppermute(value, 'rep', [(r, r ^ mask) for r in range(rep_size)])  2.01 us
  transfers between devices with their start and end apart: 21, of which 11 were waited for; matrix products, arithmetic and copies ran while one was open for 4% of the time, Pallas kernels for 6%

profile of v8, /device:TPU:0, one launch (start us, length us, event | category | flops | bytes accessed | tf_op | source)
XLA Modules:
  0.0 51.9 jit_solution(12189878095167233342)
XLA Ops:
  0.6 3.1 %collective-permute-start = (bf16[128,256]{1,0:T(8,128)(2,1)}, bf16[128,256]{1,0:T(8,128)(2,1)S(1)}, u32[]{:S(2)}, u32[]{:S(2)}) collective-permute-start(bf16[128,256]{1,0:T(8,128)(2,1)} %param.7), channel_id=1, source_target_pairs={{0,8},{1,9},{2,10},{3,11},{4,12},{5,13},{6,14},{7,15},{8,0},{9,1},... | collective-permute-start | bytes 196616 | tf_op jit(solution)/shard_map/ppermute | solution.py:30
  3.7 2.6 %collective-permute-start.2 = (bf16[128,256]{1,0:T(8,128)(2,1)}, bf16[128,256]{1,0:T(8,128)(2,1)S(1)}, u32[]{:S(2)}, u32[]{:S(2)}) collective-permute-start(bf16[128,256]{1,0:T(8,128)(2,1)} %param.7), channel_id=1, source_target_pairs={{0,16},{1,17},{2,18},{3,19},{4,20},{5,21},{6,22},{7,23},{8,24},{9,... | collective-permute-start | bytes 196616 | tf_op jit(solution)/shard_map/ppermute | solution.py:30
  7.3 1.7 %collective-permute-start.1 = (bf16[256,256]{1,0:T(8,128)(2,1)S(1)}, bf16[256,256]{1,0:T(8,128)(2,1)S(1)}, u32[]{:S(2)}, u32[]{:S(2)}) collective-permute-start(bf16[256,256]{1,0:T(8,128)(2,1)S(1)} %get-tuple-element.56), channel_id=1, source_target_pairs={{0,2},{1,5},{2,0},{3,7},{4,6},{5,1},{6,4},{7,3},{8,10},{9,13},{10,... | collective-permute-start | bytes 393224 | tf_op jit(solution)/shard_map/ppermute | solution.py:30
  9.0 2.2 %collective-permute-done.2 = bf16[128,256]{1,0:T(8,128)(2,1)S(1)} collective-permute-done((bf16[128,256]{1,0:T(8,128)(2,1)}, bf16[128,256]{1,0:T(8,128)(2,1)S(1)}, u32[]{:S(2)}, u32[]{:S(2)}) %collective-permute-start.2) | collective-permute-done | bytes 65568 | tf_op jit(solution)/shard_map/ppermute | solution.py:30
  11.2 1.4 %collective-permute-done.3 = bf16[128,256]{1,0:T(8,128)(2,1)S(1)} collective-permute-done((bf16[128,256]{1,0:T(8,128)(2,1)}, bf16[128,256]{1,0:T(8,128)(2,1)S(1)}, u32[]{:S(2)}, u32[]{:S(2)}) %collective-permute-start.3) | collective-permute-done | bytes 65568 | tf_op jit(solution)/shard_map/ppermute | solution.py:30
  12.6 1.6 %collective-permute-start.5 = (bf16[256,256]{1,0:T(8,128)(2,1)S(1)}, bf16[256,256]{1,0:T(8,128)(2,1)S(1)}, u32[]{:S(2)}, u32[]{:S(2)}) collective-permute-start(bf16[256,256]{1,0:T(8,128)(2,1)S(1)} %get-tuple-element.53), channel_id=1, source_target_pairs={{0,2},{1,5},{2,0},{3,7},{4,6},{5,1},{6,4},{7,3},{8,10},{9,13},{10,... | collective-permute-start | bytes 393224 | tf_op jit(solution)/shard_map/ppermute | solution.py:30
  14.2 1.6 %collective-permute-start.4 = (bf16[512,256]{1,0:T(8,128)(2,1)S(1)}, bf16[512,256]{1,0:T(8,128)(2,1)S(1)}, u32[]{:S(2)}, u32[]{:S(2)}) collective-permute-start(bf16[512,256]{1,0:T(8,128)(2,1)S(1)} %constant_dynamic-update-slice_fusion.4.own_ref), channel_id=1, source_target_pairs={{0,4},{1,3},{2,6},{3,1},{4,0},{5,7},{6,2},{7,5},{8,12},{9,11},{10,... | collective-permute-start | bytes 786440 | tf_op jit(solution)/shard_map/ppermute | solution.py:30
  15.8 3.3 %collective-permute-done.5 = bf16[256,256]{1,0:T(8,128)(2,1)S(1)} collective-permute-done((bf16[256,256]{1,0:T(8,128)(2,1)S(1)}, bf16[256,256]{1,0:T(8,128)(2,1)S(1)}, u32[]{:S(2)}, u32[]{:S(2)}) %collective-permute-start.5) | collective-permute-done | bytes 131104 | tf_op jit(solution)/shard_map/ppermute | solution.py:30
  19.1 1.1 %collective-permute-start.7 = (bf16[512,256]{1,0:T(8,128)(2,1)S(1)}, bf16[512,256]{1,0:T(8,128)(2,1)S(1)}, u32[]{:S(2)}, u32[]{:S(2)}) collective-permute-start(bf16[512,256]{1,0:T(8,128)(2,1)S(1)} %constant_dynamic-update-slice_fusion.7.far_own_ref), channel_id=1, source_target_pairs={{0,4},{1,3},{2,6},{3,1},{4,0},{5,7},{6,2},{7,5},{8,12},{9,11},{10,... | collective-permute-start | bytes 786440 | tf_op jit(solution)/shard_map/ppermute | solution.py:30
  22.2 1.6 %shard_map.102 = (f32[256,256]{1,0:T(8,128)S(1)}, bf16[512,1024]{1,0:T(8,128)(2,1)S(1)}, bf16[1024,512]{1,0:T(8,128)(2,1)S(1)}, bf16[1024,512]{1,0:T(8,128)(2,1)...) custom-call(s32[1,1]{1,0:T(1,128)} %bitcast.position_ref, ...), custom_call_target="tpu_custom_call" | custom-call | tf_op jit(solution)/shard_map/pallas_call | solution.py:192
  23.8 1.8 %collective-permute-done.7.come_ref = bf16[512,256]{1,0:T(8,128)(2,1)S(1)} collective-permute-done((bf16[512,256]{1,0:T(8,128)(2,1)S(1)}, bf16[512,256]{1,0:T(8,128)(2,1)S(1)}, u32[]{:S(2)}, u32[]{:S(2)}) %collective-permute-start.7) | collective-permute-done | bytes 262176 | tf_op jit(solution)/shard_map/ppermute | solution.py:30
  26.0 1.5 %collective-permute-done.8.other_ref = f32[256,256]{1,0:T(8,128)S(1)} collective-permute-done((f32[256,256]{1,0:T(8,128)S(1)}, f32[256,256]{1,0:T(8,128)S(1)}, u32[]{:S(2)}, u32[]{:S(2)}) %collective-permute-start.8) | collective-permute-done | bytes 262176 | tf_op jit(solution)/shard_map/ppermute | solution.py:34
  28.2 1.1 %collective-permute-start.11 = (bf16[512,256]{1,0:T(8,128)(2,1)S(1)}, bf16[512,256]{1,0:T(8,128)(2,1)S(1)}, u32[]{:S(2)}, u32[]{:S(2)}) collective-permute-start(bf16[512,256]{1,0:T(8,128)(2,1)S(1)} %get-tuple-element.42), channel_id=1, source_target_pairs={{0,4},{1,3},{2,6},{3,1},{4,0},{5,7},{6,2},{7,5},{8,12},{9,11},{10,... | collective-permute-start | bytes 786440 | tf_op jit(solution)/shard_map/ppermute | solution.py:30
  31.0 1.1 %shard_map.105 = (f32[512,256]{1,0:T(8,128)S(1)}, f32[512,256]{1,0:T(8,128)S(1)}, bf16[128,256]{1,0:T(8,128)(2,1)}) custom-call(bf16[1024,512]{1,0:T(8,128)(2,1)S(1)} %get-tuple-element.30.near_t_ref, bf16[1024,512]{1,0:T(8,128)(2,1)S(1)} %get-tuple-element.31.far_t_ref, bf16[512,256]{1,0:T(8,128)(2,1)S(1)} %get-tuple-element.37.back_ref, ...), custom_call_target="tpu_custom_call" | custom-call | tf_op jit(solution)/shard_map/pallas_call | solution.py:192
  32.1 2.7 %collective-permute-done.16.other_ref = bf16[144,256]{1,0:T(8,128)(2,1)S(1)} collective-permute-done((bf16[144,256]{1,0:T(8,128)(2,1)S(1)}, bf16[144,256]{1,0:T(8,128)(2,1)S(1)}, u32[]{:S(2)}, u32[]{:S(2)}) %collective-permute-start.16) | collective-permute-done | bytes 73760 | tf_op jit(solution)/shard_map/ppermute | solution.py:30
  34.8 1.4 %collective-permute-start.17 = (bf16[144,256]{1,0:T(8,128)(2,1)S(1)}, bf16[144,256]{1,0:T(8,128)(2,1)S(1)}, u32[]{:S(2)}, u32[]{:S(2)}) collective-permute-start(bf16[144,256]{1,0:T(8,128)(2,1)S(1)} %shard_map.108.mine_ref), channel_id=1, source_target_pairs={{0,16},{1,9},{2,18},{3,11},{4,20},{5,13},{6,22},{7,15},{8,24},{9,1... | collective-permute-start | bytes 221192 | tf_op jit(solution)/shard_map/ppermute | solution.py:30
  36.2 1.6 %collective-permute-start.12 = (bf16[256,256]{1,0:T(8,128)(2,1)S(1)}, bf16[256,256]{1,0:T(8,128)(2,1)S(1)}, u32[]{:S(2)}, u32[]{:S(2)}) collective-permute-start(bf16[256,256]{1,0:T(8,128)(2,1)S(1)} %add_convert_fusion), channel_id=1, source_target_pairs={{0,2},{1,5},{2,0},{3,7},{4,6},{5,1},{6,4},{7,3},{8,10},{9,13},{10,... | collective-permute-start | bytes 393224 | tf_op jit(solution)/shard_map/ppermute | solution.py:30
  37.9 1.9 %collective-permute-start.10 = (bf16[256,256]{1,0:T(8,128)(2,1)S(1)}, bf16[256,256]{1,0:T(8,128)(2,1)S(1)}, u32[]{:S(2)}, u32[]{:S(2)}) collective-permute-start(bf16[256,256]{1,0:T(8,128)(2,1)S(1)} %add_convert_fusion.1), channel_id=1, source_target_pairs={{0,2},{1,5},{2,0},{3,7},{4,6},{5,1},{6,4},{7,3},{8,10},{9,13},{10,... | collective-permute-start | bytes 393224 | tf_op jit(solution)/shard_map/ppermute | solution.py:30
  40.4 1.4 %collective-permute-start.18 = (bf16[144,256]{1,0:T(8,128)(2,1)S(1)}, bf16[144,256]{1,0:T(8,128)(2,1)S(1)}, u32[]{:S(2)}, u32[]{:S(2)}) collective-permute-start(bf16[144,256]{1,0:T(8,128)(2,1)S(1)} %shard_map.109.mine_ref), channel_id=1, source_target_pairs={{0,2},{1,5},{2,0},{3,7},{4,6},{5,1},{6,4},{7,3},{8,10},{9,13},{10,... | collective-permute-start | bytes 221192 | tf_op jit(solution)/shard_map/ppermute | solution.py:30
  41.9 1.3 %collective-permute-start.13 = (bf16[128,256]{1,0:T(8,128)(2,1)S(1)}, bf16[128,256]{1,0:T(8,128)(2,1)S(1)}, u32[]{:S(2)}, u32[]{:S(2)}) collective-permute-start(bf16[128,256]{1,0:T(8,128)(2,1)S(1)} %get-tuple-element.50), channel_id=1, source_target_pairs={{0,16},{1,17},{2,18},{3,19},{4,20},{5,21},{6,22},{7,23},{8,24},{9,... | collective-permute-start | bytes 196616 | tf_op jit(solution)/shard_map/ppermute | solution.py:30
  43.2 1.8 %collective-permute-start.14 = (bf16[128,256]{1,0:T(8,128)(2,1)S(1)}, bf16[128,256]{1,0:T(8,128)(2,1)S(1)}, u32[]{:S(2)}, u32[]{:S(2)}) collective-permute-start(bf16[128,256]{1,0:T(8,128)(2,1)S(1)} %get-tuple-element.51), channel_id=1, source_target_pairs={{0,24},{1,25},{2,26},{3,27},{4,28},{5,29},{6,30},{7,31},{8,16},{9,... | collective-permute-start | bytes 196616 | tf_op jit(solution)/shard_map/ppermute | solution.py:30
  45.0 1.1 %collective-permute-start.19 = (bf16[144,256]{1,0:T(8,128)(2,1)S(1)}, bf16[144,256]{1,0:T(8,128)(2,1)S(1)}, u32[]{:S(2)}, u32[]{:S(2)}) collective-permute-start(bf16[144,256]{1,0:T(8,128)(2,1)S(1)} %shard_map.110.mine_ref), channel_id=1, source_target_pairs={{0,4},{1,3},{2,6},{3,1},{4,0},{5,7},{6,2},{7,5},{8,12},{9,11},{10,... | collective-permute-start | bytes 221192 | tf_op jit(solution)/shard_map/ppermute | solution.py:30
  46.9 2.5 %collective-permute-done.19.other_ref = bf16[144,256]{1,0:T(8,128)(2,1)S(1)} collective-permute-done((bf16[144,256]{1,0:T(8,128)(2,1)S(1)}, bf16[144,256]{1,0:T(8,128)(2,1)S(1)}, u32[]{:S(2)}, u32[]{:S(2)}) %collective-permute-start.19) | collective-permute-done | bytes 73760 | tf_op jit(solution)/shard_map/ppermute | solution.py:30
  49.5 1.0 %collective-permute-done.15 = bf16[128,256]{1,0:T(8,128)(2,1)S(1)} collective-permute-done((bf16[128,256]{1,0:T(8,128)(2,1)S(1)}, bf16[128,256]{1,0:T(8,128)(2,1)S(1)}, u32[]{:S(2)}, u32[]{:S(2)}) %collective-permute-start.15) | collective-permute-done | bytes 65568 | tf_op jit(solution)/shard_map/ppermute | solution.py:30
  (53 shorter events, 8.9 us)
Async XLA Ops:
  0.6 20.9 %copy-start = (bf16[1,1,16,2,128,128]{5,4,3,2,1,0:T(8,128)(2,1)S(1)}, bf16[1,1,16,2,128,128]{5,4,3,2,1,0:T(8,128)(2,1)}, u32[]{:S(2)}) copy-start(bf16[1,1,16,2,128,128]{5,4,3,2,1,0:T(8,128)(2,1)} %param.10) | copy-start | bytes 3145732
  0.6 6.6 %collective-permute-start = (bf16[128,256]{1,0:T(8,128)(2,1)}, bf16[128,256]{1,0:T(8,128)(2,1)S(1)}, u32[]{:S(2)}, u32[]{:S(2)}) collective-permute-start(bf16[128,256]{1,0:T(8,128)(2,1)} %param.7), channel_id=1, source_target_pairs={{0,8},{1,9},{2,10},{3,11},{4,12},{5,13},{6,14},{7,15},{8,0},{9,1},... | collective-permute-start | bytes 196616 | tf_op jit(solution)/shard_map/ppermute | solution.py:30
  3.7 7.5 %collective-permute-start.2 = (bf16[128,256]{1,0:T(8,128)(2,1)}, bf16[128,256]{1,0:T(8,128)(2,1)S(1)}, u32[]{:S(2)}, u32[]{:S(2)}) collective-permute-start(bf16[128,256]{1,0:T(8,128)(2,1)} %param.7), channel_id=1, source_target_pairs={{0,16},{1,17},{2,18},{3,19},{4,20},{5,21},{6,22},{7,23},{8,24},{9,... | collective-permute-start | bytes 196616 | tf_op jit(solution)/shard_map/ppermute | solution.py:30
  6.3 6.3 %collective-permute-start.3 = (bf16[128,256]{1,0:T(8,128)(2,1)}, bf16[128,256]{1,0:T(8,128)(2,1)S(1)}, u32[]{:S(2)}, u32[]{:S(2)}) collective-permute-start(bf16[128,256]{1,0:T(8,128)(2,1)} %param.7), channel_id=1, source_target_pairs={{0,24},{1,25},{2,26},{3,27},{4,28},{5,29},{6,30},{7,31},{8,16},{9,... | collective-permute-start | bytes 196616 | tf_op jit(solution)/shard_map/ppermute | solution.py:30
  7.3 6.9 %collective-permute-start.1 = (bf16[256,256]{1,0:T(8,128)(2,1)S(1)}, bf16[256,256]{1,0:T(8,128)(2,1)S(1)}, u32[]{:S(2)}, u32[]{:S(2)}) collective-permute-start(bf16[256,256]{1,0:T(8,128)(2,1)S(1)} %get-tuple-element.56), channel_id=1, source_target_pairs={{0,2},{1,5},{2,0},{3,7},{4,6},{5,1},{6,4},{7,3},{8,10},{9,13},{10,... | collective-permute-start | bytes 393224 | tf_op jit(solution)/shard_map/ppermute | solution.py:30
  12.6 6.5 %collective-permute-start.5 = (bf16[256,256]{1,0:T(8,128)(2,1)S(1)}, bf16[256,256]{1,0:T(8,128)(2,1)S(1)}, u32[]{:S(2)}, u32[]{:S(2)}) collective-permute-start(bf16[256,256]{1,0:T(8,128)(2,1)S(1)} %get-tuple-element.53), channel_id=1, source_target_pairs={{0,2},{1,5},{2,0},{3,7},{4,6},{5,1},{6,4},{7,3},{8,10},{9,13},{10,... | collective-permute-start | bytes 393224 | tf_op jit(solution)/shard_map/ppermute | solution.py:30
  14.2 7.3 %collective-permute-start.4 = (bf16[512,256]{1,0:T(8,128)(2,1)S(1)}, bf16[512,256]{1,0:T(8,128)(2,1)S(1)}, u32[]{:S(2)}, u32[]{:S(2)}) collective-permute-start(bf16[512,256]{1,0:T(8,128)(2,1)S(1)} %constant_dynamic-update-slice_fusion.4.own_ref), channel_id=1, source_target_pairs={{0,4},{1,3},{2,6},{3,1},{4,0},{5,7},{6,2},{7,5},{8,12},{9,11},{10,... | collective-permute-start | bytes 786440 | tf_op jit(solution)/shard_map/ppermute | solution.py:30
  19.1 1.1 %copy-start.2 = (bf16[128,256]{1,0:T(8,128)(2,1)S(1)}, bf16[128,256]{1,0:T(8,128)(2,1)}, u32[]{:S(2)}) copy-start(bf16[128,256]{1,0:T(8,128)(2,1)} %cotangent_ref.1) | copy-start | bytes 196612
  19.1 2.4 %copy-start.1 = (bf16[256,256]{1,0:T(8,128)(2,1)S(1)}, bf16[256,256]{1,0:T(8,128)(2,1)}, u32[]{:S(2)}) copy-start(bf16[256,256]{1,0:T(8,128)(2,1)} %weight_ref.1) | copy-start | bytes 393220
  19.1 6.4 %collective-permute-start.7 = (bf16[512,256]{1,0:T(8,128)(2,1)S(1)}, bf16[512,256]{1,0:T(8,128)(2,1)S(1)}, u32[]{:S(2)}, u32[]{:S(2)}) collective-permute-start(bf16[512,256]{1,0:T(8,128)(2,1)S(1)} %constant_dynamic-update-slice_fusion.7.far_own_ref), channel_id=1, source_target_pairs={{0,4},{1,3},{2,6},{3,1},{4,0},{5,7},{6,2},{7,5},{8,12},{9,11},{10,... | collective-permute-start | bytes 786440 | tf_op jit(solution)/shard_map/ppermute | solution.py:30
  20.2 1.3 %collective-permute-start.6 = (bf16[128,256]{1,0:T(8,128)(2,1)S(1)}, bf16[128,256]{1,0:T(8,128)(2,1)S(1)}, u32[]{:S(2)}, u32[]{:S(2)}) collective-permute-start(bf16[128,256]{1,0:T(8,128)(2,1)S(1)} %copy-done.2), channel_id=1, source_target_pairs={{0,1},{1,0},{2,3},{3,2},{4,5},{5,4},{6,7},{7,6},{8,9},{9,8},{10,11... | collective-permute-start | bytes 196616 | tf_op jit(solution)/shard_map/ppermute | solution.py:34
  25.9 1.6 %collective-permute-start.8 = (f32[256,256]{1,0:T(8,128)S(1)}, f32[256,256]{1,0:T(8,128)S(1)}, u32[]{:S(2)}, u32[]{:S(2)}) collective-permute-start(f32[256,256]{1,0:T(8,128)S(1)} %shard_map.103.mine_ref), channel_id=1, source_target_pairs={{0,1},{1,0},{2,3},{3,2},{4,5},{5,4},{6,7},{7,6},{8,9},{9,8},{10,11... | collective-permute-start | bytes 786440 | tf_op jit(solution)/shard_map/ppermute | solution.py:34
  28.2 6.6 %collective-permute-start.11 = (bf16[512,256]{1,0:T(8,128)(2,1)S(1)}, bf16[512,256]{1,0:T(8,128)(2,1)S(1)}, u32[]{:S(2)}, u32[]{:S(2)}) collective-permute-start(bf16[512,256]{1,0:T(8,128)(2,1)S(1)} %get-tuple-element.42), channel_id=1, source_target_pairs={{0,4},{1,3},{2,6},{3,1},{4,0},{5,7},{6,2},{7,5},{8,12},{9,11},{10,... | collective-permute-start | bytes 786440 | tf_op jit(solution)/shard_map/ppermute | solution.py:30
  29.5 5.2 %collective-permute-start.16 = (bf16[144,256]{1,0:T(8,128)(2,1)S(1)}, bf16[144,256]{1,0:T(8,128)(2,1)S(1)}, u32[]{:S(2)}, u32[]{:S(2)}) collective-permute-start(bf16[144,256]{1,0:T(8,128)(2,1)S(1)} %shard_map.107.mine_ref), channel_id=1, source_target_pairs={{0,8},{1,17},{2,10},{3,19},{4,12},{5,21},{6,14},{7,23},{8,0},{9,25... | collective-permute-start | bytes 221192 | tf_op jit(solution)/shard_map/ppermute | solution.py:30
  30.3 7.6 %collective-permute-start.9 = (bf16[512,256]{1,0:T(8,128)(2,1)S(1)}, bf16[512,256]{1,0:T(8,128)(2,1)S(1)}, u32[]{:S(2)}, u32[]{:S(2)}) collective-permute-start(bf16[512,256]{1,0:T(8,128)(2,1)S(1)} %shard_map.106), channel_id=1, source_target_pairs={{0,4},{1,3},{2,6},{3,1},{4,0},{5,7},{6,2},{7,5},{8,12},{9,11},{10,... | collective-permute-start | bytes 786440 | tf_op jit(solution)/shard_map/ppermute | solution.py:30
  34.8 5.6 %collective-permute-start.17 = (bf16[144,256]{1,0:T(8,128)(2,1)S(1)}, bf16[144,256]{1,0:T(8,128)(2,1)S(1)}, u32[]{:S(2)}, u32[]{:S(2)}) collective-permute-start(bf16[144,256]{1,0:T(8,128)(2,1)S(1)} %shard_map.108.mine_ref), channel_id=1, source_target_pairs={{0,16},{1,9},{2,18},{3,11},{4,20},{5,13},{6,22},{7,15},{8,24},{9,1... | collective-permute-start | bytes 221192 | tf_op jit(solution)/shard_map/ppermute | solution.py:30
  36.2 5.6 %collective-permute-start.12 = (bf16[256,256]{1,0:T(8,128)(2,1)S(1)}, bf16[256,256]{1,0:T(8,128)(2,1)S(1)}, u32[]{:S(2)}, u32[]{:S(2)}) collective-permute-start(bf16[256,256]{1,0:T(8,128)(2,1)S(1)} %add_convert_fusion), channel_id=1, source_target_pairs={{0,2},{1,5},{2,0},{3,7},{4,6},{5,1},{6,4},{7,3},{8,10},{9,13},{10,... | collective-permute-start | bytes 393224 | tf_op jit(solution)/shard_map/ppermute | solution.py:30
  37.9 7.1 %collective-permute-start.10 = (bf16[256,256]{1,0:T(8,128)(2,1)S(1)}, bf16[256,256]{1,0:T(8,128)(2,1)S(1)}, u32[]{:S(2)}, u32[]{:S(2)}) collective-permute-start(bf16[256,256]{1,0:T(8,128)(2,1)S(1)} %add_convert_fusion.1), channel_id=1, source_target_pairs={{0,2},{1,5},{2,0},{3,7},{4,6},{5,1},{6,4},{7,3},{8,10},{9,13},{10,... | collective-permute-start | bytes 393224 | tf_op jit(solution)/shard_map/ppermute | solution.py:30
  40.4 4.6 %collective-permute-start.18 = (bf16[144,256]{1,0:T(8,128)(2,1)S(1)}, bf16[144,256]{1,0:T(8,128)(2,1)S(1)}, u32[]{:S(2)}, u32[]{:S(2)}) collective-permute-start(bf16[144,256]{1,0:T(8,128)(2,1)S(1)} %shard_map.109.mine_ref), channel_id=1, source_target_pairs={{0,2},{1,5},{2,0},{3,7},{4,6},{5,1},{6,4},{7,3},{8,10},{9,13},{10,... | collective-permute-start | bytes 221192 | tf_op jit(solution)/shard_map/ppermute | solution.py:30
  41.9 7.7 %collective-permute-start.13 = (bf16[128,256]{1,0:T(8,128)(2,1)S(1)}, bf16[128,256]{1,0:T(8,128)(2,1)S(1)}, u32[]{:S(2)}, u32[]{:S(2)}) collective-permute-start(bf16[128,256]{1,0:T(8,128)(2,1)S(1)} %get-tuple-element.50), channel_id=1, source_target_pairs={{0,16},{1,17},{2,18},{3,19},{4,20},{5,21},{6,22},{7,23},{8,24},{9,... | collective-permute-start | bytes 196616 | tf_op jit(solution)/shard_map/ppermute | solution.py:30
  43.2 6.3 %collective-permute-start.14 = (bf16[128,256]{1,0:T(8,128)(2,1)S(1)}, bf16[128,256]{1,0:T(8,128)(2,1)S(1)}, u32[]{:S(2)}, u32[]{:S(2)}) collective-permute-start(bf16[128,256]{1,0:T(8,128)(2,1)S(1)} %get-tuple-element.51), channel_id=1, source_target_pairs={{0,24},{1,25},{2,26},{3,27},{4,28},{5,29},{6,30},{7,31},{8,16},{9,... | collective-permute-start | bytes 196616 | tf_op jit(solution)/shard_map/ppermute | solution.py:30
  45.0 4.4 %collective-permute-start.19 = (bf16[144,256]{1,0:T(8,128)(2,1)S(1)}, bf16[144,256]{1,0:T(8,128)(2,1)S(1)}, u32[]{:S(2)}, u32[]{:S(2)}) collective-permute-start(bf16[144,256]{1,0:T(8,128)(2,1)S(1)} %shard_map.110.mine_ref), channel_id=1, source_target_pairs={{0,4},{1,3},{2,6},{3,1},{4,0},{5,7},{6,2},{7,5},{8,12},{9,11},{10,... | collective-permute-start | bytes 221192 | tf_op jit(solution)/shard_map/ppermute | solution.py:30
  46.2 4.3 %collective-permute-start.15 = (bf16[128,256]{1,0:T(8,128)(2,1)S(1)}, bf16[128,256]{1,0:T(8,128)(2,1)S(1)}, u32[]{:S(2)}, u32[]{:S(2)}) collective-permute-start(bf16[128,256]{1,0:T(8,128)(2,1)S(1)} %add_convert_fusion.3), channel_id=1, source_target_pairs={{0,8},{1,9},{2,10},{3,11},{4,12},{5,13},{6,14},{7,15},{8,0},{9,1},... | collective-permute-start | bytes 196616 | tf_op jit(solution)/shard_map/ppermute | solution.py:30
  49.4 1.7 %collective-permute-start.20 = (f32[136,256]{1,0:T(8,128)S(1)}, f32[136,256]{1,0:T(8,128)S(1)}, u32[]{:S(2)}, u32[]{:S(2)}) collective-permute-start(f32[136,256]{1,0:T(8,128)S(1)} %shard_map.111.mine_ref), channel_id=1, source_target_pairs={{0,1},{1,0},{2,3},{3,2},{4,5},{5,4},{6,7},{7,6},{8,9},{9,8},{10,11... | collective-permute-start | bytes 417800 | tf_op jit(solution)/shard_map/ppermute | solution.py:34
  (3 other events, 2.0 us)

commit v9 on v6

--- a/solution.py
+++ b/solution.py
@@ -303,7 +303,7 @@
     near_1 = move(near_message, second)
     half, one = wide // 4, rows_own
     (term,) = on_chip(repack_kernel, [(term.shape, BF16)])(term, move(term, (4, 8)))
-    far_2 = move(plus((far_keep, half, half), (far_1, half, half)).astype(BF16), first)
+    far_2 = move(after(plus((far_keep, half, half), (far_1, half, half)).astype(BF16), term), first)
     near_2 = move(plus((near_keep, half, half), (near_1, half, half)).astype(BF16), first)
     term = after(term, far_1)
     (term,) = on_chip(repack_kernel, [(term.shape, BF16)])(term, move(term, (8, 4)))

time: 52.1 us -> 52.1 us (level)
  no operation moved by 1% of the time
where the time goes in v9:
time: 52.1 us; the launch traced here: 51.9 us
  starting transfers between devices  25.2 us (48%)
  waiting for transfers between devices  17.5 us (34%)
  Pallas kernels  5.09 us (10%)
  local copies, waits for them, and re-layouts  2.4 us (5%)
  other arithmetic  0.83 us (2%)
  between operations  0.82 us (2%)
    ppermute x18, starting transfers between devices, exchange(): return lax.ppermute(value, ('loop', 'rep'), pairs)  25.1 us
    ppermute x18, waiting for transfers between devices, exchange(): return lax.ppermute(value, ('loop', 'rep'), pairs)  15.5 us
    pallas_call x11, Pallas kernels, call(): pl.pallas_call(kernel, out_shape=tuple((jax.ShapeDtypeStruct(*shape) for...  5.09 us
    unnamed x15, local copies, waits for them, and re-layouts  2.29 us
    ppermute x3, waiting for transfers between devices, swap_rep(): return lax.ppermute(value, 'rep', [(r, r ^ mask) for r in range(rep_size)])  2.01 us
  transfers between devices with their start and end apart: 21, of which 11 were waited for; matrix products, arithmetic and copies ran while one was open for 4% of the time, Pallas kernels for 6%

profile of v9, /device:TPU:0, one launch (start us, length us, event | category | flops | bytes accessed | tf_op | source)
XLA Modules:
  0.0 51.9 jit_solution(12189878095167233342)
XLA Ops:
  0.6 3.1 %collective-permute-start = (bf16[128,256]{1,0:T(8,128)(2,1)}, bf16[128,256]{1,0:T(8,128)(2,1)S(1)}, u32[]{:S(2)}, u32[]{:S(2)}) collective-permute-start(bf16[128,256]{1,0:T(8,128)(2,1)} %param.7), channel_id=1, source_target_pairs={{0,8},{1,9},{2,10},{3,11},{4,12},{5,13},{6,14},{7,15},{8,0},{9,1},... | collective-permute-start | bytes 196616 | tf_op jit(solution)/shard_map/ppermute | solution.py:30
  3.7 2.6 %collective-permute-start.2 = (bf16[128,256]{1,0:T(8,128)(2,1)}, bf16[128,256]{1,0:T(8,128)(2,1)S(1)}, u32[]{:S(2)}, u32[]{:S(2)}) collective-permute-start(bf16[128,256]{1,0:T(8,128)(2,1)} %param.7), channel_id=1, source_target_pairs={{0,16},{1,17},{2,18},{3,19},{4,20},{5,21},{6,22},{7,23},{8,24},{9,... | collective-permute-start | bytes 196616 | tf_op jit(solution)/shard_map/ppermute | solution.py:30
  7.3 1.7 %collective-permute-start.1 = (bf16[256,256]{1,0:T(8,128)(2,1)S(1)}, bf16[256,256]{1,0:T(8,128)(2,1)S(1)}, u32[]{:S(2)}, u32[]{:S(2)}) collective-permute-start(bf16[256,256]{1,0:T(8,128)(2,1)S(1)} %get-tuple-element.58), channel_id=1, source_target_pairs={{0,2},{1,5},{2,0},{3,7},{4,6},{5,1},{6,4},{7,3},{8,10},{9,13},{10,... | collective-permute-start | bytes 393224 | tf_op jit(solution)/shard_map/ppermute | solution.py:30
  9.0 2.2 %collective-permute-done.2 = bf16[128,256]{1,0:T(8,128)(2,1)S(1)} collective-permute-done((bf16[128,256]{1,0:T(8,128)(2,1)}, bf16[128,256]{1,0:T(8,128)(2,1)S(1)}, u32[]{:S(2)}, u32[]{:S(2)}) %collective-permute-start.2) | collective-permute-done | bytes 65568 | tf_op jit(solution)/shard_map/ppermute | solution.py:30
  11.2 1.4 %collective-permute-done.3 = bf16[128,256]{1,0:T(8,128)(2,1)S(1)} collective-permute-done((bf16[128,256]{1,0:T(8,128)(2,1)}, bf16[128,256]{1,0:T(8,128)(2,1)S(1)}, u32[]{:S(2)}, u32[]{:S(2)}) %collective-permute-start.3) | collective-permute-done | bytes 65568 | tf_op jit(solution)/shard_map/ppermute | solution.py:30
  12.6 1.6 %collective-permute-start.5 = (bf16[256,256]{1,0:T(8,128)(2,1)S(1)}, bf16[256,256]{1,0:T(8,128)(2,1)S(1)}, u32[]{:S(2)}, u32[]{:S(2)}) collective-permute-start(bf16[256,256]{1,0:T(8,128)(2,1)S(1)} %get-tuple-element.55), channel_id=1, source_target_pairs={{0,2},{1,5},{2,0},{3,7},{4,6},{5,1},{6,4},{7,3},{8,10},{9,13},{10,... | collective-permute-start | bytes 393224 | tf_op jit(solution)/shard_map/ppermute | solution.py:30
  14.2 1.6 %collective-permute-start.4 = (bf16[512,256]{1,0:T(8,128)(2,1)S(1)}, bf16[512,256]{1,0:T(8,128)(2,1)S(1)}, u32[]{:S(2)}, u32[]{:S(2)}) collective-permute-start(bf16[512,256]{1,0:T(8,128)(2,1)S(1)} %constant_dynamic-update-slice_fusion.4.own_ref), channel_id=1, source_target_pairs={{0,4},{1,3},{2,6},{3,1},{4,0},{5,7},{6,2},{7,5},{8,12},{9,11},{10,... | collective-permute-start | bytes 786440 | tf_op jit(solution)/shard_map/ppermute | solution.py:30
  15.8 3.3 %collective-permute-done.5 = bf16[256,256]{1,0:T(8,128)(2,1)S(1)} collective-permute-done((bf16[256,256]{1,0:T(8,128)(2,1)S(1)}, bf16[256,256]{1,0:T(8,128)(2,1)S(1)}, u32[]{:S(2)}, u32[]{:S(2)}) %collective-permute-start.5) | collective-permute-done | bytes 131104 | tf_op jit(solution)/shard_map/ppermute | solution.py:30
  19.1 1.1 %collective-permute-start.7 = (bf16[512,256]{1,0:T(8,128)(2,1)S(1)}, bf16[512,256]{1,0:T(8,128)(2,1)S(1)}, u32[]{:S(2)}, u32[]{:S(2)}) collective-permute-start(bf16[512,256]{1,0:T(8,128)(2,1)S(1)} %constant_dynamic-update-slice_fusion.7.far_own_ref), channel_id=1, source_target_pairs={{0,4},{1,3},{2,6},{3,1},{4,0},{5,7},{6,2},{7,5},{8,12},{9,11},{10,... | collective-permute-start | bytes 786440 | tf_op jit(solution)/shard_map/ppermute | solution.py:30
  22.2 1.6 %shard_map.102 = (f32[256,256]{1,0:T(8,128)S(1)}, bf16[512,1024]{1,0:T(8,128)(2,1)S(1)}, bf16[1024,512]{1,0:T(8,128)(2,1)S(1)}, bf16[1024,512]{1,0:T(8,128)(2,1)...) custom-call(s32[1,1]{1,0:T(1,128)} %bitcast.position_ref, ...), custom_call_target="tpu_custom_call" | custom-call | tf_op jit(solution)/shard_map/pallas_call | solution.py:192
  23.8 1.8 %collective-permute-done.7.come_ref = bf16[512,256]{1,0:T(8,128)(2,1)S(1)} collective-permute-done((bf16[512,256]{1,0:T(8,128)(2,1)S(1)}, bf16[512,256]{1,0:T(8,128)(2,1)S(1)}, u32[]{:S(2)}, u32[]{:S(2)}) %collective-permute-start.7) | collective-permute-done | bytes 262176 | tf_op jit(solution)/shard_map/ppermute | solution.py:30
  26.0 1.5 %collective-permute-done.8.other_ref = f32[256,256]{1,0:T(8,128)S(1)} collective-permute-done((f32[256,256]{1,0:T(8,128)S(1)}, f32[256,256]{1,0:T(8,128)S(1)}, u32[]{:S(2)}, u32[]{:S(2)}) %collective-permute-start.8) | collective-permute-done | bytes 262176 | tf_op jit(solution)/shard_map/ppermute | solution.py:34
  28.2 1.1 %collective-permute-start.11 = (bf16[512,256]{1,0:T(8,128)(2,1)S(1)}, bf16[512,256]{1,0:T(8,128)(2,1)S(1)}, u32[]{:S(2)}, u32[]{:S(2)}) collective-permute-start(bf16[512,256]{1,0:T(8,128)(2,1)S(1)} %get-tuple-element.43), channel_id=1, source_target_pairs={{0,4},{1,3},{2,6},{3,1},{4,0},{5,7},{6,2},{7,5},{8,12},{9,11},{10,... | collective-permute-start | bytes 786440 | tf_op jit(solution)/shard_map/ppermute | solution.py:30
  31.0 1.1 %shard_map.105 = (f32[512,256]{1,0:T(8,128)S(1)}, f32[512,256]{1,0:T(8,128)S(1)}, bf16[128,256]{1,0:T(8,128)(2,1)}) custom-call(bf16[1024,512]{1,0:T(8,128)(2,1)S(1)} %get-tuple-element.31.near_t_ref, bf16[1024,512]{1,0:T(8,128)(2,1)S(1)} %get-tuple-element.32.far_t_ref, bf16[512,256]{1,0:T(8,128)(2,1)S(1)} %get-tuple-element.38.back_ref, ...), custom_call_target="tpu_custom_call" | custom-call | tf_op jit(solution)/shard_map/pallas_call | solution.py:192
  32.1 2.7 %collective-permute-done.12.other_ref = bf16[144,256]{1,0:T(8,128)(2,1)S(1)} collective-permute-done((bf16[144,256]{1,0:T(8,128)(2,1)S(1)}, bf16[144,256]{1,0:T(8,128)(2,1)S(1)}, u32[]{:S(2)}, u32[]{:S(2)}) %collective-permute-start.12) | collective-permute-done | bytes 73760 | tf_op jit(solution)/shard_map/ppermute | solution.py:30
  34.8 1.4 %collective-permute-start.17 = (bf16[144,256]{1,0:T(8,128)(2,1)S(1)}, bf16[144,256]{1,0:T(8,128)(2,1)S(1)}, u32[]{:S(2)}, u32[]{:S(2)}) collective-permute-start(bf16[144,256]{1,0:T(8,128)(2,1)S(1)} %shard_map.108.mine_ref), channel_id=1, source_target_pairs={{0,16},{1,9},{2,18},{3,11},{4,20},{5,13},{6,22},{7,15},{8,24},{9,1... | collective-permute-start | bytes 221192 | tf_op jit(solution)/shard_map/ppermute | solution.py:30
  36.2 1.6 %collective-permute-start.13 = (bf16[256,256]{1,0:T(8,128)(2,1)S(1)}, bf16[256,256]{1,0:T(8,128)(2,1)S(1)}, u32[]{:S(2)}, u32[]{:S(2)}) collective-permute-start(bf16[256,256]{1,0:T(8,128)(2,1)S(1)} %add_convert_fusion), channel_id=1, source_target_pairs={{0,2},{1,5},{2,0},{3,7},{4,6},{5,1},{6,4},{7,3},{8,10},{9,13},{10,... | collective-permute-start | bytes 393224 | tf_op jit(solution)/shard_map/ppermute | solution.py:30
  37.9 1.9 %collective-permute-start.10 = (bf16[256,256]{1,0:T(8,128)(2,1)S(1)}, bf16[256,256]{1,0:T(8,128)(2,1)S(1)}, u32[]{:S(2)}, u32[]{:S(2)}) collective-permute-start(bf16[256,256]{1,0:T(8,128)(2,1)S(1)} %add_convert_fusion.1), channel_id=1, source_target_pairs={{0,2},{1,5},{2,0},{3,7},{4,6},{5,1},{6,4},{7,3},{8,10},{9,13},{10,... | collective-permute-start | bytes 393224 | tf_op jit(solution)/shard_map/ppermute | solution.py:30
  40.4 1.4 %collective-permute-start.18 = (bf16[144,256]{1,0:T(8,128)(2,1)S(1)}, bf16[144,256]{1,0:T(8,128)(2,1)S(1)}, u32[]{:S(2)}, u32[]{:S(2)}) collective-permute-start(bf16[144,256]{1,0:T(8,128)(2,1)S(1)} %shard_map.109.mine_ref), channel_id=1, source_target_pairs={{0,2},{1,5},{2,0},{3,7},{4,6},{5,1},{6,4},{7,3},{8,10},{9,13},{10,... | collective-permute-start | bytes 221192 | tf_op jit(solution)/shard_map/ppermute | solution.py:30
  41.9 1.3 %collective-permute-start.14 = (bf16[128,256]{1,0:T(8,128)(2,1)S(1)}, bf16[128,256]{1,0:T(8,128)(2,1)S(1)}, u32[]{:S(2)}, u32[]{:S(2)}) collective-permute-start(bf16[128,256]{1,0:T(8,128)(2,1)S(1)} %get-tuple-element.52), channel_id=1, source_target_pairs={{0,16},{1,17},{2,18},{3,19},{4,20},{5,21},{6,22},{7,23},{8,24},{9,... | collective-permute-start | bytes 196616 | tf_op jit(solution)/shard_map/ppermute | solution.py:30
  43.2 1.8 %collective-permute-start.15 = (bf16[128,256]{1,0:T(8,128)(2,1)S(1)}, bf16[128,256]{1,0:T(8,128)(2,1)S(1)}, u32[]{:S(2)}, u32[]{:S(2)}) collective-permute-start(bf16[128,256]{1,0:T(8,128)(2,1)S(1)} %get-tuple-element.53), channel_id=1, source_target_pairs={{0,24},{1,25},{2,26},{3,27},{4,28},{5,29},{6,30},{7,31},{8,16},{9,... | collective-permute-start | bytes 196616 | tf_op jit(solution)/shard_map/ppermute | solution.py:30
  45.0 1.1 %collective-permute-start.19 = (bf16[144,256]{1,0:T(8,128)(2,1)S(1)}, bf16[144,256]{1,0:T(8,128)(2,1)S(1)}, u32[]{:S(2)}, u32[]{:S(2)}) collective-permute-start(bf16[144,256]{1,0:T(8,128)(2,1)S(1)} %shard_map.110.mine_ref), channel_id=1, source_target_pairs={{0,4},{1,3},{2,6},{3,1},{4,0},{5,7},{6,2},{7,5},{8,12},{9,11},{10,... | collective-permute-start | bytes 221192 | tf_op jit(solution)/shard_map/ppermute | solution.py:30
  46.9 2.5 %collective-permute-done.19.other_ref = bf16[144,256]{1,0:T(8,128)(2,1)S(1)} collective-permute-done((bf16[144,256]{1,0:T(8,128)(2,1)S(1)}, bf16[144,256]{1,0:T(8,128)(2,1)S(1)}, u32[]{:S(2)}, u32[]{:S(2)}) %collective-permute-start.19) | collective-permute-done | bytes 73760 | tf_op jit(solution)/shard_map/ppermute | solution.py:30
  49.5 1.0 %collective-permute-done.16 = bf16[128,256]{1,0:T(8,128)(2,1)S(1)} collective-permute-done((bf16[128,256]{1,0:T(8,128)(2,1)S(1)}, bf16[128,256]{1,0:T(8,128)(2,1)S(1)}, u32[]{:S(2)}, u32[]{:S(2)}) %collective-permute-start.16) | collective-permute-done | bytes 65568 | tf_op jit(solution)/shard_map/ppermute | solution.py:30
  (53 shorter events, 8.9 us)
Async XLA Ops:
  0.6 20.9 %copy-start = (bf16[1,1,16,2,128,128]{5,4,3,2,1,0:T(8,128)(2,1)S(1)}, bf16[1,1,16,2,128,128]{5,4,3,2,1,0:T(8,128)(2,1)}, u32[]{:S(2)}) copy-start(bf16[1,1,16,2,128,128]{5,4,3,2,1,0:T(8,128)(2,1)} %param.10) | copy-start | bytes 3145732
  0.6 6.6 %collective-permute-start = (bf16[128,256]{1,0:T(8,128)(2,1)}, bf16[128,256]{1,0:T(8,128)(2,1)S(1)}, u32[]{:S(2)}, u32[]{:S(2)}) collective-permute-start(bf16[128,256]{1,0:T(8,128)(2,1)} %param.7), channel_id=1, source_target_pairs={{0,8},{1,9},{2,10},{3,11},{4,12},{5,13},{6,14},{7,15},{8,0},{9,1},... | collective-permute-start | bytes 196616 | tf_op jit(solution)/shard_map/ppermute | solution.py:30
  3.7 7.5 %collective-permute-start.2 = (bf16[128,256]{1,0:T(8,128)(2,1)}, bf16[128,256]{1,0:T(8,128)(2,1)S(1)}, u32[]{:S(2)}, u32[]{:S(2)}) collective-permute-start(bf16[128,256]{1,0:T(8,128)(2,1)} %param.7), channel_id=1, source_target_pairs={{0,16},{1,17},{2,18},{3,19},{4,20},{5,21},{6,22},{7,23},{8,24},{9,... | collective-permute-start | bytes 196616 | tf_op jit(solution)/shard_map/ppermute | solution.py:30
  6.3 6.3 %collective-permute-start.3 = (bf16[128,256]{1,0:T(8,128)(2,1)}, bf16[128,256]{1,0:T(8,128)(2,1)S(1)}, u32[]{:S(2)}, u32[]{:S(2)}) collective-permute-start(bf16[128,256]{1,0:T(8,128)(2,1)} %param.7), channel_id=1, source_target_pairs={{0,24},{1,25},{2,26},{3,27},{4,28},{5,29},{6,30},{7,31},{8,16},{9,... | collective-permute-start | bytes 196616 | tf_op jit(solution)/shard_map/ppermute | solution.py:30
  7.3 6.9 %collective-permute-start.1 = (bf16[256,256]{1,0:T(8,128)(2,1)S(1)}, bf16[256,256]{1,0:T(8,128)(2,1)S(1)}, u32[]{:S(2)}, u32[]{:S(2)}) collective-permute-start(bf16[256,256]{1,0:T(8,128)(2,1)S(1)} %get-tuple-element.58), channel_id=1, source_target_pairs={{0,2},{1,5},{2,0},{3,7},{4,6},{5,1},{6,4},{7,3},{8,10},{9,13},{10,... | collective-permute-start | bytes 393224 | tf_op jit(solution)/shard_map/ppermute | solution.py:30
  12.6 6.5 %collective-permute-start.5 = (bf16[256,256]{1,0:T(8,128)(2,1)S(1)}, bf16[256,256]{1,0:T(8,128)(2,1)S(1)}, u32[]{:S(2)}, u32[]{:S(2)}) collective-permute-start(bf16[256,256]{1,0:T(8,128)(2,1)S(1)} %get-tuple-element.55), channel_id=1, source_target_pairs={{0,2},{1,5},{2,0},{3,7},{4,6},{5,1},{6,4},{7,3},{8,10},{9,13},{10,... | collective-permute-start | bytes 393224 | tf_op jit(solution)/shard_map/ppermute | solution.py:30
  14.2 7.3 %collective-permute-start.4 = (bf16[512,256]{1,0:T(8,128)(2,1)S(1)}, bf16[512,256]{1,0:T(8,128)(2,1)S(1)}, u32[]{:S(2)}, u32[]{:S(2)}) collective-permute-start(bf16[512,256]{1,0:T(8,128)(2,1)S(1)} %constant_dynamic-update-slice_fusion.4.own_ref), channel_id=1, source_target_pairs={{0,4},{1,3},{2,6},{3,1},{4,0},{5,7},{6,2},{7,5},{8,12},{9,11},{10,... | collective-permute-start | bytes 786440 | tf_op jit(solution)/shard_map/ppermute | solution.py:30
  19.1 1.1 %copy-start.2 = (bf16[128,256]{1,0:T(8,128)(2,1)S(1)}, bf16[128,256]{1,0:T(8,128)(2,1)}, u32[]{:S(2)}) copy-start(bf16[128,256]{1,0:T(8,128)(2,1)} %cotangent_ref.1) | copy-start | bytes 196612
  19.1 2.4 %copy-start.1 = (bf16[256,256]{1,0:T(8,128)(2,1)S(1)}, bf16[256,256]{1,0:T(8,128)(2,1)}, u32[]{:S(2)}) copy-start(bf16[256,256]{1,0:T(8,128)(2,1)} %weight_ref.1) | copy-start | bytes 393220
  19.1 6.4 %collective-permute-start.7 = (bf16[512,256]{1,0:T(8,128)(2,1)S(1)}, bf16[512,256]{1,0:T(8,128)(2,1)S(1)}, u32[]{:S(2)}, u32[]{:S(2)}) collective-permute-start(bf16[512,256]{1,0:T(8,128)(2,1)S(1)} %constant_dynamic-update-slice_fusion.7.far_own_ref), channel_id=1, source_target_pairs={{0,4},{1,3},{2,6},{3,1},{4,0},{5,7},{6,2},{7,5},{8,12},{9,11},{10,... | collective-permute-start | bytes 786440 | tf_op jit(solution)/shard_map/ppermute | solution.py:30
  20.2 1.3 %collective-permute-start.6 = (bf16[128,256]{1,0:T(8,128)(2,1)S(1)}, bf16[128,256]{1,0:T(8,128)(2,1)S(1)}, u32[]{:S(2)}, u32[]{:S(2)}) collective-permute-start(bf16[128,256]{1,0:T(8,128)(2,1)S(1)} %copy-done.2), channel_id=1, source_target_pairs={{0,1},{1,0},{2,3},{3,2},{4,5},{5,4},{6,7},{7,6},{8,9},{9,8},{10,11... | collective-permute-start | bytes 196616 | tf_op jit(solution)/shard_map/ppermute | solution.py:34
  25.9 1.6 %collective-permute-start.8 = (f32[256,256]{1,0:T(8,128)S(1)}, f32[256,256]{1,0:T(8,128)S(1)}, u32[]{:S(2)}, u32[]{:S(2)}) collective-permute-start(f32[256,256]{1,0:T(8,128)S(1)} %shard_map.103.mine_ref), channel_id=1, source_target_pairs={{0,1},{1,0},{2,3},{3,2},{4,5},{5,4},{6,7},{7,6},{8,9},{9,8},{10,11... | collective-permute-start | bytes 786440 | tf_op jit(solution)/shard_map/ppermute | solution.py:34
  28.2 6.6 %collective-permute-start.11 = (bf16[512,256]{1,0:T(8,128)(2,1)S(1)}, bf16[512,256]{1,0:T(8,128)(2,1)S(1)}, u32[]{:S(2)}, u32[]{:S(2)}) collective-permute-start(bf16[512,256]{1,0:T(8,128)(2,1)S(1)} %get-tuple-element.43), channel_id=1, source_target_pairs={{0,4},{1,3},{2,6},{3,1},{4,0},{5,7},{6,2},{7,5},{8,12},{9,11},{10,... | collective-permute-start | bytes 786440 | tf_op jit(solution)/shard_map/ppermute | solution.py:30
  29.5 5.2 %collective-permute-start.12 = (bf16[144,256]{1,0:T(8,128)(2,1)S(1)}, bf16[144,256]{1,0:T(8,128)(2,1)S(1)}, u32[]{:S(2)}, u32[]{:S(2)}) collective-permute-start(bf16[144,256]{1,0:T(8,128)(2,1)S(1)} %shard_map.107.mine_ref), channel_id=1, source_target_pairs={{0,8},{1,17},{2,10},{3,19},{4,12},{5,21},{6,14},{7,23},{8,0},{9,25... | collective-permute-start | bytes 221192 | tf_op jit(solution)/shard_map/ppermute | solution.py:30
  30.3 7.6 %collective-permute-start.9 = (bf16[512,256]{1,0:T(8,128)(2,1)S(1)}, bf16[512,256]{1,0:T(8,128)(2,1)S(1)}, u32[]{:S(2)}, u32[]{:S(2)}) collective-permute-start(bf16[512,256]{1,0:T(8,128)(2,1)S(1)} %shard_map.106), channel_id=1, source_target_pairs={{0,4},{1,3},{2,6},{3,1},{4,0},{5,7},{6,2},{7,5},{8,12},{9,11},{10,... | collective-permute-start | bytes 786440 | tf_op jit(solution)/shard_map/ppermute | solution.py:30
  34.8 5.6 %collective-permute-start.17 = (bf16[144,256]{1,0:T(8,128)(2,1)S(1)}, bf16[144,256]{1,0:T(8,128)(2,1)S(1)}, u32[]{:S(2)}, u32[]{:S(2)}) collective-permute-start(bf16[144,256]{1,0:T(8,128)(2,1)S(1)} %shard_map.108.mine_ref), channel_id=1, source_target_pairs={{0,16},{1,9},{2,18},{3,11},{4,20},{5,13},{6,22},{7,15},{8,24},{9,1... | collective-permute-start | bytes 221192 | tf_op jit(solution)/shard_map/ppermute | solution.py:30
  36.2 5.6 %collective-permute-start.13 = (bf16[256,256]{1,0:T(8,128)(2,1)S(1)}, bf16[256,256]{1,0:T(8,128)(2,1)S(1)}, u32[]{:S(2)}, u32[]{:S(2)}) collective-permute-start(bf16[256,256]{1,0:T(8,128)(2,1)S(1)} %add_convert_fusion), channel_id=1, source_target_pairs={{0,2},{1,5},{2,0},{3,7},{4,6},{5,1},{6,4},{7,3},{8,10},{9,13},{10,... | collective-permute-start | bytes 393224 | tf_op jit(solution)/shard_map/ppermute | solution.py:30
  37.9 7.1 %collective-permute-start.10 = (bf16[256,256]{1,0:T(8,128)(2,1)S(1)}, bf16[256,256]{1,0:T(8,128)(2,1)S(1)}, u32[]{:S(2)}, u32[]{:S(2)}) collective-permute-start(bf16[256,256]{1,0:T(8,128)(2,1)S(1)} %add_convert_fusion.1), channel_id=1, source_target_pairs={{0,2},{1,5},{2,0},{3,7},{4,6},{5,1},{6,4},{7,3},{8,10},{9,13},{10,... | collective-permute-start | bytes 393224 | tf_op jit(solution)/shard_map/ppermute | solution.py:30
  40.4 4.6 %collective-permute-start.18 = (bf16[144,256]{1,0:T(8,128)(2,1)S(1)}, bf16[144,256]{1,0:T(8,128)(2,1)S(1)}, u32[]{:S(2)}, u32[]{:S(2)}) collective-permute-start(bf16[144,256]{1,0:T(8,128)(2,1)S(1)} %shard_map.109.mine_ref), channel_id=1, source_target_pairs={{0,2},{1,5},{2,0},{3,7},{4,6},{5,1},{6,4},{7,3},{8,10},{9,13},{10,... | collective-permute-start | bytes 221192 | tf_op jit(solution)/shard_map/ppermute | solution.py:30
  41.9 7.7 %collective-permute-start.14 = (bf16[128,256]{1,0:T(8,128)(2,1)S(1)}, bf16[128,256]{1,0:T(8,128)(2,1)S(1)}, u32[]{:S(2)}, u32[]{:S(2)}) collective-permute-start(bf16[128,256]{1,0:T(8,128)(2,1)S(1)} %get-tuple-element.52), channel_id=1, source_target_pairs={{0,16},{1,17},{2,18},{3,19},{4,20},{5,21},{6,22},{7,23},{8,24},{9,... | collective-permute-start | bytes 196616 | tf_op jit(solution)/shard_map/ppermute | solution.py:30
  43.2 6.3 %collective-permute-start.15 = (bf16[128,256]{1,0:T(8,128)(2,1)S(1)}, bf16[128,256]{1,0:T(8,128)(2,1)S(1)}, u32[]{:S(2)}, u32[]{:S(2)}) collective-permute-start(bf16[128,256]{1,0:T(8,128)(2,1)S(1)} %get-tuple-element.53), channel_id=1, source_target_pairs={{0,24},{1,25},{2,26},{3,27},{4,28},{5,29},{6,30},{7,31},{8,16},{9,... | collective-permute-start | bytes 196616 | tf_op jit(solution)/shard_map/ppermute | solution.py:30
  45.0 4.4 %collective-permute-start.19 = (bf16[144,256]{1,0:T(8,128)(2,1)S(1)}, bf16[144,256]{1,0:T(8,128)(2,1)S(1)}, u32[]{:S(2)}, u32[]{:S(2)}) collective-permute-start(bf16[144,256]{1,0:T(8,128)(2,1)S(1)} %shard_map.110.mine_ref), channel_id=1, source_target_pairs={{0,4},{1,3},{2,6},{3,1},{4,0},{5,7},{6,2},{7,5},{8,12},{9,11},{10,... | collective-permute-start | bytes 221192 | tf_op jit(solution)/shard_map/ppermute | solution.py:30
  46.2 4.3 %collective-permute-start.16 = (bf16[128,256]{1,0:T(8,128)(2,1)S(1)}, bf16[128,256]{1,0:T(8,128)(2,1)S(1)}, u32[]{:S(2)}, u32[]{:S(2)}) collective-permute-start(bf16[128,256]{1,0:T(8,128)(2,1)S(1)} %add_convert_fusion.3), channel_id=1, source_target_pairs={{0,8},{1,9},{2,10},{3,11},{4,12},{5,13},{6,14},{7,15},{8,0},{9,1},... | collective-permute-start | bytes 196616 | tf_op jit(solution)/shard_map/ppermute | solution.py:30
  49.4 1.7 %collective-permute-start.20 = (f32[136,256]{1,0:T(8,128)S(1)}, f32[136,256]{1,0:T(8,128)S(1)}, u32[]{:S(2)}, u32[]{:S(2)}) collective-permute-start(f32[136,256]{1,0:T(8,128)S(1)} %shard_map.111.mine_ref), channel_id=1, source_target_pairs={{0,1},{1,0},{2,3},{3,2},{4,5},{5,4},{6,7},{7,6},{8,9},{9,8},{10,11... | collective-permute-start | bytes 417800 | tf_op jit(solution)/shard_map/ppermute | solution.py:34
  (3 other events, 2.0 us)
